TPU v7x, 32 devices: a whole 2x2x4 slice. The times are simulated.
32 devices in a mesh: dp: 4 (over z), expert: 8 (over y, x, core).
Axes of the slice: x: 2, y: 2, z: 4, core: 2. Of those that a mesh axis runs over, the one named last changes fastest.
Arguments:
- inputs: float32 [25216, 768], P(('dp', 'expert')), may hold values from -6 to 6
- gain_one: bfloat16 [768], P('dp'), may hold values from 0.5 to 1.5
- shift_one: bfloat16 [768], P('dp'), may hold values from -0.59765625 to 0.59765625
- qkv_weight: bfloat16 [768, 2304], P('dp'), may hold values from -0.21875 to 0.21875
- proj_weight: bfloat16 [768, 768], P('dp'), may hold values from -1.25 to 1.25
- gain_two: bfloat16 [768], P('dp'), may hold values from 0.5 to 1.5
- shift_two: bfloat16 [768], P('dp'), may hold values from -0.59765625 to 0.59765625
- router_weight: bfloat16 [768, 8], P('dp'), may hold values from -0.15625 to 0.15625
- expert_in: bfloat16 [8, 768, 3072], P('expert', None, 'dp'), may hold values from -0.21875 to 0.21875
- expert_bias: bfloat16 [8, 3072], P('expert', 'dp'), may hold values from -0.59765625 to 0.59765625
- expert_out: bfloat16 [8, 3072, 768], P('expert', 'dp'), may hold values from -0.875 to 0.875
- out_grad: float32 [25216, 768], P(('dp', 'expert')), may hold values from -6 to 6
- routes: int32 [25216, 2], P(('dp', 'expert')), may hold values from 0 to 7, all different within a row
- priority: int32 [128, 394], P(('dp', 'expert')), may hold values from 0 to 393, each once within a row
- capacity: int32 [128], P(('dp', 'expert')), may hold values from 45 to 62, as said below
Outputs:
- outputs: float32 [25216, 768], P(('dp', 'expert'))
- inputs_grad: float32 [25216, 768], P(('dp', 'expert'))
- gainone_grad: float32 [768], P('dp')
- shiftone_grad: float32 [768], P('dp')
- qkv_grad: float32 [768, 2304], P('dp')
- proj_grad: float32 [768, 768], P('dp')
- gaintwo_grad: float32 [768], P('dp')
- shifttwo_grad: float32 [768], P('dp')
- router_grad: float32 [768, 8], P('dp')
- expin_grad: float32 [8, 768, 3072], P('expert', None, 'dp')
- bias_grad: float32 [8, 3072], P('expert', 'dp')
- expout_grad: float32 [8, 3072, 768], P('expert', 'dp')
Inputs may be any that keep to these rules, and one draw needn't show every extreme that they name: Each row of priority is a permutation; lower values fill first. `routes`: the two experts of a token differ. capacity[b] is at most 62 and equals 62 for some micro-batch in every draw.
All inputs are finite; a program needn't handle non-finite values.
Results may differ from a plain program's by a relative error of at most 0.022.
Values may be sent and summed in bfloat16 or wider, within the bound.
A program may use at most 152 MiB of HBM per device.

v0:
```python
from functools import partial

import jax
import jax.numpy as jnp
from jax import lax
from jax.sharding import PartitionSpec as P

HEADS = 12
HEAD = 64
SEQ = 197


EPS = 1e-06


def for_sending(array):
    return jax.tree.map(lambda a: a.astype(jnp.bfloat16) if a.dtype == jnp.float32 else a, array)


def norm_apply(values, gain, shift):
    average = jnp.mean(values, axis=-1, keepdims=True)
    centered = values - average
    spread = jnp.mean(centered * centered, axis=-1, keepdims=True)
    return centered * lax.rsqrt(spread + EPS) * gain + shift


def exact_gelu(values):
    return jax.nn.gelu(values, approximate=False)


def gate_pick(logits, route_rows):
    return jnp.take_along_axis(jax.nn.softmax(logits, axis=-1), route_rows, axis=1)


def add_all(accum, fresh):
    if accum is None:
        return fresh
    return tuple((left + right for left, right in zip(accum, fresh)))


def micro_step(dense, experts, rows, grad_rows, route_rows, order_row, limit):
    gain_a, shift_a, w_qkv, w_proj, gain_b, shift_b, w_router = dense
    w_in, bias_in, w_out = experts
    count = rows.shape[0]
    width = rows.shape[1]
    images = count // SEQ
    total_experts = w_router.shape[1]
    groups = lax.axis_size("expert")
    local_experts = total_experts // groups
    cap = max(2, (5 * count + 2 * total_experts - 1) // (2 * total_experts))
    slots = total_experts * cap
    scale = HEAD ** (-0.5)
    gain_af = gain_a.astype(jnp.float32)
    shift_af = shift_a.astype(jnp.float32)
    gain_bf = gain_b.astype(jnp.float32)
    shift_bf = shift_b.astype(jnp.float32)
    act_one = norm_apply(rows, gain_af, shift_af).astype(jnp.bfloat16)
    qkv = jnp.dot(act_one, w_qkv, preferred_element_type=jnp.float32).astype(jnp.bfloat16)
    split = qkv.reshape(images, SEQ, 3, HEADS, HEAD)
    query = split[:, :, 0]
    keys = split[:, :, 1]
    values = split[:, :, 2]
    scores = jnp.einsum("bqhd,bkhd->bhqk", query, keys, preferred_element_type=jnp.float32) * scale
    highest = jnp.max(scores, axis=-1, keepdims=True)
    expo = jnp.exp(scores - highest)
    denom = jnp.sum(expo, axis=-1, keepdims=True)
    log_total = highest + jnp.log(denom)
    weights = (expo / denom).astype(jnp.bfloat16)
    mixed = jnp.einsum("bhqk,bkhd->bqhd", weights, values, preferred_element_type=jnp.float32)
    mixed = mixed.reshape(count, width).astype(jnp.bfloat16)
    hidden = rows + jnp.dot(mixed, w_proj, preferred_element_type=jnp.float32)
    act_two = norm_apply(hidden, gain_bf, shift_bf).astype(jnp.bfloat16)
    logits = jnp.dot(act_two, w_router, preferred_element_type=jnp.float32)
    gates, gate_back = jax.vjp(partial(gate_pick, route_rows=route_rows), logits)
    pair_expert = route_rows.reshape(-1)
    same = pair_expert[:, None] == pair_expert[None, :]
    before = order_row[None, :] < order_row[:, None]
    ranks = jnp.sum(jnp.logical_and(same, before).astype(jnp.int32), axis=1)
    kept = ranks < limit
    flat = pair_expert * cap + ranks
    target = jnp.where(kept, flat, slots)
    pair_ids = lax.broadcasted_iota(jnp.int32, (2 * count,), 0)
    slot_pair = jnp.zeros((slots,), jnp.int32).at[target].set(pair_ids, mode="drop")
    slot_valid = (
        jnp.zeros((slots,), jnp.bfloat16)
        .at[target]
        .set(jnp.ones((2 * count,), jnp.bfloat16), mode="drop")
    )
    send = (act_two[slot_pair // 2] * slot_valid[:, None]).reshape(
        groups, local_experts, cap, width
    )
    block = lax.all_to_all(send, "expert", split_axis=0, concat_axis=0, tiled=True)
    pre_act = jnp.einsum("nkcd,kdf->nkcf", block, w_in, preferred_element_type=jnp.float32)
    pre_act = pre_act + bias_in.astype(jnp.float32)[None, :, None, :]
    active = exact_gelu(pre_act).astype(jnp.bfloat16)
    result = jnp.einsum("nkcf,kfd->nkcd", active, w_out, preferred_element_type=jnp.float32)
    result, pre_kept, received = (result.astype(jnp.bfloat16), pre_act, block)
    back = lax.all_to_all(result, "expert", split_axis=0, concat_axis=0, tiled=True).reshape(
        slots, width
    )
    pair_slot = jnp.where(kept, flat, 0)
    keep_pairs = kept.astype(jnp.float32).reshape(count, 2)
    picked = back[pair_slot].astype(jnp.float32).reshape(count, 2, width)
    mixing = gates * keep_pairs
    out_rows = hidden + jnp.sum(picked * mixing[:, :, None], axis=1)
    d_gates = jnp.sum(picked * grad_rows[:, None, :], axis=-1) * keep_pairs
    d_logits = gate_back(d_gates)[0]
    d_pairs = (
        (grad_rows[:, None, :] * mixing[:, :, None]).astype(jnp.bfloat16).reshape(2 * count, width)
    )
    grad_send = (d_pairs[slot_pair] * slot_valid[:, None]).reshape(
        groups, local_experts, cap, width
    )
    grad_recv = lax.all_to_all(grad_send, "expert", split_axis=0, concat_axis=0, tiled=True)
    active = exact_gelu(pre_kept).astype(jnp.bfloat16)
    d_active = jnp.einsum("nkcd,kfd->nkcf", grad_recv, w_out, preferred_element_type=jnp.float32)
    gelu_back = jax.vjp(exact_gelu, pre_kept)[1]
    d_pre = gelu_back(d_active)[0].astype(jnp.bfloat16)
    grad_out_w = jnp.einsum("nkcf,nkcd->kfd", active, grad_recv, preferred_element_type=jnp.float32)
    grad_in_w = jnp.einsum("nkcd,nkcf->kdf", received, d_pre, preferred_element_type=jnp.float32)
    grad_bias = jnp.sum(d_pre, axis=(0, 2), dtype=jnp.float32)
    d_rows = jnp.einsum("nkcf,kdf->nkcd", d_pre, w_in, preferred_element_type=jnp.float32).astype(
        jnp.bfloat16
    )
    back_grad = lax.all_to_all(d_rows, "expert", split_axis=0, concat_axis=0, tiled=True).reshape(
        slots, width
    )
    returned_grad = back_grad[pair_slot].astype(jnp.float32).reshape(count, 2, width)
    d_two = jnp.dot(d_logits, w_router.astype(jnp.float32).T, precision=lax.Precision.HIGHEST)
    d_two = d_two + jnp.sum(returned_grad * keep_pairs[:, :, None], axis=1)
    grad_router = jnp.dot(act_two.astype(jnp.float32).T, d_logits, precision=lax.Precision.HIGHEST)
    norm_back_two = jax.vjp(norm_apply, hidden, gain_bf, shift_bf)[1]
    hidden_part, grad_gain_b, grad_shift_b = norm_back_two(d_two)
    d_hidden = grad_rows + hidden_part
    d_branch = d_hidden.astype(jnp.bfloat16)
    grad_proj = jnp.einsum("rd,re->de", mixed, d_branch, preferred_element_type=jnp.float32)
    d_mixed = jnp.einsum("re,de->rd", d_branch, w_proj, preferred_element_type=jnp.float32)
    d_mixed = d_mixed.astype(jnp.bfloat16).reshape(images, SEQ, HEADS, HEAD)
    scores_again = (
        jnp.einsum("bqhd,bkhd->bhqk", query, keys, preferred_element_type=jnp.float32) * scale
    )
    probs_again = jnp.exp(scores_again - log_total)
    weights_again = probs_again.astype(jnp.bfloat16)
    d_weights = jnp.einsum("bqhd,bkhd->bhqk", d_mixed, values, preferred_element_type=jnp.float32)
    d_values = jnp.einsum(
        "bhqk,bqhd->bkhd", weights_again, d_mixed, preferred_element_type=jnp.float32
    )
    row_terms = jnp.sum(d_weights * probs_again, axis=-1, keepdims=True)
    d_scores = (probs_again * (d_weights - row_terms) * scale).astype(jnp.bfloat16)
    d_query = jnp.einsum("bhqk,bkhd->bqhd", d_scores, keys, preferred_element_type=jnp.float32)
    d_keys = jnp.einsum("bhqk,bqhd->bkhd", d_scores, query, preferred_element_type=jnp.float32)
    d_qkv = (
        jnp.stack([d_query, d_keys, d_values], axis=2)
        .reshape(count, 3 * width)
        .astype(jnp.bfloat16)
    )
    grad_qkv = jnp.einsum("rd,re->de", act_one, d_qkv, preferred_element_type=jnp.float32)
    d_one = jnp.einsum("re,de->rd", d_qkv, w_qkv, preferred_element_type=jnp.float32)
    norm_back_one = jax.vjp(norm_apply, rows, gain_af, shift_af)[1]
    input_part, grad_gain_a, grad_shift_a = norm_back_one(d_one)
    d_inputs = d_hidden + input_part
    dense_terms = (
        grad_gain_a,
        grad_shift_a,
        grad_qkv,
        grad_proj,
        grad_gain_b,
        grad_shift_b,
        grad_router,
    )
    expert_terms = (grad_in_w, grad_bias, grad_out_w)
    return (out_rows, d_inputs, dense_terms, expert_terms)


def per_device(
    inputs,
    gain_one,
    shift_one,
    qkv_weight,
    proj_weight,
    gain_two,
    shift_two,
    router_weight,
    expert_in,
    expert_bias,
    expert_out,
    out_grad,
    routes,
    priority,
    capacity,
):
    batches = priority.shape[0]
    rows_mb = inputs.shape[0] // batches
    out_parts = []
    grad_parts = []
    dense_accum = None
    expert_accum = None
    for index in range(batches):
        dense = (
            lax.all_gather(gain_one, "dp", axis=0, tiled=True),
            lax.all_gather(shift_one, "dp", axis=0, tiled=True),
            lax.all_gather(qkv_weight, "dp", axis=0, tiled=True),
            lax.all_gather(proj_weight, "dp", axis=0, tiled=True),
            lax.all_gather(gain_two, "dp", axis=0, tiled=True),
            lax.all_gather(shift_two, "dp", axis=0, tiled=True),
            lax.all_gather(router_weight, "dp", axis=0, tiled=True),
        )
        experts = (
            lax.all_gather(expert_in, "dp", axis=2, tiled=True),
            lax.all_gather(expert_bias, "dp", axis=1, tiled=True),
            lax.all_gather(expert_out, "dp", axis=1, tiled=True),
        )
        lower = index * rows_mb
        upper = lower + rows_mb
        out_rows, d_inputs, dense_terms, expert_terms = micro_step(
            dense,
            experts,
            inputs[lower:upper],
            out_grad[lower:upper],
            routes[lower:upper],
            priority[index],
            capacity[index],
        )
        out_parts.append(out_rows)
        grad_parts.append(d_inputs)
        dense_accum = add_all(dense_accum, dense_terms)
        expert_accum = add_all(expert_accum, expert_terms)
    dense_shards = (
        lax.psum_scatter(
            dense_accum[0].astype(jnp.bfloat16), "dp", scatter_dimension=0, tiled=True
        ).astype(jnp.float32),
        lax.psum_scatter(
            dense_accum[1].astype(jnp.bfloat16), "dp", scatter_dimension=0, tiled=True
        ).astype(jnp.float32),
        lax.psum_scatter(
            dense_accum[2].astype(jnp.bfloat16), "dp", scatter_dimension=0, tiled=True
        ).astype(jnp.float32),
        lax.psum_scatter(
            dense_accum[3].astype(jnp.bfloat16), "dp", scatter_dimension=0, tiled=True
        ).astype(jnp.float32),
        lax.psum_scatter(
            dense_accum[4].astype(jnp.bfloat16), "dp", scatter_dimension=0, tiled=True
        ).astype(jnp.float32),
        lax.psum_scatter(
            dense_accum[5].astype(jnp.bfloat16), "dp", scatter_dimension=0, tiled=True
        ).astype(jnp.float32),
        lax.psum_scatter(
            dense_accum[6].astype(jnp.bfloat16), "dp", scatter_dimension=0, tiled=True
        ).astype(jnp.float32),
    )
    dense_final = jax.tree.map(
        lambda part: part.astype(jnp.float32), lax.psum(for_sending(dense_shards), "expert")
    )
    expert_final = (
        lax.psum_scatter(
            expert_accum[0].astype(jnp.bfloat16), "dp", scatter_dimension=2, tiled=True
        ).astype(jnp.float32),
        lax.psum_scatter(
            expert_accum[1].astype(jnp.bfloat16), "dp", scatter_dimension=1, tiled=True
        ).astype(jnp.float32),
        lax.psum_scatter(
            expert_accum[2].astype(jnp.bfloat16), "dp", scatter_dimension=1, tiled=True
        ).astype(jnp.float32),
    )
    outputs = jnp.concatenate(out_parts, axis=0)
    inputs_grad = jnp.concatenate(grad_parts, axis=0)
    return (
        outputs,
        inputs_grad,
        dense_final[0],
        dense_final[1],
        dense_final[2],
        dense_final[3],
        dense_final[4],
        dense_final[5],
        dense_final[6],
        expert_final[0],
        expert_final[1],
        expert_final[2],
    )


def solution(mesh):
    return jax.shard_map(
        per_device,
        mesh=mesh,
        in_specs=(
            P(("dp", "expert"), None),
            P("dp"),
            P("dp"),
            P("dp", None),
            P("dp", None),
            P("dp"),
            P("dp"),
            P("dp", None),
            P("expert", None, "dp"),
            P("expert", "dp"),
            P("expert", "dp", None),
            P(("dp", "expert"), None),
            P(("dp", "expert"), None),
            P(("dp", "expert"), None),
            P(("dp", "expert")),
        ),
        out_specs=(
            P(("dp", "expert"), None),
            P(("dp", "expert"), None),
            P("dp"),
            P("dp"),
            P("dp", None),
            P("dp", None),
            P("dp"),
            P("dp"),
            P("dp", None),
            P("expert", None, "dp"),
            P("expert", "dp"),
            P("expert", "dp", None),
        ),
        check_vma=False,
    )
```

profile of v0, /device:TPU:0, one launch (start us, length us, event | category | flops | bytes accessed | tf_op | source)
XLA Modules:
  0.0 1334.1 jit_solution(2933856009234556657)
XLA Ops:
  18.2 14.4 %all-reduce.11 = (bf16[768]{0:T(1024)(128)(2,1)S(1)}, bf16[768]{0:T(1024)(128)(2,1)S(1)}, bf16[768]{0:T(1024)(128)(2,1)S(1)}, bf16[768]{0:T(1024)(128)(2,1)S(1)}) all-reduce(bf16[768]{0:T(1024)(128)(2,1)S(1)} %dynamic-update-slice.1, bf16[768]{0:T(1024)(128)(2,1)S(1)} %dynamic-update-slice, ...), channel_id=1, replica_groups=mesh['dp'=4,'expert'=8] {'dp'}, use_global_device_ids=true, to_apply=%add.1 | all-reduce | flops 3072 | bytes 12288
  40.8 13.3 %all-gather = bf16[4,192,8]{1,2,0:T(8,128)(2,1)S(1)} all-gather(bf16[1,192,8]{1,2,0:T(8,128)(2,1)S(1)} %bitcast.1159), channel_id=1, replica_groups=mesh['dp'=4,'expert'=8] {'dp'}, dimensions={0}, use_global_device_ids=true | all-gather | bytes 15360 | tf_op jit(solution)/shard_map/all_gather | solution.py:206
  94.1 19.6 %all-gather.8.cloned.1.call-done = bf16[768,768]{1,0:T(8,128)(2,1)} async-done(((bf16[192,768]{1,0:T(8,128)(2,1)}), bf16[768,768]{1,0:T(8,128)(2,1)}) %all-gather.8.cloned.1.call-update) | async-done | bytes 1179664 | tf_op jit(solution)/shard_map/all_gather | solution.py:203
  117.4 4.6 gather_fusion.18
  133.0 11.8 all-to-all-done.4
  149.7 13.4 %all_gather.27 = bf16[1,3072]{1,0:T(2,128)(2,1)S(1)} all-gather(bf16[1,768]{1,0:T(2,128)(2,1)S(1)} %copy-done.278), channel_id=1, replica_groups=mesh['dp'=4,'expert'=8] {'dp'}, dimensions={1}, use_global_device_ids=true | all-gather | bytes 7680 | tf_op jit(solution)/shard_map/all_gather | solution.py:210
  181.4 22.5 %all-gather.10.cloned.1.call-done = bf16[1,768,3072]{2,1,0:T(8,128)(2,1)} async-done(((bf16[1,768,768]{2,1,0:T(8,128)(2,1)}), bf16[1,768,3072]{2,1,0:T(8,128)(2,1)}) %all-gather.10.cloned.1.call-update) | async-done | bytes 4718608 | tf_op jit(solution)/shard_map/all_gather | solution.py:209
  203.9 6.9 fusion.124
  210.9 82.4 %all-gather.12.cloned.1.call-done = bf16[1,3072,768]{2,1,0:T(8,128)(2,1)} async-done(((bf16[1,768,768]{2,1,0:T(8,128)(2,1)}), bf16[1,3072,768]{2,1,0:T(8,128)(2,1)}) %all-gather.12.cloned.1.call-update) | async-done | bytes 4718608 | tf_op jit(solution)/shard_map/all_gather | solution.py:211
  293.3 19.3 %convert_reduce_fusion.1 = (f32[3072]{0:T(1024)}, bf16[8,1,62,3072]{3,2,0,1:T(8,128)(2,1)S(1)}) fusion(bf16[1,3072,768]{2,1,0:T(8,128)(2,1)} %all-gather.12.cloned.1.call-done, bf16[8,1,62,768]{3,2,1,0:T(8,128)(2,1)S(1)} %all-to-all-done.12, f32[3072]{0:T(1024)S(1)} %bitcast.1143, f32[8,62,3072]{2,1,0:T(8,128)} %fusion.124), kind=kOutput, calls=%fused_computation.122 | convolution fusion | flops 2454696960 | bytes 14647296 | tf_op jit(solution)/shard_map/nkcd,kfd->nkcf/dot_general | solution.py:116
  322.0 20.0 %fusion.230 = bf16[8,1,62,768]{3,2,1,0:T(8,128)(2,1)} fusion(bf16[1,3072,768]{2,1,0:T(8,128)(2,1)} %all-gather.12.cloned.1.call-done, f32[8,62,3072]{2,1,0:T(8,128)} %fusion.124, f32[3072]{0:T(1024)S(1)} %bitcast.1144), kind=kOutput, calls=%fused_computation.286 | convolution fusion | flops 2441367552 | bytes 11587584 | tf_op jit(solution)/shard_map/nkcf,kfd->nkcd/dot_general | solution.py:96
  342.0 4.4 all-to-all-start.5
  351.4 7.7 all-to-all-done.5
  365.9 4.5 multiply_reduce_fusion.11
  370.7 20.9 %scatter_fusion.2 = f32[197,8]{0,1:T(8,128)S(1)} fusion(f32[197,8]{0,1:T(8,128)S(1)} %broadcast_in_dim.82.clone, s32[394]{0:T(512)S(1)} %reshape.1678, f32[394]{0:T(512)S(1)} %reshape.1680), kind=kCustom, calls=%fused_computation.30 | custom fusion | flops 394 | bytes 7880 | tf_op jit(solution)/shard_map/transpose(jvp(jit(take_along_axis)))/scatter-add | solution.py:32
  404.0 5.3 fusion.307
  409.3 6.0 fusion.310
  417.6 6.1 multiply_reduce_fusion.25
  470.7 4.6 gather_fusion.17
  498.8 4.6 gather_fusion.16
  519.6 4.6 gather_fusion.19
  544.6 5.2 fusion.459
  549.8 6.8 all-to-all-done.2
  560.7 6.8 fusion.126
  567.6 5.1 all-to-all-done
  576.9 20.5 %convert_reduce_fusion.2 = (f32[3072]{0:T(1024)}, bf16[8,1,62,3072]{3,2,0,1:T(8,128)(2,1)}) fusion(bf16[1,3072,768]{2,1,0:T(8,128)(2,1)} %all-gather.12.cloned.1.call-done, bf16[8,1,62,768]{3,2,1,0:T(8,128)(2,1)} %all-to-all-done.10, f32[3072]{0:T(1024)S(1)} %bitcast.1145, f32[8,62,3072]{2,1,0:T(8,128)} %fusion.126), kind=kOutput, calls=%fused_computation.123 | convolution fusion | flops 2454696960 | bytes 14647296 | tf_op jit(solution)/shard_map/nkcd,kfd->nkcf/dot_general | solution.py:116
  597.4 4.5 fusion.128
  606.3 20.4 %convert_reduce_fusion.3 = (f32[3072]{0:T(1024)}, bf16[8,1,62,3072]{3,2,0,1:T(8,128)(2,1)}) fusion(bf16[1,3072,768]{2,1,0:T(8,128)(2,1)} %all-gather.12.cloned.1.call-done, bf16[8,1,62,768]{3,2,1,0:T(8,128)(2,1)} %all-to-all-done.8, f32[3072]{0:T(1024)S(1)} %bitcast.1146, f32[8,62,3072]{2,1,0:T(8,128)} %fusion.128), kind=kOutput, calls=%fused_computation.124 | convolution fusion | flops 2454696960 | bytes 14647296 | tf_op jit(solution)/shard_map/nkcd,kfd->nkcf/dot_general | solution.py:116
  626.8 17.0 %fusion.233 = bf16[8,1,62,768]{3,2,1,0:T(8,128)(2,1)} fusion(bf16[1,3072,768]{2,1,0:T(8,128)(2,1)S(1)} %copy-done.280, f32[8,62,3072]{2,1,0:T(8,128)S(1)} %bitcast.1089, f32[3072]{0:T(1024)S(1)} %bitcast.1147), kind=kOutput, calls=%fused_computation.287 | convolution fusion | flops 2441367552 | bytes 11587584 | tf_op jit(solution)/shard_map/nkcf,kfd->nkcd/dot_general | solution.py:96
  648.0 7.0 fusion.249
  654.9 5.8 fusion.122
  665.9 20.6 %convert_reduce_fusion = (f32[3072]{0:T(1024)}, bf16[8,1,62,3072]{3,2,0,1:T(8,128)(2,1)}) fusion(bf16[1,3072,768]{2,1,0:T(8,128)(2,1)} %all-gather.12.cloned.1.call-done, bf16[8,1,62,768]{3,2,1,0:T(8,128)(2,1)} %copy-done.112, f32[3072]{0:T(1024)S(1)} %bitcast.1148, f32[8,62,3072]{2,1,0:T(8,128)} %fusion.122), kind=kOutput, calls=%fused_computation.121 | convolution fusion | flops 2454696960 | bytes 14647296 | tf_op jit(solution)/shard_map/nkcd,kfd->nkcf/dot_general | solution.py:116
  686.5 19.4 %fusion.236 = bf16[8,1,62,768]{3,2,1,0:T(8,128)(2,1)} fusion(bf16[1,3072,768]{2,1,0:T(8,128)(2,1)} %all-gather.12.cloned.1.call-done, f32[8,62,3072]{2,1,0:T(8,128)S(1)} %bitcast.1091, f32[3072]{0:T(1024)S(1)} %bitcast.1149), kind=kOutput, calls=%fused_computation.288 | convolution fusion | flops 2441367552 | bytes 11587584 | tf_op jit(solution)/shard_map/nkcf,kfd->nkcd/dot_general | solution.py:96
  710.1 6.8 fusion.254
  716.9 5.8 all-to-all-done.3
  726.4 20.0 %fusion.227 = bf16[8,1,62,768]{3,2,1,0:T(8,128)(2,1)} fusion(bf16[1,3072,768]{2,1,0:T(8,128)(2,1)} %all-gather.12.cloned.1.call-done, f32[8,62,3072]{2,1,0:T(8,128)} %fusion.122, f32[3072]{0:T(1024)S(1)} %bitcast.1150), kind=kOutput, calls=%fused_computation.285 | convolution fusion | flops 2441367552 | bytes 11587584 | tf_op jit(solution)/shard_map/nkcf,kfd->nkcd/dot_general | solution.py:96
  746.4 4.4 all-to-all-start.1
  750.9 6.8 fusion.239
  766.3 20.7 %scatter_fusion.1 = f32[197,8]{0,1:T(8,128)S(1)} fusion(f32[197,8]{0,1:T(8,128)S(1)} %broadcast_in_dim.82.clone.1, s32[394]{0:T(512)S(1)} %copy-done.30, f32[394]{0:T(512)S(1)} %reshape.1674), kind=kCustom, calls=%fused_computation.29 | custom fusion | flops 394 | bytes 7880 | tf_op jit(solution)/shard_map/transpose(jvp(jit(take_along_axis)))/scatter-add | solution.py:32
  787.0 4.6 all-to-all-start.15
  808.2 20.7 %scatter_fusion = f32[197,8]{0,1:T(8,128)S(1)} fusion(f32[197,8]{0,1:T(8,128)S(1)} %broadcast_in_dim.82.clone.2, s32[394]{0:T(512)S(1)} %copy-done.29, f32[394]{0:T(512)S(1)} %reshape.1668), kind=kCustom, calls=%fused_computation.28 | custom fusion | flops 394 | bytes 7880 | tf_op jit(solution)/shard_map/transpose(jvp(jit(take_along_axis)))/scatter-add | solution.py:32
  854.5 4.5 multiply_reduce_fusion.9
  859.3 20.9 %scatter_fusion.3 = f32[197,8]{0,1:T(8,128)S(1)} fusion(f32[197,8]{0,1:T(8,128)S(1)} %broadcast_in_dim.82.clone.3, s32[394]{0:T(512)S(1)} %copy-done.28, f32[394]{0:T(512)S(1)} %reshape.1686), kind=kCustom, calls=%fused_computation.31 | custom fusion | flops 394 | bytes 7880 | tf_op jit(solution)/shard_map/transpose(jvp(jit(take_along_axis)))/scatter-add | solution.py:32
  897.1 6.2 fusion.301
  903.2 6.3 fusion.304
  918.0 6.1 fusion.295
  924.1 6.1 fusion.298
  938.9 4.7 add_convert_fusion.1
  943.7 6.0 fusion.316
  953.6 6.0 fusion.313
  970.1 7.1 add_convert_fusion
  977.4 7.4 fusion.138
  984.8 19.0 %fusion.334 = f32[3072,768,1]{1,0,2:T(8,128)} fusion(bf16[8,1,62,768]{3,2,1,0:T(8,128)(2,1)S(1)} %copy-done.111, f32[8,62,3072]{2,1,0:T(8,128)} %fusion.124, f32[3072]{0:T(1024)S(1)} %bitcast.1151), kind=kOutput, calls=%fused_computation.384 | convolution fusion | flops 2440986624 | bytes 16306176 | tf_op jit(solution)/shard_map/nkcf,nkcd->kfd/dot_general | solution.py:119
  1005.5 7.3 fusion.141
  1014.9 7.0 fusion.144
  1021.9 20.8 %reduce-scatter.11.cloned.1.call-done = bf16[192,2304]{1,0:T(8,128)(2,1)} async-done(((bf16[768,2304]{1,0:T(8,128)(2,1)}), bf16[192,2304]{1,0:T(8,128)(2,1)}) %reduce-scatter.11.cloned.1.call-update) | async-done | bytes 884752 | tf_op jit(solution)/shard_map/reduce_scatter | solution.py:235
  1042.8 16.0 %fusion.130 = bf16[1,768,3072]{2,1,0:T(8,128)(2,1)} fusion(f32[768,3072,1]{1,0,2:T(8,128)} %fusion.138, f32[768,3072,1]{1,0,2:T(8,128)} %fusion.141, f32[768,3072,1]{1,0,2:T(8,128)} %fusion.144, bf16[8,1,62,3072]{3,2,0,1:T(8,128)(2,1)} %get-tuple-element.214, bf16[8,1,62,768]{3,2,1,0:T(8,128)(2,1)} %all-to-all-done.6), kind=kOutput, calls=%fused_computation.213 | convolution fusion | flops 2349858816 | bytes 36839424 | tf_op jit(solution)/shard_map/nkcd,nkcf->kdf/dot_general | solution.py:120
  1059.1 19.3 %fusion.337 = f32[3072,768,1]{1,0,2:T(8,128)} fusion(bf16[8,1,62,768]{3,2,1,0:T(8,128)(2,1)} %all-to-all-done.10, f32[8,62,3072]{2,1,0:T(8,128)} %fusion.126, f32[3072]{0:T(1024)S(1)} %bitcast.1152), kind=kOutput, calls=%fused_computation.387 | convolution fusion | flops 2440986624 | bytes 16306176 | tf_op jit(solution)/shard_map/nkcf,nkcd->kfd/dot_general | solution.py:119
  1078.3 19.3 %fusion.340 = f32[3072,768,1]{1,0,2:T(8,128)} fusion(bf16[8,1,62,768]{3,2,1,0:T(8,128)(2,1)} %all-to-all-done.8, f32[8,62,3072]{2,1,0:T(8,128)} %fusion.128, f32[3072]{0:T(1024)S(1)} %bitcast.1153), kind=kOutput, calls=%fused_computation.390 | convolution fusion | flops 2440986624 | bytes 16306176 | tf_op jit(solution)/shard_map/nkcf,nkcd->kfd/dot_general | solution.py:119
  1097.7 19.4 %fusion.131 = bf16[1,3072,768]{2,1,0:T(8,128)(2,1)} fusion(f32[3072,768,1]{1,0,2:T(8,128)S(1)} %bitcast.1169, f32[3072,768,1]{1,0,2:T(8,128)} %fusion.337, f32[3072,768,1]{1,0,2:T(8,128)} %fusion.340, bf16[8,1,62,768]{3,2,1,0:T(8,128)(2,1)S(1)} %copy-done.113, f32[8,62,3072]{2,1,0:T(8,128)S(1)} %bitcast.1093, f32[3072]{0:T(1024)S(1)} %bitcast.1154), kind=kOutput, calls=%fused_computation.214 | convolution fusion | flops 2450423808 | bytes 39899136 | tf_op jit(solution)/shard_map/nkcf,nkcd->kfd/dot_general | solution.py:119
  1132.2 10.8 all-reduce.10
  1152.1 12.1 all-reduce.8
  1171.4 65.0 %reduce-scatter.15.cloned.1.call-done = bf16[1,768,768]{2,1,0:T(8,128)(2,1)} async-done(((bf16[1,768,3072]{2,1,0:T(8,128)(2,1)}), bf16[1,768,768]{2,1,0:T(8,128)(2,1)}) %reduce-scatter.15.cloned.1.call-update) | async-done | bytes 1179664 | tf_op jit(solution)/shard_map/reduce_scatter | solution.py:255
  1239.2 85.3 %reduce-scatter.17.cloned.1.call-done = bf16[1,768,768]{2,1,0:T(8,128)(2,1)} async-done(((bf16[1,3072,768]{2,1,0:T(8,128)(2,1)}), bf16[1,768,768]{2,1,0:T(8,128)(2,1)}) %reduce-scatter.17.cloned.1.call-update) | async-done | bytes 1179664 | tf_op jit(solution)/shard_map/reduce_scatter | solution.py:261
  (994 shorter events, 405.0 us)
Async XLA Ops:
  7.2 31.9 %copy-start.260 = (s32[4]{0:T(128)S(1)}, s32[4]{0:T(128)}, u32[]{:S(2)}) copy-start(s32[4]{0:T(128)} %param.31) | copy-start | bytes 52
  7.2 33.6 %copy-start.266 = (bf16[192,8]{0,1:T(8,128)(2,1)S(1)}, bf16[192,8]{0,1:T(8,128)(2,1)}, u32[]{:S(2)}) copy-start(bf16[192,8]{0,1:T(8,128)(2,1)} %param.24) | copy-start | bytes 9220
  7.2 71.0 %copy-start.17 = (f32[788,768]{1,0:T(8,128)S(1)}, f32[788,768]{1,0:T(8,128)}, u32[]{:S(2)}) copy-start(f32[788,768]{1,0:T(8,128)} %param.17) | copy-start | bytes 7262212
  7.2 75.8 %all-gather.6.cloned.1.call-start = ((), (), s32[]{:S(2)}) async-start(), calls=%async_computation.22 | async-start | bytes 4423680 | tf_op jit(solution)/shard_map/all_gather | solution.py:202
  8.0 105.7 %all-gather.8.cloned.1.call-start = ((), (), s32[]{:S(2)}) async-start(), calls=%async_computation.23 | async-start | bytes 1474560 | tf_op jit(solution)/shard_map/all_gather | solution.py:203
  8.7 195.2 %all-gather.10.cloned.1.call-start = ((), (), s32[]{:S(2)}) async-start(), calls=%async_computation.24 | async-start | bytes 5898240 | tf_op jit(solution)/shard_map/all_gather | solution.py:209
  9.4 283.8 %all-gather.12.cloned.1.call-start = ((), (), s32[]{:S(2)}) async-start(), calls=%async_computation.25 | async-start | bytes 5898240 | tf_op jit(solution)/shard_map/all_gather | solution.py:211
  12.0 75.0 %copy-start.80 = (s32[197,2]{1,0:T(8,128)}, s32[197,2]{1,0:T(8,128)S(1)}, u32[]{:S(2)}) copy-start(s32[197,2]{1,0:T(8,128)S(1)} %copy.211) | copy-start | bytes 4732
  12.3 120.6 %copy-start.78 = (s32[197,2]{1,0:T(8,128)}, s32[197,2]{1,0:T(8,128)S(1)}, u32[]{:S(2)}) copy-start(s32[197,2]{1,0:T(8,128)S(1)} %copy.210) | copy-start | bytes 4732
  12.6 120.4 %copy-start.76 = (s32[197,2]{1,0:T(8,128)}, s32[197,2]{1,0:T(8,128)S(1)}, u32[]{:S(2)}) copy-start(s32[197,2]{1,0:T(8,128)S(1)} %copy.213) | copy-start | bytes 4732
  32.6 54.4 %copy-start.107 = (f32[768]{0:T(1024)}, f32[768]{0:T(1024)S(1)}, u32[]{:S(2)}) copy-start(f32[768]{0:T(1024)S(1)} %convert_element_type.568) | copy-start | bytes 9220
  32.6 54.4 %copy-start.92 = (f32[768]{0:T(1024)}, f32[768]{0:T(1024)S(1)}, u32[]{:S(2)}) copy-start(f32[768]{0:T(1024)S(1)} %convert_element_type.567) | copy-start | bytes 9220
  32.6 83.1 %copy-start.144 = (f32[768]{0:T(1024)}, f32[768]{0:T(1024)S(1)}, u32[]{:S(2)}) copy-start(f32[768]{0:T(1024)S(1)} %convert_element_type.576) | copy-start | bytes 9220
  40.8 75.0 %copy-start.154 = (f32[768]{0:T(1024)}, f32[768]{0:T(1024)S(1)}, u32[]{:S(2)}) copy-start(f32[768]{0:T(1024)S(1)} %convert_element_type.577) | copy-start | bytes 9220
  54.3 62.8 %copy-start.96 = (bf16[768,8]{0,1:T(8,128)(2,1)}, bf16[768,8]{0,1:T(8,128)(2,1)S(1)}, u32[]{:S(2)}) copy-start(bf16[768,8]{0,1:T(8,128)(2,1)S(1)} %reshape.1711) | copy-start | bytes 36868
  124.9 38.5 %copy-start.115 = (s32[197,2,1]{1,0,2:T(8,128)S(1)}, s32[197,2,1]{1,0,2:T(8,128)}, u32[]{:S(2)}) copy-start(s32[197,2,1]{1,0,2:T(8,128)} %get-tuple-element.129) | copy-start | bytes 4732
  128.6 16.3 %all-to-all-start.4 = ((bf16[8,1,62,768]{3,2,1,0:T(8,128)(2,1)}), bf16[8,1,62,768]{3,2,1,0:T(8,128)(2,1)S(1)}, u32[]{:S(2)}, u32[]{:S(2)}) async-start(bf16[8,1,62,768]{3,2,1,0:T(8,128)(2,1)} %get-tuple-element.175), calls=%async_computation.4 | async-start | bytes 1572864 | tf_op jit(solution)/shard_map/all_to_all | solution.py:92
  144.8 66.0 %copy-start.54 = (bf16[8,1,62,768]{3,2,1,0:T(8,128)(2,1)}, bf16[8,1,62,768]{3,2,1,0:T(8,128)(2,1)S(1)}, u32[]{:S(2)}) copy-start(bf16[8,1,62,768]{3,2,1,0:T(8,128)(2,1)S(1)} %all-to-all-done.4) | copy-start | bytes 2285572
  144.8 66.0 %all-to-all-start.12 = ((bf16[8,1,62,768]{3,2,1,0:T(8,128)(2,1)}), bf16[8,1,62,768]{3,2,1,0:T(8,128)(2,1)S(1)}, u32[]{:S(2)}, u32[]{:S(2)}) async-start(bf16[8,1,62,768]{3,2,1,0:T(8,128)(2,1)} %get-tuple-element.174), calls=%async_computation.12 | async-start | bytes 1572864 | tf_op jit(solution)/shard_map/all_to_all | solution.py:114
  163.1 158.9 %copy-start.225 = (f32[1,3072]{1,0:T(1,128)}, f32[1,3072]{1,0:T(1,128)S(1)}, u32[]{:S(2)}) copy-start(f32[1,3072]{1,0:T(1,128)S(1)} %add.711) | copy-start | bytes 36868
  163.4 47.4 %copy-start.122 = (pred[197,2]{1,0:T(8,128)(4,1)}, pred[197,2]{1,0:T(8,128)(4,1)S(1)}, u32[]{:S(2)}) copy-start(pred[197,2]{1,0:T(8,128)(4,1)S(1)} %lt.309) | copy-start | bytes 1186
  169.4 143.2 %copy-start.119 = (pred[197,2]{1,0:T(8,128)(4,1)}, pred[197,2]{1,0:T(8,128)(4,1)S(1)}, u32[]{:S(2)}) copy-start(pred[197,2]{1,0:T(8,128)(4,1)S(1)} %lt.297) | copy-start | bytes 1186
  175.4 137.2 %copy-start.116 = (pred[197,2]{1,0:T(8,128)(4,1)}, pred[197,2]{1,0:T(8,128)(4,1)S(1)}, u32[]{:S(2)}) copy-start(pred[197,2]{1,0:T(8,128)(4,1)S(1)} %lt.333) | copy-start | bytes 1186
  203.9 110.3 %slice-start = ((s8[4718592]{0:T(1024)(128)(4,1)}), s8[524288]{0:T(1024)(128)(4,1)S(1)}, s32[]{:S(2)}) async-start(s8[4718592]{0:T(1024)(128)(4,1)} %bitcast.1078), calls=%async_computation.33 | async-start | bytes 1048576
  210.9 101.7 %copy-start.110 = (bf16[8,1,62,768]{3,2,1,0:T(8,128)(2,1)}, bf16[8,1,62,768]{3,2,1,0:T(8,128)(2,1)S(1)}, u32[]{:S(2)}) copy-start(bf16[8,1,62,768]{3,2,1,0:T(8,128)(2,1)S(1)} %all-to-all-done.12) | copy-start | bytes 2285572
  317.8 24.3 %all-to-all-start.13 = ((bf16[8,1,62,768]{3,2,1,0:T(8,128)(2,1)}), bf16[8,1,62,768]{3,2,1,0:T(8,128)(2,1)S(1)}, u32[]{:S(2)}, u32[]{:S(2)}) async-start(bf16[8,1,62,768]{3,2,1,0:T(8,128)(2,1)} %fusion.244), calls=%async_computation.13 | async-start | bytes 1572864 | tf_op jit(solution)/shard_map/all_to_all | solution.py:125
  342.0 17.1 %all-to-all-start.5 = ((bf16[8,1,62,768]{3,2,1,0:T(8,128)(2,1)}), bf16[8,1,62,768]{3,2,1,0:T(8,128)(2,1)}, u32[]{:S(2)}, u32[]{:S(2)}) async-start(bf16[8,1,62,768]{3,2,1,0:T(8,128)(2,1)} %fusion.230), calls=%async_computation.5 | async-start | bytes 1572864 | tf_op jit(solution)/shard_map/all_to_all | solution.py:98
  346.5 77.2 %copy-start.218 = (f32[197]{0:T(256)}, f32[197]{0:T(256)S(1)}, u32[]{:S(2)}) copy-start(f32[197]{0:T(256)S(1)} %get-tuple-element.223) | copy-start | bytes 2368
  346.5 89.3 %copy-start.189 = (f32[197]{0:T(256)}, f32[197]{0:T(256)S(1)}, u32[]{:S(2)}) copy-start(f32[197]{0:T(256)S(1)} %get-tuple-element.224) | copy-start | bytes 2368
  398.0 116.3 %copy-start.60 = (f32[197,768]{1,0:T(8,128)}, f32[197,768]{1,0:T(8,128)S(1)}, u32[]{:S(2)}) copy-start(f32[197,768]{1,0:T(8,128)S(1)} %get-tuple-element.121) | copy-start | bytes 1815556
  398.0 140.0 %copy-start.46 = (f32[197,768]{1,0:T(8,128)}, f32[197,768]{1,0:T(8,128)S(1)}, u32[]{:S(2)}) copy-start(f32[197,768]{1,0:T(8,128)S(1)} %get-tuple-element.119) | copy-start | bytes 1815556
  469.7 39.6 %copy-start.12 = (bf16[197,768]{1,0:T(8,128)(2,1)}, bf16[197,768]{1,0:T(8,128)(2,1)S(1)}, u32[]{:S(2)}) copy-start(bf16[197,768]{1,0:T(8,128)(2,1)S(1)} %get-tuple-element.138) | copy-start | bytes 907780
  469.7 60.7 %copy-start.8 = (bf16[197,768]{1,0:T(8,128)(2,1)}, bf16[197,768]{1,0:T(8,128)(2,1)S(1)}, u32[]{:S(2)}) copy-start(bf16[197,768]{1,0:T(8,128)(2,1)S(1)} %get-tuple-element.140) | copy-start | bytes 907780
  470.7 56.8 %copy-start.183 = (f32[197]{0:T(256)}, f32[197]{0:T(256)S(1)}, u32[]{:S(2)}) copy-start(f32[197]{0:T(256)S(1)} %fusion.387) | copy-start | bytes 2368
  489.8 50.0 %all-to-all-start.10 = ((bf16[8,1,62,768]{3,2,1,0:T(8,128)(2,1)}), bf16[8,1,62,768]{3,2,1,0:T(8,128)(2,1)}, u32[]{:S(2)}, u32[]{:S(2)}) async-start(bf16[8,1,62,768]{3,2,1,0:T(8,128)(2,1)} %get-tuple-element.166), calls=%async_computation.10 | async-start | bytes 1572864 | tf_op jit(solution)/shard_map/all_to_all | solution.py:114
  498.8 45.2 %copy-start.178 = (f32[197]{0:T(256)}, f32[197]{0:T(256)S(1)}, u32[]{:S(2)}) copy-start(f32[197]{0:T(256)S(1)} %fusion.385) | copy-start | bytes 2368
  519.6 40.6 %copy-start.181 = (f32[197]{0:T(256)}, f32[197]{0:T(256)S(1)}, u32[]{:S(2)}) copy-start(f32[197]{0:T(256)S(1)} %fusion.391) | copy-start | bytes 2368
  539.9 16.7 %all-to-all-start.2 = ((bf16[8,1,62,768]{3,2,1,0:T(8,128)(2,1)}), bf16[8,1,62,768]{3,2,1,0:T(8,128)(2,1)S(1)}, u32[]{:S(2)}, u32[]{:S(2)}) async-start(bf16[8,1,62,768]{3,2,1,0:T(8,128)(2,1)} %get-tuple-element.167), calls=%async_computation.2 | async-start | bytes 1572864 | tf_op jit(solution)/shard_map/all_to_all | solution.py:92
  556.6 16.1 %all-to-all-start = ((bf16[8,1,62,768]{3,2,1,0:T(8,128)(2,1)}), bf16[8,1,62,768]{3,2,1,0:T(8,128)(2,1)S(1)}, u32[]{:S(2)}, u32[]{:S(2)}) async-start(bf16[8,1,62,768]{3,2,1,0:T(8,128)(2,1)} %get-tuple-element.163), calls=%async_computation | async-start | bytes 1572864 | tf_op jit(solution)/shard_map/all_to_all | solution.py:92
  560.7 36.7 %slice-start.2 = ((s8[4718592]{0:T(1024)(128)(4,1)}), s8[524288]{0:T(1024)(128)(4,1)S(1)}, s32[]{:S(2)}) async-start(s8[4718592]{0:T(1024)(128)(4,1)} %bitcast.1080), calls=%async_computation.35 | async-start | bytes 1048576
  572.7 29.3 %all-to-all-start.8 = ((bf16[8,1,62,768]{3,2,1,0:T(8,128)(2,1)}), bf16[8,1,62,768]{3,2,1,0:T(8,128)(2,1)}, u32[]{:S(2)}, u32[]{:S(2)}) async-start(bf16[8,1,62,768]{3,2,1,0:T(8,128)(2,1)} %get-tuple-element.162), calls=%async_computation.8 | async-start | bytes 1572864 | tf_op jit(solution)/shard_map/all_to_all | solution.py:114
  601.9 41.9 %all-to-all-start.6 = ((bf16[8,1,62,768]{3,2,1,0:T(8,128)(2,1)}), bf16[8,1,62,768]{3,2,1,0:T(8,128)(2,1)}, u32[]{:S(2)}, u32[]{:S(2)}) async-start(bf16[8,1,62,768]{3,2,1,0:T(8,128)(2,1)} %get-tuple-element.171), calls=%async_computation.6 | async-start | bytes 1572864 | tf_op jit(solution)/shard_map/all_to_all | solution.py:92
  643.8 16.9 %all-to-all-start.14 = ((bf16[8,1,62,768]{3,2,1,0:T(8,128)(2,1)}), bf16[8,1,62,768]{3,2,1,0:T(8,128)(2,1)S(1)}, u32[]{:S(2)}, u32[]{:S(2)}) async-start(bf16[8,1,62,768]{3,2,1,0:T(8,128)(2,1)} %get-tuple-element.170), calls=%async_computation.14 | async-start | bytes 1572864 | tf_op jit(solution)/shard_map/all_to_all | solution.py:114
  661.7 44.2 %all-to-all-start.11 = ((bf16[8,1,62,768]{3,2,1,0:T(8,128)(2,1)}), bf16[8,1,62,768]{3,2,1,0:T(8,128)(2,1)S(1)}, u32[]{:S(2)}, u32[]{:S(2)}) async-start(bf16[8,1,62,768]{3,2,1,0:T(8,128)(2,1)} %fusion.249), calls=%async_computation.11 | async-start | bytes 1572864 | tf_op jit(solution)/shard_map/all_to_all | solution.py:125
  705.9 16.8 %all-to-all-start.3 = ((bf16[8,1,62,768]{3,2,1,0:T(8,128)(2,1)}), bf16[8,1,62,768]{3,2,1,0:T(8,128)(2,1)S(1)}, u32[]{:S(2)}, u32[]{:S(2)}) async-start(bf16[8,1,62,768]{3,2,1,0:T(8,128)(2,1)} %fusion.233), calls=%async_computation.3 | async-start | bytes 1572864 | tf_op jit(solution)/shard_map/all_to_all | solution.py:98
  722.7 23.7 %all-to-all-start.9 = ((bf16[8,1,62,768]{3,2,1,0:T(8,128)(2,1)}), bf16[8,1,62,768]{3,2,1,0:T(8,128)(2,1)S(1)}, u32[]{:S(2)}, u32[]{:S(2)}) async-start(bf16[8,1,62,768]{3,2,1,0:T(8,128)(2,1)} %fusion.254), calls=%async_computation.9 | async-start | bytes 1572864 | tf_op jit(solution)/shard_map/all_to_all | solution.py:125
  746.4 40.6 %all-to-all-start.1 = ((bf16[8,1,62,768]{3,2,1,0:T(8,128)(2,1)}), bf16[8,1,62,768]{3,2,1,0:T(8,128)(2,1)}, u32[]{:S(2)}, u32[]{:S(2)}) async-start(bf16[8,1,62,768]{3,2,1,0:T(8,128)(2,1)} %fusion.236), calls=%async_computation.1 | async-start | bytes 1572864 | tf_op jit(solution)/shard_map/all_to_all | solution.py:98
  787.0 55.0 %copy-start.2 = (f32[197,8]{0,1:T(8,128)}, f32[197,8]{0,1:T(8,128)S(1)}, u32[]{:S(2)}) copy-start(f32[197,8]{0,1:T(8,128)S(1)} %scatter_fusion.1) | copy-start | bytes 18916
  787.0 42.0 %all-to-all-start.15 = ((bf16[8,1,62,768]{3,2,1,0:T(8,128)(2,1)}), bf16[8,1,62,768]{3,2,1,0:T(8,128)(2,1)}, u32[]{:S(2)}, u32[]{:S(2)}) async-start(bf16[8,1,62,768]{3,2,1,0:T(8,128)(2,1)} %fusion.239), calls=%async_computation.15 | async-start | bytes 1572864 | tf_op jit(solution)/shard_map/all_to_all | solution.py:125
  795.9 46.1 %copy-start.248 = (f32[197]{0:T(256)}, f32[197]{0:T(256)S(1)}, u32[]{:S(2)}) copy-start(f32[197]{0:T(256)S(1)} %neg.96) | copy-start | bytes 2368
  829.0 18.7 %all-to-all-start.7 = ((bf16[8,1,62,768]{3,2,1,0:T(8,128)(2,1)}), bf16[8,1,62,768]{3,2,1,0:T(8,128)(2,1)}, u32[]{:S(2)}, u32[]{:S(2)}) async-start(bf16[8,1,62,768]{3,2,1,0:T(8,128)(2,1)} %fusion.227), calls=%async_computation.7 | async-start | bytes 1572864 | tf_op jit(solution)/shard_map/all_to_all | solution.py:98
  833.3 188.7 %reduce-scatter.13.cloned.1.call-start = ((), (), s32[]{:S(2)}) async-start(), calls=%async_computation.27 | async-start | bytes 1474560 | tf_op jit(solution)/shard_map/reduce_scatter | solution.py:238
  888.5 41.7 %copy-start.48 = (f32[197,768]{1,0:T(8,128)}, f32[197,768]{1,0:T(8,128)S(1)}, u32[]{:S(2)}) copy-start(f32[197,768]{1,0:T(8,128)S(1)} %get-tuple-element.115) | copy-start | bytes 1815556
  888.5 43.6 %copy-start.50 = (f32[197,768]{1,0:T(8,128)}, f32[197,768]{1,0:T(8,128)S(1)}, u32[]{:S(2)}) copy-start(f32[197,768]{1,0:T(8,128)S(1)} %get-tuple-element.116) | copy-start | bytes 1815556
  888.5 50.3 %copy-start.52 = (f32[197,768]{1,0:T(8,128)}, f32[197,768]{1,0:T(8,128)S(1)}, u32[]{:S(2)}) copy-start(f32[197,768]{1,0:T(8,128)S(1)} %get-tuple-element.117) | copy-start | bytes 1815556
  943.6 99.1 %reduce-scatter.11.cloned.1.call-start = ((), (), s32[]{:S(2)}) async-start(), calls=%async_computation.26 | async-start | bytes 4423680 | tf_op jit(solution)/shard_map/reduce_scatter | solution.py:235
  977.3 140.9 %reduce-scatter.21.cloned.1.call-start = ((), (), s32[]{:S(2)}) async-start(), calls=%async_computation.31 | async-start | bytes 983040
  1005.5 145.8 %reduce-scatter.19.cloned.1.call-start = ((), (), s32[]{:S(2)}) async-start(), calls=%async_computation.30 | async-start | bytes 245760
  1014.8 152.3 %all-reduce.14.cloned.1.call-start = ((), (), s32[]{:S(2)}) async-start(), calls=%async_computation.32 | async-start | bytes 2359296 | tf_op jit(solution)/shard_map/psum | solution.py:252
  1042.8 193.6 %reduce-scatter.15.cloned.1.call-start = ((), (), s32[]{:S(2)}) async-start(), calls=%async_computation.28 | async-start | bytes 5898240 | tf_op jit(solution)/shard_map/reduce_scatter | solution.py:255
  1058.8 265.7 %reduce-scatter.17.cloned.1.call-start = ((), (), s32[]{:S(2)}) async-start(), calls=%async_computation.29 | async-start | bytes 5898240 | tf_op jit(solution)/shard_map/reduce_scatter | solution.py:261
  1059.0 38.6 %slice-start.10 = ((s8[6291456]{0:T(1024)(128)(4,1)}), s8[4194304]{0:T(1024)(128)(4,1)S(1)}, s32[]{:S(2)}) async-start(s8[6291456]{0:T(1024)(128)(4,1)} %bitcast.1092), calls=%async_computation.43 | async-start | bytes 8388608
  1059.1 38.6 %slice-start.12 = ((s8[9437184]{0:T(1024)(128)(4,1)}), s8[4194304]{0:T(1024)(128)(4,1)S(1)}, s32[]{:S(2)}) async-start(s8[9437184]{0:T(1024)(128)(4,1)} %bitcast.1168), calls=%async_computation.45 | async-start | bytes 8388608
  1059.1 38.6 %slice-start.13 = ((s8[9437184]{0:T(1024)(128)(4,1)}), s8[4194304]{0:T(1024)(128)(4,1)S(1)}, s32[]{:S(2)}) async-start(s8[9437184]{0:T(1024)(128)(4,1)} %bitcast.1168), calls=%async_computation.46 | async-start | bytes 8388608
  (259 other events, 2771.8 us)
Sparse Core Ops, SparseCore 0:
  9.6 73.3 all-gather.5
  84.6 29.0 all-gather.7
  115.2 88.6 all-gather.9
  205.4 87.8 all-gather.11
  943.8 28.1 reduce-scatter.12
  977.4 65.3 reduce-scatter.10
  1045.6 23.5 reduce-scatter.20
  1072.1 18.6 reduce-scatter.18
  1094.3 55.3 all-reduce.13
  1151.9 84.4 reduce-scatter.14
  1238.7 85.7 reduce-scatter.16
where the time goes:
time: 1350 us; the launch traced here: 1330 us
  matrix products  489 us (36%)
  waiting for transfers between devices  337 us (25%)
  local copies, waits for them, and re-layouts  179 us (13%)
  other arithmetic  179 us (13%)
  starting transfers between devices  66.4 us (5%)
  blocking collectives  64.1 us (5%)
  between operations  20.4 us (2%)
    reduce_scatter x1, waiting for transfers between devices, per_device(): lax.psum_scatter(expert_accum[2].astype(jnp.bfloat16), 'dp', scatter_dime...  85.3 us
    scatter-add x8, other arithmetic, gate_pick(): jnp.take_along_axis(jax.nn.softmax(logits, axis=-1), route_rows, axis=1)  84 us
    all_gather x1, waiting for transfers between devices, per_device(): lax.all_gather(expert_out, 'dp', axis=1, tiled=True)  82.4 us
    dot_general x4, matrix products, micro_step(): jnp.einsum('nkcd,kfd->nkcf', grad_recv, w_out, preferred_element_type=jnp...  80.9 us
    dot_general x4, matrix products, micro_step(): jnp.einsum('nkcf,nkcd->kfd', active, grad_recv, preferred_element_type=jn...  77 us
    dot_general x4, matrix products, micro_step(): jnp.einsum('nkcf,kfd->nkcd', active, w_out, preferred_element_type=jnp.fl...  76.4 us
    reduce_scatter x1, waiting for transfers between devices, per_device(): lax.psum_scatter(expert_accum[0].astype(jnp.bfloat16), 'dp', scatter_dime...  65 us
    dot_general x4, matrix products, micro_step(): jnp.einsum('nkcd,nkcf->kdf', received, d_pre, preferred_element_type=jnp....  37.7 us
  transfers between devices with their start and end apart: 27, of which 12 were waited for; matrix products, arithmetic and copies ran while one was open for 44% of the time, Pallas kernels for 0%

commit v1 on v0

v1 whole, which is shorter than its diff:
```python
import functools

import jax
import jax.numpy as jnp
from jax import lax
from jax.experimental import pallas as pl
from jax.experimental.pallas import tpu as pltpu
from jax.sharding import PartitionSpec as P

HEADS = 12
HEAD = 64
SEQ = 197
SEQ_PAD = 208
EPS = 1e-06
BF = jnp.bfloat16
F32 = jnp.float32
SMALL = 128
BIAS_ROWS = 16
NEG = -1e30
VMEM_LIMIT = 60 * 1024 * 1024


def ceil_to(value, step):
    return (value + step - 1) // step * step


def dot(a, b):
    return jnp.dot(a, b, preferred_element_type=F32)


def dot_nt(a, b):
    return lax.dot_general(a, b, (((1,), (1,)), ((), ())), preferred_element_type=F32)


def dot_tn(a, b):
    return lax.dot_general(a, b, (((0,), (0,)), ((), ())), preferred_element_type=F32)


def params(count=1):
    return pltpu.CompilerParams(
        dimension_semantics=("arbitrary",) * count, vmem_limit_bytes=VMEM_LIMIT
    )


def route_kernel(cap_pad, cols_ref, rows_ref, limit_ref, slot_rows_ref, slot_cols_ref):
    for b in range(cols_ref.shape[0]):
        limit = limit_ref[b]
        col = [cols_ref[b, :, k : k + 1] for k in range(4)]
        row = [rows_ref[b, k : k + 1, :] for k in range(4)]
        slot_rows_ref[b] = jnp.full(slot_rows_ref.shape[1:], -1, jnp.int32)
        slot_cols_ref[b] = jnp.full(slot_cols_ref.shape[1:], -1, jnp.int32)
        for j in range(2):
            rank_row = 0
            rank_col = 0
            for k in range(2):
                hit = (col[k] == row[j]) & (col[2 + k] < row[2 + j])
                rank_row = rank_row + jnp.sum(hit.astype(jnp.int32), axis=0, keepdims=True)
                hit = (row[k] == col[j]) & (row[2 + k] < col[2 + j])
                rank_col = rank_col + jnp.sum(hit.astype(jnp.int32), axis=1, keepdims=True)
            keep_row = (rank_row < limit) & (row[j] >= 0)
            keep_col = (rank_col < limit) & (col[j] >= 0)
            slot_rows_ref[b, j : j + 1, :] = jnp.where(keep_row, row[j] * cap_pad + rank_row, -1)
            slot_cols_ref[b, :, j : j + 1] = jnp.where(keep_col, col[j] * cap_pad + rank_col, -1)


def run_route(cols, rows, limits, cap_pad):
    batches = cols.shape[0]
    return pl.pallas_call(
        functools.partial(route_kernel, cap_pad),
        out_shape=(
            jax.ShapeDtypeStruct((batches, 8, SEQ_PAD), jnp.int32),
            jax.ShapeDtypeStruct((batches, SEQ_PAD, 8), jnp.int32),
        ),
        in_specs=[
            pl.BlockSpec(memory_space=pltpu.VMEM),
            pl.BlockSpec(memory_space=pltpu.VMEM),
            pl.BlockSpec(memory_space=pltpu.SMEM),
        ],
        out_specs=(
            pl.BlockSpec(memory_space=pltpu.VMEM),
            pl.BlockSpec(memory_space=pltpu.VMEM),
        ),
        compiler_params=pltpu.CompilerParams(vmem_limit_bytes=VMEM_LIMIT),
        cost_estimate=pl.CostEstimate(flops=4000000, bytes_accessed=1000000, transcendentals=0),
        name="route",
    )(cols, rows, limits)


def norm_stats(values):
    average = jnp.mean(values, axis=-1, keepdims=True)
    centered = values - average
    spread = jnp.mean(centered * centered, axis=-1, keepdims=True)
    inverse = lax.rsqrt(spread + EPS)
    return centered * inverse, inverse


def front_kernel(
    experts,
    x_ref,
    grad_ref,
    weight_ref,
    cols_ref,
    slot_rows_ref,
    send_ref,
    qkv_ref,
    mixed_ref,
    lse_ref,
    hidden_ref,
    one_ref,
    two_ref,
    probs_ref,
    small_ref,
):
    width = x_ref.shape[-1]
    rows = x_ref.shape[1]

    @pl.when(pl.program_id(0) == 0)
    def _():
        small_ref[...] = weight_ref[:, 4 * width :].astype(F32).T

    x = x_ref[0]
    hat, _ = norm_stats(x)
    one = (hat * small_ref[0:1, :] + small_ref[1:2, :]).astype(BF)
    one_ref[0] = one
    qkv_ref[0] = dot(one, weight_ref[:, : 3 * width]).astype(BF)
    lane = lax.broadcasted_iota(jnp.int32, (1, 128), 1)
    key_ok = lax.broadcasted_iota(jnp.int32, (1, rows), 1) < SEQ
    lse = jnp.zeros((rows, 128), F32)
    scale = HEAD ** (-0.5)
    for pair in range(HEADS // 2):
        low = pair * 128
        query = qkv_ref[0, :, low : low + 128]
        keys = qkv_ref[0, :, width + low : width + low + 128]
        values = qkv_ref[0, :, 2 * width + low : 2 * width + low + 128]
        total = None
        for side in range(2):
            mine = (lane // HEAD) == side
            scores = dot_nt(jnp.where(mine, query, jnp.zeros_like(query)), keys) * scale
            scores = jnp.where(key_ok, scores, NEG)
            highest = jnp.max(scores, axis=-1, keepdims=True)
            expo = jnp.exp(scores - highest)
            denom = jnp.sum(expo, axis=-1, keepdims=True)
            weights = (expo / denom).astype(BF)
            lse = jnp.where(lane == 2 * pair + side, highest + jnp.log(denom), lse)
            part = dot(weights, jnp.where(mine, values, jnp.zeros_like(values)))
            total = part if total is None else total + part
        mixed_ref[0, :, low : low + 128] = total.astype(BF)
    lse_ref[0] = lse
    hidden = x + dot(mixed_ref[0], weight_ref[:, 3 * width : 4 * width])
    hidden_ref[0] = hidden
    hat, _ = norm_stats(hidden)
    two = (hat * small_ref[2:3, :] + small_ref[3:4, :]).astype(BF)
    two_ref[0] = two
    logits = dot(two, weight_ref[:, 4 * width :])
    in_router = (lane >= 4) & (lane < 4 + experts)
    logits = jnp.where(in_router, logits, NEG)
    expo = jnp.exp(logits - jnp.max(logits, axis=-1, keepdims=True))
    probs = expo / jnp.sum(expo, axis=-1, keepdims=True)
    probs_ref[0] = probs
    out_grad = grad_ref[0]
    slots = send_ref.shape[0] * send_ref.shape[3]
    slot = lax.broadcasted_iota(jnp.int32, (slots, 1), 0)
    both = None
    grads = None
    for j in range(2):
        gate = jnp.sum(
            jnp.where(lane - 4 == cols_ref[0, :, j : j + 1], probs, 0.0), axis=-1, keepdims=True
        )
        pick = (slot == slot_rows_ref[0, j : j + 1, :]).astype(F32)
        both = pick if both is None else both + pick
        part = dot(pick.astype(BF), (gate * out_grad).astype(BF))
        grads = part if grads is None else grads + part
    sent = dot(both.astype(BF), two).astype(BF)
    send_ref[:, 0, 0] = sent.reshape(send_ref.shape[0], send_ref.shape[3], width)
    send_ref[:, 0, 1] = grads.astype(BF).reshape(send_ref.shape[0], send_ref.shape[3], width)


def run_front(x, grad, weight, cols, slot_rows, experts, cap_pad):
    batches, rows, width = x.shape
    total = weight.shape[1]

    def block(*shape):
        return pl.BlockSpec((1,) + shape, lambda i: (i,) + (0,) * len(shape))

    def out(shape, dtype):
        return jax.ShapeDtypeStruct((batches,) + shape, dtype)

    return pl.pallas_call(
        functools.partial(front_kernel, experts),
        grid=(batches,),
        out_shape=(
            jax.ShapeDtypeStruct((experts, batches, 2, cap_pad, width), BF),
            out((rows, 3 * width), BF),
            out((rows, width), BF),
            out((rows, 128), F32),
            out((rows, width), F32),
            out((rows, width), BF),
            out((rows, width), BF),
            out((rows, SMALL), F32),
        ),
        in_specs=[
            block(rows, width),
            block(rows, width),
            pl.BlockSpec((width, total), lambda i: (0, 0), pipeline_mode=pl.Buffered(1)),
            block(rows, 4),
            block(8, rows),
        ],
        out_specs=(
            pl.BlockSpec((experts, 1, 2, cap_pad, width), lambda i: (0, i, 0, 0, 0)),
            block(rows, 3 * width),
            block(rows, width),
            block(rows, 128),
            block(rows, width),
            block(rows, width),
            block(rows, width),
            block(rows, SMALL),
        ),
        scratch_shapes=[pltpu.VMEM((SMALL, width), F32)],
        compiler_params=params(),
        cost_estimate=pl.CostEstimate(
            flops=8000000000, bytes_accessed=40000000, transcendentals=3000000
        ),
        name="front",
    )(x, grad, weight, cols, slot_rows)


def expert_kernel(first, last, *refs):
    refs = list(refs)
    x_ref, grad_ref, win_ref, wout_ref = refs[:4]
    refs = refs[4:]
    if not first:
        y_in, dx_in = refs[:2]
        refs = refs[2:]
    back_refs = refs[:1] if last else refs[:2]
    refs = refs[len(back_refs) :]
    gin_ref, gout_ref, y_acc, dx_acc, gin_acc, gout_acc = refs
    shard = pl.program_id(0)
    block = pl.program_id(1)
    shards = pl.num_programs(0)
    blocks = pl.num_programs(1)
    width = x_ref.shape[-1]
    rows = x_ref.shape[0] * x_ref.shape[1] * x_ref.shape[3]
    x = x_ref[...].reshape(rows, width)
    grad = grad_ref[...].reshape(rows, width)
    win = win_ref[0, :width, :]
    wout = wout_ref[0]
    pre = dot(x, win) + win_ref[0, width : width + 1, :].astype(F32)
    cdf = 0.5 * lax.erf(pre * (0.5**0.5)) + 0.5
    active = (pre * cdf).astype(BF)
    slope = cdf + pre * (jnp.exp(-0.5 * pre * pre) * 0.3989422804014327)
    d_pre = dot_nt(grad, wout) * slope
    d_pre = d_pre.astype(BF)
    here = pl.ds(pl.multiple_of(block * rows, rows), rows)
    y_part = dot(active, wout)
    dx_part = dot_nt(d_pre, win)

    @pl.when(shard == 0)
    def _():
        if first:
            y_acc[here, :] = y_part
            dx_acc[here, :] = dx_part
        else:
            y_acc[here, :] = y_part + y_in[here, :]
            dx_acc[here, :] = dx_part + dx_in[here, :]

    @pl.when(shard > 0)
    def _():
        y_acc[here, :] += y_part
        dx_acc[here, :] += dx_part

    gout = dot_tn(active, grad)
    gin = dot_tn(x, d_pre)
    gbias = jnp.sum(d_pre.astype(F32), axis=0, keepdims=True)

    @pl.when(block == 0)
    def _():
        gout_acc[...] = gout
        gin_acc[:width, :] = gin
        gin_acc[width : width + 1, :] = gbias

    @pl.when(block > 0)
    def _():
        gout_acc[...] += gout
        gin_acc[:width, :] += gin
        gin_acc[width : width + 1, :] += gbias

    @pl.when(block == blocks - 1)
    def _():
        gout_ref[0] = gout_acc[...].astype(BF)
        gin_ref[0, :width, :] = gin_acc[:width, :].astype(BF)
        gin_ref[0, width:, :] = jnp.broadcast_to(
            gin_acc[width : width + 1, :].astype(BF), (BIAS_ROWS, gin_acc.shape[1])
        )

    @pl.when(shard == shards - 1)
    def _():
        if last:
            shape = (x_ref.shape[0], x_ref.shape[1], x_ref.shape[3], width)
            back_refs[0][:, :, 0] = y_acc[here, :].astype(BF).reshape(shape)
            back_refs[0][:, :, 1] = dx_acc[here, :].astype(BF).reshape(shape)
        else:
            back_refs[0][...] = y_acc[here, :]
            back_refs[1][...] = dx_acc[here, :]


def run_expert(received, win, wout, carried, last):
    sources, batches, _, cap_pad, width = received.shape
    shards, tall, span = win.shape
    group = max(1, 512 // (batches * cap_pad))
    while sources % group:
        group -= 1
    blocks = sources // group
    rows = group * batches * cap_pad
    total = sources * batches * cap_pad
    first = carried is None
    final = shards - 1

    def take(kind):
        return pl.BlockSpec((group, batches, 1, cap_pad, width), lambda s, r: (r, 0, kind, 0, 0))

    in_specs = [
        take(0),
        take(1),
        pl.BlockSpec((1, tall, span), lambda s, r: (s, 0, 0)),
        pl.BlockSpec((1, span, width), lambda s, r: (s, 0, 0)),
    ]
    operands = [received, received, win, wout]
    if not first:
        in_specs += [pl.BlockSpec((total, width), lambda s, r: (0, 0), pipeline_mode=pl.Buffered(1))] * 2
        operands += list(carried)
    if last:
        out_shape = [jax.ShapeDtypeStruct(received.shape, BF)]
        out_specs = [
            pl.BlockSpec(
                (group, batches, 2, cap_pad, width),
                lambda s, r: (jnp.where(s == final, r, 0), 0, 0, 0, 0),
            )
        ]
    else:
        out_shape = [jax.ShapeDtypeStruct((total, width), F32)] * 2
        out_specs = [pl.BlockSpec((rows, width), lambda s, r: (jnp.where(s == final, r, 0), 0))] * 2
    out_shape += [
        jax.ShapeDtypeStruct(win.shape, BF),
        jax.ShapeDtypeStruct(wout.shape, BF),
    ]
    out_specs += [
        pl.BlockSpec((1, tall, span), lambda s, r: (s, 0, 0)),
        pl.BlockSpec((1, span, width), lambda s, r: (s, 0, 0)),
    ]
    return pl.pallas_call(
        functools.partial(expert_kernel, first, last),
        grid=(shards, blocks),
        out_shape=tuple(out_shape),
        in_specs=in_specs,
        out_specs=tuple(out_specs),
        scratch_shapes=[
            pltpu.VMEM((total, width), F32),
            pltpu.VMEM((total, width), F32),
            pltpu.VMEM((tall, span), F32),
            pltpu.VMEM((span, width), F32),
        ],
        compiler_params=params(2),
        cost_estimate=pl.CostEstimate(
            flops=12 * total * width * span * shards,
            bytes_accessed=40000000,
            transcendentals=2 * total * span * shards,
        ),
        name="expert",
    )(*operands)


def tail_kernel(
    experts,
    x_ref,
    grad_ref,
    weight_ref,
    cols_ref,
    slot_cols_ref,
    back_ref,
    qkv_ref,
    mixed_ref,
    lse_ref,
    hidden_ref,
    one_ref,
    two_ref,
    probs_ref,
    out_ref,
    dx_ref,
    dense_ref,
    small_ref,
    sums_ref,
    d_qkv_ref,
    d_branch_ref,
    d_logits_ref,
    one_all,
    two_all,
    mixed_all,
):
    width = x_ref.shape[-1]
    rows = x_ref.shape[1]
    index = pl.program_id(0)

    @pl.when(index == 0)
    def _():
        small_ref[...] = weight_ref[:, 4 * width :].astype(F32).T
        sums_ref[...] = jnp.zeros_like(sums_ref)

    here = pl.ds(pl.multiple_of(index * rows, rows), rows)
    one_all[here, :] = one_ref[0]
    two_all[here, :] = two_ref[0]
    mixed_all[here, :] = mixed_ref[0]
    out_grad = grad_ref[0]
    hidden = hidden_ref[0]
    probs = probs_ref[0]
    lane = lax.broadcasted_iota(jnp.int32, (1, 128), 1)
    slots = back_ref.shape[0] * back_ref.shape[3]
    slot = lax.broadcasted_iota(jnp.int32, (1, slots), 1)
    answers = back_ref[:, 0, 0].reshape(slots, width)
    answer_grads = back_ref[:, 0, 1].reshape(slots, width)
    result = hidden
    d_probs = jnp.zeros_like(probs)
    both = None
    for j in range(2):
        pick = (slot == slot_cols_ref[0, :, j : j + 1]).astype(F32)
        both = pick if both is None else both + pick
        chosen = lane - 4 == cols_ref[0, :, j : j + 1]
        gate = jnp.sum(jnp.where(chosen, probs, 0.0), axis=-1, keepdims=True)
        picked = dot(pick.astype(BF), answers)
        result = result + gate * picked
        d_gate = jnp.sum(picked * out_grad, axis=-1, keepdims=True)
        d_probs = jnp.where(chosen, d_gate, d_probs)
    out_ref[0] = result
    d_logits = probs * (d_probs - jnp.sum(d_probs * probs, axis=-1, keepdims=True))
    d_logits = d_logits.astype(BF)
    d_logits_ref[here, :] = d_logits
    d_two = dot(both.astype(BF), answer_grads) + dot_nt(d_logits, weight_ref[:, 4 * width :])
    hat, inverse = norm_stats(hidden)
    sums_ref[2:3, :] += jnp.sum(d_two * hat, axis=0, keepdims=True)
    sums_ref[3:4, :] += jnp.sum(d_two, axis=0, keepdims=True)
    d_hat = d_two * small_ref[2:3, :]
    d_hidden = out_grad + inverse * (
        d_hat
        - jnp.mean(d_hat, axis=-1, keepdims=True)
        - hat * jnp.mean(d_hat * hat, axis=-1, keepdims=True)
    )
    d_branch = d_hidden.astype(BF)
    d_branch_ref[here, :] = d_branch
    d_mixed_all = dot_nt(d_branch, weight_ref[:, 3 * width : 4 * width]).astype(BF)
    key_ok = lax.broadcasted_iota(jnp.int32, (1, rows), 1) < SEQ
    scale = HEAD ** (-0.5)
    for pair in range(HEADS // 2):
        low = pair * 128
        query = qkv_ref[0, :, low : low + 128]
        keys = qkv_ref[0, :, width + low : width + low + 128]
        values = qkv_ref[0, :, 2 * width + low : 2 * width + low + 128]
        d_mixed = d_mixed_all[:, low : low + 128]
        d_query = d_keys = d_values = None
        for side in range(2):
            mine = (lane // HEAD) == side
            head = 2 * pair + side

            def own(array):
                return jnp.where(mine, array, jnp.zeros_like(array))

            my_query = own(query)
            my_keys = own(keys)
            my_d_mixed = own(d_mixed)
            scores = dot_nt(my_query, keys) * scale
            scores = jnp.where(key_ok, scores, NEG)
            probs_h = jnp.exp(scores - lse_ref[0, :, head : head + 1])
            d_weights = dot_nt(my_d_mixed, values)
            row_terms = jnp.sum(d_weights * probs_h, axis=-1, keepdims=True)
            d_scores = (probs_h * (d_weights - row_terms) * scale).astype(BF)
            parts = (
                dot(d_scores, my_keys),
                dot_tn(d_scores, my_query),
                dot_tn(probs_h.astype(BF), my_d_mixed),
            )
            if side == 0:
                d_query, d_keys, d_values = parts
            else:
                d_query, d_keys, d_values = (
                    d_query + parts[0],
                    d_keys + parts[1],
                    d_values + parts[2],
                )
        d_qkv_ref[here, low : low + 128] = d_query.astype(BF)
        d_qkv_ref[here, width + low : width + low + 128] = d_keys.astype(BF)
        d_qkv_ref[here, 2 * width + low : 2 * width + low + 128] = d_values.astype(BF)
    d_one = dot_nt(d_qkv_ref[here, :], weight_ref[:, : 3 * width])
    hat, inverse = norm_stats(x_ref[0])
    sums_ref[0:1, :] += jnp.sum(d_one * hat, axis=0, keepdims=True)
    sums_ref[1:2, :] += jnp.sum(d_one, axis=0, keepdims=True)
    d_hat = d_one * small_ref[0:1, :]
    dx_ref[0] = d_hidden + inverse * (
        d_hat
        - jnp.mean(d_hat, axis=-1, keepdims=True)
        - hat * jnp.mean(d_hat * hat, axis=-1, keepdims=True)
    )

    @pl.when(index == pl.num_programs(0) - 1)
    def _():
        dense_ref[:, 4 * width :] = (dot_tn(two_all[...], d_logits_ref[...]) + sums_ref[...].T).astype(BF)
        dense_ref[:, 3 * width : 4 * width] = dot_tn(mixed_all[...], d_branch_ref[...]).astype(BF)
        for part in range(3):
            cut = slice(part * width, (part + 1) * width)
            dense_ref[:, cut] = dot_tn(one_all[...], d_qkv_ref[:, cut]).astype(BF)


def run_tail(x, grad, weight, cols, slot_cols, back, saved, experts):
    batches, rows, width = x.shape
    total = weight.shape[1]
    cap_pad = back.shape[3]
    qkv, mixed, lse, hidden, one, two, probs = saved

    def block(*shape):
        return pl.BlockSpec((1,) + shape, lambda i: (i,) + (0,) * len(shape))

    return pl.pallas_call(
        functools.partial(tail_kernel, experts),
        grid=(batches,),
        out_shape=(
            jax.ShapeDtypeStruct(x.shape, F32),
            jax.ShapeDtypeStruct(x.shape, F32),
            jax.ShapeDtypeStruct((width, total), BF),
        ),
        in_specs=[
            block(rows, width),
            block(rows, width),
            pl.BlockSpec((width, total), lambda i: (0, 0), pipeline_mode=pl.Buffered(1)),
            block(rows, 4),
            block(rows, 8),
            pl.BlockSpec((experts, 1, 2, cap_pad, width), lambda i: (0, i, 0, 0, 0)),
            block(rows, 3 * width),
            block(rows, width),
            block(rows, 128),
            block(rows, width),
            block(rows, width),
            block(rows, width),
            block(rows, SMALL),
        ],
        out_specs=(
            block(rows, width),
            block(rows, width),
            pl.BlockSpec((width, total), lambda i: (0, 0), pipeline_mode=pl.Buffered(1)),
        ),
        scratch_shapes=[
            pltpu.VMEM((SMALL, width), F32),
            pltpu.VMEM((SMALL, width), F32),
            pltpu.VMEM((batches * rows, 3 * width), BF),
            pltpu.VMEM((batches * rows, width), BF),
            pltpu.VMEM((batches * rows, SMALL), BF),
            pltpu.VMEM((batches * rows, width), BF),
            pltpu.VMEM((batches * rows, width), BF),
            pltpu.VMEM((batches * rows, width), BF),
        ],
        compiler_params=params(),
        cost_estimate=pl.CostEstimate(
            flops=16000000000, bytes_accessed=50000000, transcendentals=2000000
        ),
        name="tail",
    )(x, grad, weight, cols, slot_cols, back, qkv, mixed, lse, hidden, one, two, probs)


def per_device(
    inputs,
    gain_one,
    shift_one,
    qkv_weight,
    proj_weight,
    gain_two,
    shift_two,
    router_weight,
    expert_in,
    expert_bias,
    expert_out,
    out_grad,
    routes,
    priority,
    capacity,
):
    batches = priority.shape[0]
    count = inputs.shape[0] // batches
    width = inputs.shape[1]
    experts = router_weight.shape[1]
    groups = lax.axis_size("expert")
    cap_pad = ceil_to(max(2, (5 * count + 2 * experts - 1) // (2 * experts)), 16)
    depth = qkv_weight.shape[0]
    both = ("dp", "expert")

    vectors = jnp.stack([gain_one, shift_one, gain_two, shift_two], axis=1)
    small = jnp.concatenate([vectors, router_weight], axis=1)
    small = jnp.pad(small, ((0, 0), (0, SMALL - small.shape[1])))
    pack = jnp.concatenate([qkv_weight, proj_weight, small], axis=1)
    slice_rows = depth // groups
    mine = lax.axis_index("expert")
    pack = lax.dynamic_slice_in_dim(pack, mine * slice_rows, slice_rows, axis=0)
    weight = lax.all_gather(pack, both, axis=0, tiled=True)

    hidden_units = expert_out.shape[1]
    cuts = 3
    span = hidden_units // cuts
    bias_rows = jnp.pad(expert_bias, ((0, BIAS_ROWS - 1), (0, 0)))
    tall_in = jnp.concatenate([expert_in[0], bias_rows], axis=0)
    gathered = []
    for cut in range(cuts):
        part_in = lax.all_gather(tall_in[:, cut * span : (cut + 1) * span], "dp", axis=0)
        part_out = lax.all_gather(expert_out[0, cut * span : (cut + 1) * span], "dp", axis=0)
        gathered.append((part_in, part_out))

    extra = SEQ_PAD - SEQ
    x = jnp.pad(inputs.reshape(batches, SEQ, width), ((0, 0), (0, extra), (0, 0)))
    grad = jnp.pad(out_grad.reshape(batches, SEQ, width), ((0, 0), (0, extra), (0, 0)))
    cols = jnp.concatenate(
        [routes.reshape(batches, SEQ, 2), priority.reshape(batches, SEQ, 2)], axis=2
    )
    cols = jnp.pad(cols, ((0, 0), (0, extra), (0, 0)), constant_values=-1)
    rows = jnp.swapaxes(cols, 1, 2)
    slot_rows, slot_cols = run_route(cols, rows, capacity, cap_pad)
    send, *saved = run_front(x, grad, weight, cols, slot_rows, experts, cap_pad)
    received = lax.all_to_all(send, "expert", split_axis=0, concat_axis=0, tiled=True)
    carried = None
    expert_sums = []
    for cut in range(cuts):
        last = cut == cuts - 1
        *carried, sum_in, sum_out = run_expert(received, *gathered[cut], carried, last)
        sum_in = lax.psum_scatter(sum_in, "dp", scatter_dimension=0, tiled=False)
        sum_out = lax.psum_scatter(sum_out, "dp", scatter_dimension=0, tiled=False)
        expert_sums.append((sum_in, sum_out))
    back = lax.all_to_all(carried[0], "expert", split_axis=0, concat_axis=0, tiled=True)
    outputs, inputs_grad, dense = run_tail(
        x, grad, weight, cols, slot_cols, back, saved, experts
    )
    dense = lax.psum_scatter(dense, both, scatter_dimension=0, tiled=True)
    dense = lax.all_gather(dense, "expert", axis=0, tiled=True).astype(F32)
    grad_in = jnp.concatenate([part[0] for part in expert_sums], axis=1).astype(F32)
    grad_out = jnp.concatenate([part[1] for part in expert_sums], axis=0).astype(F32)
    spot = 4 * width
    return (
        outputs[:, :SEQ].reshape(batches * SEQ, width),
        inputs_grad[:, :SEQ].reshape(batches * SEQ, width),
        dense[:, spot],
        dense[:, spot + 1],
        dense[:, : 3 * width],
        dense[:, 3 * width : spot],
        dense[:, spot + 2],
        dense[:, spot + 3],
        dense[:, spot + 4 : spot + 4 + experts],
        grad_in[None, :width],
        grad_in[None, width],
        grad_out[None],
    )


def solution(mesh):
    token = P(("dp", "expert"), None)
    vector = P("dp")
    matrix = P("dp", None)
    return jax.shard_map(
        per_device,
        mesh=mesh,
        in_specs=(
            token,
            vector,
            vector,
            matrix,
            matrix,
            vector,
            vector,
            matrix,
            P("expert", None, "dp"),
            P("expert", "dp"),
            P("expert", "dp", None),
            token,
            token,
            token,
            P(("dp", "expert")),
        ),
        out_specs=(
            token,
            token,
            vector,
            vector,
            matrix,
            matrix,
            vector,
            vector,
            matrix,
            P("expert", None, "dp"),
            P("expert", "dp"),
            P("expert", "dp", None),
        ),
        check_vma=False,
    )
```

time: 1350 us -> 833 us (0.62); the launches traced: 1330 us -> 832 us
  matrix products: 489 us -> 0 us
  Pallas kernels: 0 us -> 195 us
  other arithmetic: 179 us -> 8.89 us
  waiting for transfers between devices: 337 us -> 503 us
  local copies, waits for them, and re-layouts: 179 us -> 28.6 us
  starting transfers between devices: 66.4 us -> 5.55 us
    dot_general x84 -> x0, matrix products: 489 us -> none  [the longest x4 80.9 us: micro_step(): jnp.einsum('nkcd,kfd->nkcf', grad_recv, w_out, preferred_element_type=jnp...]
    pallas_call x0 -> x6, Pallas kernels: none -> 195 us  [the longest x3 127 us: run_expert(): pl.pallas_call(functools.partial(expert_kernel, first, last), grid=(shard...]
    unnamed x13 -> x16, waiting for transfers between devices: 2.72 us -> 103 us
    scatter-add x8 -> x0, other arithmetic: 84 us -> none  [gate_pick(): jnp.take_along_axis(jax.nn.softmax(logits, axis=-1), route_rows, axis=1)]
    all_to_all x0 -> x1, blocking collectives: none -> 76.9 us  [per_device(): lax.all_to_all(carried[0], 'expert', split_axis=0, concat_axis=0, tiled=T...]
    gather x36 -> x0, local copies, waits for them, and re-layouts: 72 us -> none  [the longest x12 21.2 us: gate_pick(): jnp.take_along_axis(jax.nn.softmax(logits, axis=-1), route_rows, axis=1)]
    all_to_all x16 -> x1, starting transfers between devices: 65.8 us -> 4.78 us  [per_device(): lax.all_to_all(send, 'expert', split_axis=0, concat_axis=0, tiled=True)]
    reduce_scatter x4 -> x6, waiting for transfers between devices: 171 us -> 221 us  [the longest x3 111 us: per_device(): sum_out = lax.psum_scatter(sum_out, 'dp', scatter_dimension=0, tiled=False)]
  transfers between devices with their start and end apart: 27 -> 16, of which waited for: 12 -> 14; matrix products, arithmetic and copies ran while one was open for 44% -> 3% of each run, Pallas kernels for 0% -> 13%
where the time goes in v1:
time: 833 us; the launch traced here: 832 us
  waiting for transfers between devices  503 us (60%)
  Pallas kernels  195 us (23%)
  blocking collectives  76.9 us (9%)
  local copies, waits for them, and re-layouts  28.6 us (3%)
  between operations  14.1 us (2%)
  other arithmetic  8.89 us (1%)
    pallas_call x3, Pallas kernels, run_expert(): pl.pallas_call(functools.partial(expert_kernel, first, last), grid=(shard...  127 us
    reduce_scatter x3, waiting for transfers between devices, per_device(): sum_out = lax.psum_scatter(sum_out, 'dp', scatter_dimension=0, tiled=False)  111 us
    reduce_scatter x3, waiting for transfers between devices, per_device(): sum_in = lax.psum_scatter(sum_in, 'dp', scatter_dimension=0, tiled=False)  110 us
    unnamed x16, waiting for transfers between devices  103 us
    all_gather x3, waiting for transfers between devices, per_device(): lax.all_gather(tall_in[:, cut * span:(cut + 1) * span], 'dp', axis=0)  83.8 us
    all_to_all x1, blocking collectives, per_device(): lax.all_to_all(carried[0], 'expert', split_axis=0, concat_axis=0, tiled=T...  76.9 us
    all_gather x1, waiting for transfers between devices, per_device(): weight = lax.all_gather(pack, both, axis=0, tiled=True)  49.1 us
    pallas_call x1, Pallas kernels, run_tail(): pl.pallas_call(functools.partial(tail_kernel, experts), grid=(batches,),...  40.1 us
  transfers between devices with their start and end apart: 16, of which 14 were waited for; matrix products, arithmetic and copies ran while one was open for 3% of the time, Pallas kernels for 13%

profile of v1, /device:TPU:0, one launch (start us, length us, event | category | flops | bytes accessed | tf_op | source)
XLA Modules:
  0.0 832.0 jit_solution(3114766517046496211)
XLA Ops:
  7.3 0.8 stack.12
  8.1 0.7 stack.13
  8.7 0.7 stack.14
  9.4 0.7 stack.15
  10.0 0.8 concatenate.25
  11.0 1.6 fusion.4
  12.7 1.0 fusion.6
  13.9 1.0 fusion.5
  15.0 0.5 all-gather.16.cloned.1.call-update
  15.6 0.2 copy.46
  15.9 0.2 reshape.81
  16.1 0.2 pad_add_fusion
  16.2 0.8 pad_bitcast_fusion
  17.1 0.8 copy.47.rows_ref
  17.8 1.7 reshape.78
  19.5 2.0 reshape.79
  21.5 3.4 pad.19.x_ref
  25.0 1.7 pad.20.grad_ref
  26.6 4.1 route.1
  30.7 49.1 %all-gather.12.cloned.1.call-done.weight_ref = bf16[768,3200]{1,0:T(8,128)(2,1)} async-done(((bf16[24,3200]{1,0:T(8,128)(2,1)}), bf16[768,3200]{1,0:T(8,128)(2,1)}) %all-gather.12.cloned.1.call-update) | async-done | bytes 4915216 | tf_op jit(solution)/shard_map/all_gather | solution.py:598
  79.8 23.9 %front.1 = (bf16[8,4,2,64,768]{4,3,2,1,0:T(8,128)(2,1)}, bf16[4,208,2304]{2,1,0:T(8,128)(2,1)}, bf16[4,208,768]{2,1,0:T(8,128)(2,1)}, f32[4,208,128]{2,1,0:T(8,1...) custom-call(f32[4,208,768]{2,1,0:T(8,128)} %pad.19.x_ref, ...), custom_call_target="tpu_custom_call" | custom-call | flops 8000000000 | bytes 40000000 | tf_op jit(solution)/shard_map/front/pallas_call | solution.py:188
  103.8 4.8 all-to-all-start
  108.6 0.5 all-gather.24.cloned.1.call-update
  109.2 0.5 all-gather.14.cloned.1.call-update
  109.8 0.7 all-gather.22.cloned.1.call-update
  110.5 0.2 reduce-scatter.22.cloned.1.call-start
  110.7 7.2 all-gather.18.cloned.1.call-done.refs_3_
  117.9 38.7 %all-gather.26.cloned.1.call-done = bf16[3136,256]{1,0:T(8,128)(2,1)} async-done(((bf16[784,256]{1,0:T(8,128)(2,1)}), bf16[3136,256]{1,0:T(8,128)(2,1)}) %all-gather.26.cloned.1.call-update) | async-done | bytes 1605648 | tf_op jit(solution)/shard_map/all_gather | solution.py:607
  156.6 23.6 %all-to-all-done.refs_0_.refs_1_ = bf16[8,4,2,64,768]{4,3,2,1,0:T(8,128)(2,1)} async-done(((bf16[8,4,2,64,768]{4,3,2,1,0:T(8,128)(2,1)}), bf16[8,4,2,64,768]{4,3,2,1,0:T(8,128)(2,1)}, u32[]{:S(2)}, u32[]{:S(2)}) %all-to-all-start) | async-done | bytes 6291488 | tf_op jit(solution)/shard_map/all_to_all | solution.py:621
  180.1 39.8 %expert.3 = (f32[2048,768]{1,0:T(8,128)}, f32[2048,768]{1,0:T(8,128)}, bf16[4,784,256]{2,1,0:T(8,128)(2,1)}, bf16[4,256,768]{2,1,0:T(8,128)(2,1)}) custom-call(bf16[8,4,2,64,768]{4,3,2,1,0:T(8,128)(2,1)} %all-to-all-done.refs_0_.refs_1_, bf16[8,4,2,64,768]{4,3,2,1,0:T(8,128)(2,1)} %all-to-all-done.refs_0_.refs_1_, bf16[4,784,256]{2,1,0:T(8,128)(2,1)} %bitcast.20, ...), custom_call_target="tpu_custom_call" | custom-call | flops 19327352832 | bytes 40000000 | tf_op jit(solution)/shard_map/expert/pallas_call | solution.py:350
  219.9 13.2 %all-gather.24.cloned.1.call-done = bf16[3136,256]{1,0:T(8,128)(2,1)} async-done(((bf16[784,256]{1,0:T(8,128)(2,1)}), bf16[3136,256]{1,0:T(8,128)(2,1)}) %all-gather.24.cloned.1.call-update) | async-done | bytes 1605648 | tf_op jit(solution)/shard_map/all_gather | solution.py:607
  233.1 44.1 %expert.4 = (f32[2048,768]{1,0:T(8,128)}, f32[2048,768]{1,0:T(8,128)}, bf16[4,784,256]{2,1,0:T(8,128)(2,1)}, bf16[4,256,768]{2,1,0:T(8,128)(2,1)}) custom-call(bf16[8,4,2,64,768]{4,3,2,1,0:T(8,128)(2,1)} %all-to-all-done.refs_0_.refs_1_, bf16[8,4,2,64,768]{4,3,2,1,0:T(8,128)(2,1)} %all-to-all-done.refs_0_.refs_1_, bf16[4,784,256]{2,1,0:T(8,128)(2,1)} %bitcast.21, ...), custom_call_target="tpu_custom_call" | custom-call | flops 19327352832 | bytes 40000000 | tf_op jit(solution)/shard_map/expert/pallas_call | solution.py:350
  277.2 32.0 %all-gather.22.cloned.1.call-done = bf16[3136,256]{1,0:T(8,128)(2,1)} async-done(((bf16[784,256]{1,0:T(8,128)(2,1)}), bf16[3136,256]{1,0:T(8,128)(2,1)}) %all-gather.22.cloned.1.call-update) | async-done | bytes 1605648 | tf_op jit(solution)/shard_map/all_gather | solution.py:607
  309.2 43.2 %expert.5 = (bf16[8,4,2,64,768]{4,3,2,1,0:T(8,128)(2,1)}, bf16[4,784,256]{2,1,0:T(8,128)(2,1)}, bf16[4,256,768]{2,1,0:T(8,128)(2,1)}) custom-call(bf16[8,4,2,64,768]{4,3,2,1,0:T(8,128)(2,1)} %all-to-all-done.refs_0_.refs_1_, bf16[8,4,2,64,768]{4,3,2,1,0:T(8,128)(2,1)} %all-to-all-done.refs_0_.refs_1_, bf16[4,784,256]{2,1,0:T(8,128)(2,1)} %bitcast.22, ...), custom_call_target="tpu_custom_call" | custom-call | flops 19327352832 | bytes 40000000 | tf_op jit(solution)/shard_map/expert/pallas_call | solution.py:350
  352.4 76.9 %all_to_all.10.back_ref = bf16[8,4,2,64,768]{4,3,2,1,0:T(8,128)(2,1)} all-to-all(bf16[8,4,2,64,768]{4,3,2,1,0:T(8,128)(2,1)} %get-tuple-element.43), channel_id=1, replica_groups=mesh['dp'=4,'expert'=8] {'expert'}, dimensions={0} | all-to-all | bytes 12582912 | tf_op jit(solution)/shard_map/all_to_all | solution.py:630
  429.3 40.1 %tail.1 = (f32[4,208,768]{2,1,0:T(8,128)}, f32[4,208,768]{2,1,0:T(8,128)}, bf16[768,3200]{1,0:T(8,128)(2,1)}) custom-call(f32[4,208,768]{2,1,0:T(8,128)} %pad.19.x_ref, f32[4,208,768]{2,1,0:T(8,128)} %pad.20.grad_ref, bf16[768,3200]{1,0:T(8,128)(2,1)} %all-gather.12.cloned.1.call-done.weight_ref, s32[4,208,4]{2,1,0:T(8,128)} %get-tuple-element.119.cols_ref, ...), custom_call_target="tpu_custom_call" | custom-call | flops 16000000000 | bytes 50000000 | tf_op jit(solution)/shard_map/tail/pallas_call | solution.py:519
  469.5 0.7 reduce-scatter.20.cloned.1.call-update
  470.2 0.5 reduce-scatter.18.cloned.1.call-update
  470.8 0.7 reduce-scatter.16.cloned.1.call-update
  471.5 0.5 reduce-scatter.14.cloned.1.call-update
  472.1 0.7 reduce-scatter.12.cloned.1.call-update
  472.9 0.5 reduce-scatter.10.cloned.1.call-update
  473.4 97.1 %reduce-scatter.22.cloned.1.call-done = bf16[24,3200]{1,0:T(8,128)(2,1)} async-done(((bf16[768,3200]{1,0:T(8,128)(2,1)}), bf16[24,3200]{1,0:T(8,128)(2,1)}) %reduce-scatter.22.cloned.1.call-update) | async-done | bytes 153616
  570.6 36.7 %reduce-scatter.20.cloned.1.call-done = bf16[1,256,768]{2,1,0:T(8,128)(2,1)} async-done(((bf16[4,256,768]{2,1,0:T(8,128)(2,1)}), bf16[1,256,768]{2,1,0:T(8,128)(2,1)}) %reduce-scatter.20.cloned.1.call-update) | async-done | bytes 393232 | tf_op jit(solution)/shard_map/reduce_scatter | solution.py:628
  607.3 37.1 %reduce-scatter.18.cloned.1.call-done = bf16[1,256,768]{2,1,0:T(8,128)(2,1)} async-done(((bf16[4,256,768]{2,1,0:T(8,128)(2,1)}), bf16[1,256,768]{2,1,0:T(8,128)(2,1)}) %reduce-scatter.18.cloned.1.call-update) | async-done | bytes 393232 | tf_op jit(solution)/shard_map/reduce_scatter | solution.py:628
  644.4 37.3 %reduce-scatter.16.cloned.1.call-done = bf16[1,256,768]{2,1,0:T(8,128)(2,1)} async-done(((bf16[4,256,768]{2,1,0:T(8,128)(2,1)}), bf16[1,256,768]{2,1,0:T(8,128)(2,1)}) %reduce-scatter.16.cloned.1.call-update) | async-done | bytes 393232 | tf_op jit(solution)/shard_map/reduce_scatter | solution.py:628
  681.7 2.8 maximum_convert_fusion.1
  684.5 34.9 %reduce-scatter.14.cloned.1.call-done = bf16[1,784,256]{2,1,0:T(8,128)(2,1)} async-done(((bf16[4,784,256]{2,1,0:T(8,128)(2,1)}), bf16[1,784,256]{2,1,0:T(8,128)(2,1)}) %reduce-scatter.14.cloned.1.call-update) | async-done | bytes 401424 | tf_op jit(solution)/shard_map/reduce_scatter | solution.py:627
  719.4 37.8 %reduce-scatter.12.cloned.1.call-done = bf16[1,784,256]{2,1,0:T(8,128)(2,1)} async-done(((bf16[4,784,256]{2,1,0:T(8,128)(2,1)}), bf16[1,784,256]{2,1,0:T(8,128)(2,1)}) %reduce-scatter.12.cloned.1.call-update) | async-done | bytes 401424 | tf_op jit(solution)/shard_map/reduce_scatter | solution.py:627
  757.2 37.7 %reduce-scatter.10.cloned.1.call-done = bf16[1,784,256]{2,1,0:T(8,128)(2,1)} async-done(((bf16[4,784,256]{2,1,0:T(8,128)(2,1)}), bf16[1,784,256]{2,1,0:T(8,128)(2,1)}) %reduce-scatter.10.cloned.1.call-update) | async-done | bytes 401424 | tf_op jit(solution)/shard_map/reduce_scatter | solution.py:627
  794.8 1.3 maximum_convert_fusion.2
  796.1 1.4 maximum_convert_fusion
  797.6 1.6 slice_bitcast_fusion
  799.1 1.0 copy-done.2
  800.1 0.2 slice.57
  800.3 1.7 reshape.82
  802.0 1.9 slice.58
  803.9 1.7 reshape.83
  805.7 14.4 %all-gather.20.cloned.1.call-done = bf16[192,3200]{1,0:T(8,128)(2,1)} async-done(((bf16[24,3200]{1,0:T(8,128)(2,1)}), bf16[192,3200]{1,0:T(8,128)(2,1)}) %all-gather.20.cloned.1.call-update) | async-done | bytes 1228816 | tf_op jit(solution)/shard_map/all_gather | solution.py:635
  820.0 1.5 convert_element_type.23
  821.6 0.9 slice_reduce_fusion
  822.6 0.7 copy.48
  823.2 1.3 slice.73
  824.6 0.9 slice.74
  (40 shorter events, 1.1 us)
Async XLA Ops:
  7.2 5.5 copy-start.4
  7.2 6.6 copy-start.3
  7.2 6.6 copy-start.7
  7.2 72.6 %all-gather.12.cloned.1.call-start = ((), (), s32[]{:S(2)}) async-start(), calls=%async_computation.9 | async-start | bytes 5068800 | tf_op jit(solution)/shard_map/all_gather | solution.py:598
  12.6 105.3 %all-gather.18.cloned.1.call-start = ((), (), s32[]{:S(2)}) async-start(), calls=%async_computation.12 | async-start | bytes 1966080 | tf_op jit(solution)/shard_map/all_gather | solution.py:608
  13.7 142.9 %all-gather.26.cloned.1.call-start = ((), (), s32[]{:S(2)}) async-start(), calls=%async_computation.22 | async-start | bytes 2007040 | tf_op jit(solution)/shard_map/all_gather | solution.py:607
  13.8 1.8 copy-start.6
  13.9 2.0 copy-start.5
  14.9 2.9 copy-start.1
  15.0 204.9 %all-gather.16.cloned.1.call-start = ((), (), s32[]{:S(2)}) async-start(), calls=%async_computation.11 | async-start | bytes 1966080 | tf_op jit(solution)/shard_map/all_gather | solution.py:608
  103.8 76.4 %all-to-all-start = ((bf16[8,4,2,64,768]{4,3,2,1,0:T(8,128)(2,1)}), bf16[8,4,2,64,768]{4,3,2,1,0:T(8,128)(2,1)}, u32[]{:S(2)}, u32[]{:S(2)}) async-start(bf16[8,4,2,64,768]{4,3,2,1,0:T(8,128)(2,1)} %get-tuple-element.38), calls=%async_computation | async-start | bytes 12582912 | tf_op jit(solution)/shard_map/all_to_all | solution.py:621
  108.5 124.5 %all-gather.24.cloned.1.call-start = ((), (), s32[]{:S(2)}) async-start(), calls=%async_computation.21 | async-start | bytes 2007040 | tf_op jit(solution)/shard_map/all_gather | solution.py:607
  109.1 168.0 %all-gather.14.cloned.1.call-start = ((), (), s32[]{:S(2)}) async-start(), calls=%async_computation.10 | async-start | bytes 1966080 | tf_op jit(solution)/shard_map/all_gather | solution.py:608
  109.7 199.5 %all-gather.22.cloned.1.call-start = ((), (), s32[]{:S(2)}) async-start(), calls=%async_computation.20 | async-start | bytes 2007040 | tf_op jit(solution)/shard_map/all_gather | solution.py:607
  110.5 460.1 %reduce-scatter.22.cloned.1.call-start = ((), (), s32[]{:S(2)}) async-start(), calls=%async_computation.23 | async-start | bytes 5068800
  469.4 137.8 %reduce-scatter.20.cloned.1.call-start = ((), (), s32[]{:S(2)}) async-start(), calls=%async_computation.19 | async-start | bytes 1966080 | tf_op jit(solution)/shard_map/reduce_scatter | solution.py:628
  470.2 174.2 %reduce-scatter.18.cloned.1.call-start = ((), (), s32[]{:S(2)}) async-start(), calls=%async_computation.18 | async-start | bytes 1966080 | tf_op jit(solution)/shard_map/reduce_scatter | solution.py:628
  470.8 210.9 %reduce-scatter.16.cloned.1.call-start = ((), (), s32[]{:S(2)}) async-start(), calls=%async_computation.17 | async-start | bytes 1966080 | tf_op jit(solution)/shard_map/reduce_scatter | solution.py:628
  471.5 247.9 %reduce-scatter.14.cloned.1.call-start = ((), (), s32[]{:S(2)}) async-start(), calls=%async_computation.16 | async-start | bytes 2007040 | tf_op jit(solution)/shard_map/reduce_scatter | solution.py:627
  472.1 285.1 %reduce-scatter.12.cloned.1.call-start = ((), (), s32[]{:S(2)}) async-start(), calls=%async_computation.15 | async-start | bytes 2007040 | tf_op jit(solution)/shard_map/reduce_scatter | solution.py:627
  472.8 322.0 %reduce-scatter.10.cloned.1.call-start = ((), (), s32[]{:S(2)}) async-start(), calls=%async_computation.14 | async-start | bytes 2007040 | tf_op jit(solution)/shard_map/reduce_scatter | solution.py:627
  473.4 346.6 %all-gather.20.cloned.1.call-start = ((), (), s32[]{:S(2)}) async-start(), calls=%async_computation.13 | async-start | bytes 1382400 | tf_op jit(solution)/shard_map/all_gather | solution.py:635
  797.5 2.6 copy-start.2
  820.0 2.5 copy-start
Sparse Core Ops, SparseCore 0:
  12.7 67.0 all-gather.11
  82.0 35.8 all-gather.17
  120.1 36.4 all-gather.25
  158.6 35.9 all-gather.15
  196.6 36.4 all-gather.23
  234.5 35.9 all-gather.13
  272.6 36.4 all-gather.21
  469.6 100.9 reduce-scatter.21
  573.0 34.2 reduce-scatter.19
  610.1 34.2 reduce-scatter.17
  647.4 34.2 reduce-scatter.15
  684.5 34.7 reduce-scatter.13
  722.3 34.7 reduce-scatter.11
  760.0 34.7 reduce-scatter.9
  796.7 23.2 all-gather.19

commit v2 on v1

--- a/solution.py
+++ b/solution.py
@@ -15,9 +15,12 @@
 BF = jnp.bfloat16
 F32 = jnp.float32
 SMALL = 128
+MESH = pl.DeviceIdType.MESH
+EARLY = 2
 BIAS_ROWS = 16
 NEG = -1e30
 VMEM_LIMIT = 60 * 1024 * 1024
+VMEM_MAX = 67043328
 
 
 def ceil_to(value, step):
@@ -40,6 +43,89 @@
     return pltpu.CompilerParams(
         dimension_semantics=("arbitrary",) * count, vmem_limit_bytes=VMEM_LIMIT
     )
+
+
+class Line:
+    def __init__(self, shards):
+        self.shards = shards
+        self.me = lax.axis_index("dp")
+        self.has_below = self.me > 0
+        self.has_above = self.me < shards - 1
+
+    def greet(self, me, groups):
+        barrier = pltpu.get_barrier_semaphore()
+        for k in range(1, groups):
+            pl.semaphore_signal(
+                barrier, inc=1, device_id={"expert": lax.rem(me + k, groups)}, device_id_type=MESH
+            )
+
+        @pl.when(self.has_below)
+        def _():
+            pl.semaphore_signal(barrier, inc=1, device_id={"dp": self.me - 1}, device_id_type=MESH)
+
+        @pl.when(self.has_above)
+        def _():
+            pl.semaphore_signal(barrier, inc=1, device_id={"dp": self.me + 1}, device_id_type=MESH)
+
+        ends = self.has_below.astype(jnp.int32) + self.has_above.astype(jnp.int32)
+        pl.semaphore_wait(barrier, groups - 1 + ends)
+
+    def hop(self, way, round_id, source, target, send_sem, arrived):
+        step = 1 - 2 * way
+        slot = self.me - step * round_id
+        copies = []
+        for part in range(2):
+            origin = source[part] if round_id == 0 else source[part].at[slot]
+            copies.append(
+                pltpu.make_async_remote_copy(
+                    src_ref=origin,
+                    dst_ref=target[part].at[slot],
+                    send_sem=send_sem.at[way, round_id, part],
+                    recv_sem=arrived.at[slot, part],
+                    device_id={"dp": self.me + step},
+                    device_id_type=MESH,
+                )
+            )
+        return copies
+
+    def sends(self, way, round_id):
+        if way == 0:
+            return (self.me >= round_id) & self.has_above
+        return (self.me + round_id < self.shards) & self.has_below
+
+    def push(self, round_id, own, spread, send_sem, arrived, source=None):
+        source = own if round_id == 0 else (source or spread)
+        for way in range(2):
+
+            @pl.when(self.sends(way, round_id))
+            def _():
+                for copy in self.hop(way, round_id, source, spread, send_sem, arrived):
+                    copy.start()
+
+    def drain(self, round_id, own, spread, send_sem, arrived, source=None):
+        source = own if round_id == 0 else (source or spread)
+        for way in range(2):
+
+            @pl.when(self.sends(way, round_id))
+            def _():
+                for copy in self.hop(way, round_id, source, spread, send_sem, arrived):
+                    copy.wait_send()
+
+    def receive(self, round_id, spread, arrived):
+        far = round_id + 1
+
+        @pl.when(self.me >= far)
+        def _():
+            self.wait_slot(self.me - far, spread, arrived)
+
+        @pl.when(self.me + far < self.shards)
+        def _():
+            self.wait_slot(self.me + far, spread, arrived)
+
+    def wait_slot(self, slot, spread, arrived):
+        for part in range(2):
+            view = spread[part].at[slot]
+            pltpu.make_async_copy(view, view, arrived.at[slot, part]).wait()
 
 
 def route_kernel(cap_pad, cols_ref, rows_ref, limit_ref, slot_rows_ref, slot_cols_ref):
@@ -96,12 +182,15 @@
 
 def front_kernel(
     experts,
+    shards,
     x_ref,
     grad_ref,
     weight_ref,
     cols_ref,
     slot_rows_ref,
-    send_ref,
+    own_in_ref,
+    own_out_ref,
+    received_ref,
     qkv_ref,
     mixed_ref,
     lse_ref,
@@ -109,14 +198,29 @@
     one_ref,
     two_ref,
     probs_ref,
+    spread_in_ref,
+    spread_out_ref,
     small_ref,
+    send_ref,
+    send_sem,
+    arrived,
+    rows_send,
+    rows_recv,
 ):
+    index = pl.program_id(0)
+    me = lax.axis_index("expert")
+    groups = received_ref.shape[0]
     width = x_ref.shape[-1]
     rows = x_ref.shape[1]
+    line = Line(shards)
+    own = (own_in_ref, own_out_ref)
+    spread = (spread_in_ref, spread_out_ref)
 
     @pl.when(pl.program_id(0) == 0)
     def _():
+        line.greet(me, groups)
         small_ref[...] = weight_ref[:, 4 * width :].astype(F32).T
+        line.push(0, own, spread, send_sem, arrived)
 
     x = x_ref[0]
     hat, _ = norm_stats(x)
@@ -158,8 +262,8 @@
     probs = expo / jnp.sum(expo, axis=-1, keepdims=True)
     probs_ref[0] = probs
     out_grad = grad_ref[0]
-    slots = send_ref.shape[0] * send_ref.shape[3]
-    slot = lax.broadcasted_iota(jnp.int32, (slots, 1), 0)
+    cap_pad = send_ref.shape[3]
+    slot = lax.broadcasted_iota(jnp.int32, (groups * cap_pad, 1), 0)
     both = None
     grads = None
     for j in range(2):
@@ -171,12 +275,50 @@
         part = dot(pick.astype(BF), (gate * out_grad).astype(BF))
         grads = part if grads is None else grads + part
     sent = dot(both.astype(BF), two).astype(BF)
-    send_ref[:, 0, 0] = sent.reshape(send_ref.shape[0], send_ref.shape[3], width)
-    send_ref[:, 0, 1] = grads.astype(BF).reshape(send_ref.shape[0], send_ref.shape[3], width)
-
-
-def run_front(x, grad, weight, cols, slot_rows, experts, cap_pad):
+    send_ref[index, :, 0] = sent.reshape(groups, cap_pad, width)
+    send_ref[index, :, 1] = grads.astype(BF).reshape(groups, cap_pad, width)
+
+    def rows_copy(image, target):
+        return pltpu.make_async_remote_copy(
+            src_ref=send_ref.at[image, target],
+            dst_ref=received_ref.at[me, image],
+            send_sem=rows_send.at[image, target],
+            recv_sem=rows_recv.at[me, image],
+            device_id={"expert": target},
+            device_id_type=MESH,
+        )
+
+    for k in range(1, groups):
+        rows_copy(index, lax.rem(me + k, groups)).start()
+    pltpu.make_async_copy(
+        send_ref.at[index, me], received_ref.at[me, index], rows_recv.at[me, index]
+    ).start()
+
+    @pl.when(index == pl.num_programs(0) - 1)
+    def _():
+        rounds = min(EARLY, shards - 1)
+        for round_id in range(1, rounds):
+            line.receive(round_id - 1, spread, arrived)
+            line.push(round_id, own, spread, send_sem, arrived)
+
+        def finish(image, carry):
+            for k in range(groups):
+                source = lax.rem(me + k, groups)
+                if k:
+                    rows_copy(image, source).wait_send()
+                view = received_ref.at[source, image]
+                pltpu.make_async_copy(view, view, rows_recv.at[source, image]).wait()
+            return carry
+
+        lax.fori_loop(0, send_ref.shape[0], finish, 0)
+        line.receive(rounds - 1, spread, arrived)
+        for round_id in range(rounds):
+            line.drain(round_id, own, spread, send_sem, arrived)
+
+
+def run_front(x, grad, weight, cols, slot_rows, own_in, own_out, experts, cap_pad):
     batches, rows, width = x.shape
+    shards = lax.axis_size("dp")
     total = weight.shape[1]
 
     def block(*shape):
@@ -186,7 +328,7 @@
         return jax.ShapeDtypeStruct((batches,) + shape, dtype)
 
     return pl.pallas_call(
-        functools.partial(front_kernel, experts),
+        functools.partial(front_kernel, experts, shards),
         grid=(batches,),
         out_shape=(
             jax.ShapeDtypeStruct((experts, batches, 2, cap_pad, width), BF),
@@ -197,6 +339,8 @@
             out((rows, width), BF),
             out((rows, width), BF),
             out((rows, SMALL), F32),
+            jax.ShapeDtypeStruct((shards,) + own_in.shape, BF),
+            jax.ShapeDtypeStruct((shards,) + own_out.shape, BF),
         ),
         in_specs=[
             block(rows, width),
@@ -204,9 +348,11 @@
             pl.BlockSpec((width, total), lambda i: (0, 0), pipeline_mode=pl.Buffered(1)),
             block(rows, 4),
             block(8, rows),
+            pl.BlockSpec(memory_space=pl.ANY),
+            pl.BlockSpec(memory_space=pl.ANY),
         ],
         out_specs=(
-            pl.BlockSpec((experts, 1, 2, cap_pad, width), lambda i: (0, i, 0, 0, 0)),
+            pl.BlockSpec(memory_space=pl.ANY),
             block(rows, 3 * width),
             block(rows, width),
             block(rows, 128),
@@ -214,159 +360,379 @@
             block(rows, width),
             block(rows, width),
             block(rows, SMALL),
-        ),
-        scratch_shapes=[pltpu.VMEM((SMALL, width), F32)],
-        compiler_params=params(),
+            pl.BlockSpec(memory_space=pl.ANY),
+            pl.BlockSpec(memory_space=pl.ANY),
+        ),
+        scratch_shapes=[
+            pltpu.VMEM((SMALL, width), F32),
+            pltpu.VMEM((batches, experts, 2, cap_pad, width), BF),
+            pltpu.SemaphoreType.DMA((2, EARLY, 2)),
+            pltpu.SemaphoreType.DMA((shards, 2)),
+            pltpu.SemaphoreType.DMA((batches, experts)),
+            pltpu.SemaphoreType.DMA((experts, batches)),
+        ],
+        compiler_params=pltpu.CompilerParams(
+            dimension_semantics=("arbitrary",),
+            vmem_limit_bytes=VMEM_LIMIT,
+            collective_id=1,
+            has_side_effects=True,
+        ),
         cost_estimate=pl.CostEstimate(
             flops=8000000000, bytes_accessed=40000000, transcendentals=3000000
         ),
         name="front",
-    )(x, grad, weight, cols, slot_rows)
-
-
-def expert_kernel(first, last, *refs):
-    refs = list(refs)
-    x_ref, grad_ref, win_ref, wout_ref = refs[:4]
-    refs = refs[4:]
-    if not first:
-        y_in, dx_in = refs[:2]
-        refs = refs[2:]
-    back_refs = refs[:1] if last else refs[:2]
-    refs = refs[len(back_refs) :]
-    gin_ref, gout_ref, y_acc, dx_acc, gin_acc, gout_acc = refs
-    shard = pl.program_id(0)
-    block = pl.program_id(1)
-    shards = pl.num_programs(0)
-    blocks = pl.num_programs(1)
-    width = x_ref.shape[-1]
-    rows = x_ref.shape[0] * x_ref.shape[1] * x_ref.shape[3]
-    x = x_ref[...].reshape(rows, width)
-    grad = grad_ref[...].reshape(rows, width)
-    win = win_ref[0, :width, :]
-    wout = wout_ref[0]
-    pre = dot(x, win) + win_ref[0, width : width + 1, :].astype(F32)
-    cdf = 0.5 * lax.erf(pre * (0.5**0.5)) + 0.5
-    active = (pre * cdf).astype(BF)
-    slope = cdf + pre * (jnp.exp(-0.5 * pre * pre) * 0.3989422804014327)
-    d_pre = dot_nt(grad, wout) * slope
-    d_pre = d_pre.astype(BF)
-    here = pl.ds(pl.multiple_of(block * rows, rows), rows)
-    y_part = dot(active, wout)
-    dx_part = dot_nt(d_pre, win)
-
-    @pl.when(shard == 0)
-    def _():
-        if first:
-            y_acc[here, :] = y_part
-            dx_acc[here, :] = dx_part
+    )(x, grad, weight, cols, slot_rows, own_in, own_out)
+
+
+def pieces_of(tall, span):
+    half = ceil_to(tall // 2, 16)
+    mid = ceil_to(span // 2, 16)
+    return ((0, 0, half), (0, half, tall - half), (1, 0, mid), (1, mid, span - mid))
+
+
+def moe_kernel(
+    shards,
+    groups,
+    x_hbm,
+    own_in_ref,
+    own_out_ref,
+    spread_in_ref,
+    spread_out_ref,
+    back_ref,
+    sum_in_ref,
+    sum_out_ref,
+    rows_ref,
+    win_ref,
+    wout_ref,
+    y_acc,
+    dx_acc,
+    gin_acc,
+    gout_acc,
+    part_in_ref,
+    part_out_ref,
+    land_in_ref,
+    land_out_ref,
+    rows_sem,
+    weight_send,
+    arrived,
+    sum_send,
+    sum_recv,
+    back_send,
+    back_recv,
+    final_sem,
+):
+    line = Line(shards)
+    z = line.me
+    me = lax.axis_index("expert")
+    _, batches, _, cap_pad, width = rows_ref.shape
+    tall, span = own_in_ref.shape
+    group = max(1, 512 // (batches * cap_pad))
+    while groups % group:
+        group -= 1
+    blocks = groups // group
+    rows = group * batches * cap_pad
+    early = min(EARLY, shards - 1)
+    spread = (win_ref, wout_ref)
+    early_spread = (spread_in_ref, spread_out_ref)
+    own = (own_in_ref, own_out_ref)
+    parts = (part_in_ref, part_out_ref)
+    lands = (land_in_ref, land_out_ref)
+    pieces = pieces_of(tall, span)
+
+    for k in range(groups):
+        source = lax.rem(me + k, groups)
+        pltpu.make_async_copy(x_hbm.at[source], rows_ref.at[source], rows_sem.at[source]).start()
+    for part in range(2):
+        pltpu.make_async_copy(own[part], spread[part].at[z], arrived.at[z, part]).start()
+    for far in range(1, early + 1):
+        for sign in (-1, 1):
+            slot = z + sign * far
+
+            @pl.when((slot >= 0) & (slot < shards))
+            def _():
+                for part in range(2):
+                    pltpu.make_async_copy(
+                        early_spread[part].at[slot], spread[part].at[slot], arrived.at[slot, part]
+                    ).start()
+
+    line.greet(me, groups)
+    if early < shards - 1:
+        line.push(early, own, spread, weight_send, arrived, early_spread)
+
+    table = []
+    for at in range(shards):
+        near = sorted(range(shards), key=lambda q: (abs(q - at), q))
+        table.append(near[1:] + near[:1])
+
+    def quarter(step):
+        total = 0
+        for at in range(shards):
+            for s in range(shards):
+                hit = jnp.where((z == at) & (step == s), table[at][s], 0)
+                total = total + hit
+        return total
+
+    def sum_copy(way, q, piece):
+        kind, low, size = pieces[piece]
+        if way == 0:
+            slot = q
+            peer = z + 1
         else:
-            y_acc[here, :] = y_part + y_in[here, :]
-            dx_acc[here, :] = dx_part + dx_in[here, :]
-
-    @pl.when(shard > 0)
-    def _():
-        y_acc[here, :] += y_part
-        dx_acc[here, :] += dx_part
-
-    gout = dot_tn(active, grad)
-    gin = dot_tn(x, d_pre)
-    gbias = jnp.sum(d_pre.astype(F32), axis=0, keepdims=True)
-
-    @pl.when(block == 0)
-    def _():
-        gout_acc[...] = gout
-        gin_acc[:width, :] = gin
-        gin_acc[width : width + 1, :] = gbias
-
-    @pl.when(block > 0)
-    def _():
-        gout_acc[...] += gout
-        gin_acc[:width, :] += gin
-        gin_acc[width : width + 1, :] += gbias
-
-    @pl.when(block == blocks - 1)
-    def _():
-        gout_ref[0] = gout_acc[...].astype(BF)
-        gin_ref[0, :width, :] = gin_acc[:width, :].astype(BF)
-        gin_ref[0, width:, :] = jnp.broadcast_to(
-            gin_acc[width : width + 1, :].astype(BF), (BIAS_ROWS, gin_acc.shape[1])
+            slot = jnp.where(q == z - 1, shards, q)
+            peer = z - 1
+        cut = pl.ds(low, size)
+        return pltpu.make_async_remote_copy(
+            src_ref=parts[kind].at[q, cut],
+            dst_ref=lands[kind].at[slot, cut],
+            send_sem=sum_send.at[way, q, piece],
+            recv_sem=sum_recv.at[slot, piece],
+            device_id={"dp": peer},
+            device_id_type=MESH,
         )
 
-    @pl.when(shard == shards - 1)
-    def _():
-        if last:
-            shape = (x_ref.shape[0], x_ref.shape[1], x_ref.shape[3], width)
-            back_refs[0][:, :, 0] = y_acc[here, :].astype(BF).reshape(shape)
-            back_refs[0][:, :, 1] = dx_acc[here, :].astype(BF).reshape(shape)
-        else:
-            back_refs[0][...] = y_acc[here, :]
-            back_refs[1][...] = dx_acc[here, :]
-
-
-def run_expert(received, win, wout, carried, last):
-    sources, batches, _, cap_pad, width = received.shape
-    shards, tall, span = win.shape
-    group = max(1, 512 // (batches * cap_pad))
-    while sources % group:
-        group -= 1
-    blocks = sources // group
-    rows = group * batches * cap_pad
-    total = sources * batches * cap_pad
-    first = carried is None
-    final = shards - 1
-
-    def take(kind):
-        return pl.BlockSpec((group, batches, 1, cap_pad, width), lambda s, r: (r, 0, kind, 0, 0))
-
-    in_specs = [
-        take(0),
-        take(1),
-        pl.BlockSpec((1, tall, span), lambda s, r: (s, 0, 0)),
-        pl.BlockSpec((1, span, width), lambda s, r: (s, 0, 0)),
+    def take_sum(slot, q, piece):
+        kind, low, size = pieces[piece]
+        cut = pl.ds(low, size)
+        view = lands[kind].at[slot, cut]
+        pltpu.make_async_copy(view, view, sum_recv.at[slot, piece]).wait()
+        parts[kind][q, cut] = (
+            parts[kind][q, cut].astype(F32) + lands[kind][slot, cut].astype(F32)
+        ).astype(BF)
+
+    def back_copy(source):
+        return pltpu.make_async_remote_copy(
+            src_ref=rows_ref.at[source],
+            dst_ref=back_ref.at[me],
+            send_sem=back_send.at[source],
+            recv_sem=back_recv.at[me],
+            device_id={"expert": source},
+            device_id_type=MESH,
+        )
+
+    def back_start(first):
+        for k in range(group):
+            source = first + k
+
+            @pl.when(source != me)
+            def _():
+                back_copy(source).start()
+
+            @pl.when(source == me)
+            def _():
+                pltpu.make_async_copy(
+                    rows_ref.at[source], back_ref.at[source], back_recv.at[source]
+                ).start()
+
+    def block_first(block):
+        return lax.rem(me // group + 1 + block, blocks) * group
+
+    def do_step(step, carry):
+        q = quarter(step)
+        line.wait_slot(q, spread, arrived)
+        for round_id in range(early, shards - 2):
+            for way in range(2):
+                forward = 1 - 2 * way
+
+                @pl.when((q == z - forward * (round_id + 1)) & line.sends(way, round_id + 1))
+                def _():
+                    for copy in line.hop(way, round_id + 1, spread, spread, weight_send, arrived):
+                        copy.start()
+
+        def do_block(block, inner):
+            lead = block_first(block)
+            low = pl.multiple_of(lead * (batches * cap_pad), rows)
+            here = pl.ds(low, rows)
+            mine = pl.ds(lead, group)
+
+            @pl.when(step == 0)
+            def _():
+                for k in range(group):
+                    view = rows_ref.at[lead + k]
+                    pltpu.make_async_copy(view, view, rows_sem.at[lead + k]).wait()
+
+            x = rows_ref[mine, :, 0].reshape(rows, width)
+            grad = rows_ref[mine, :, 1].reshape(rows, width)
+            win = win_ref[q, :width, :]
+            wout = wout_ref[q]
+            pre = dot(x, win) + win_ref[q, width : width + 1, :].astype(F32)
+            cdf = 0.5 * lax.erf(pre * (0.5**0.5)) + 0.5
+            active = (pre * cdf).astype(BF)
+            slope = cdf + pre * (jnp.exp(-0.5 * pre * pre) * 0.3989422804014327)
+            d_pre = (dot_nt(grad, wout) * slope).astype(BF)
+            y_part = dot(active, wout)
+            dx_part = dot_nt(d_pre, win)
+
+            @pl.when(step == 0)
+            def _():
+                y_acc[here, :] = y_part
+                dx_acc[here, :] = dx_part
+
+            @pl.when(step > 0)
+            def _():
+                y_acc[here, :] += y_part
+                dx_acc[here, :] += dx_part
+
+            gout = dot_tn(active, grad)
+            gin = dot_tn(x, d_pre)
+            gbias = jnp.sum(d_pre.astype(F32), axis=0, keepdims=True)
+
+            @pl.when(block == 0)
+            def _():
+                gout_acc[...] = gout
+                gin_acc[:width, :] = gin
+                gin_acc[width : width + 1, :] = gbias
+
+            @pl.when(block > 0)
+            def _():
+                gout_acc[...] += gout
+                gin_acc[:width, :] += gin
+                gin_acc[width : width + 1, :] += gbias
+
+            @pl.when(step == shards - 1)
+            def _():
+                shape = (group, batches, cap_pad, width)
+                rows_ref[mine, :, 0] = y_acc[here, :].astype(BF).reshape(shape)
+                rows_ref[mine, :, 1] = dx_acc[here, :].astype(BF).reshape(shape)
+
+                @pl.when(block > 0)
+                def _():
+                    back_start(block_first(block - 1))
+
+            return inner
+
+        lax.fori_loop(0, blocks, do_block, 0)
+
+        @pl.when(step == shards - 1)
+        def _():
+            back_start(block_first(blocks - 1))
+
+        part_in_ref[q, :width, :] = gin_acc[:width, :].astype(BF)
+        part_in_ref[q, width:, :] = jnp.broadcast_to(
+            gin_acc[width : width + 1, :].astype(BF), (tall - width, span)
+        )
+        part_out_ref[q] = gout_acc[...].astype(BF)
+
+        @pl.when((z == 0) & (q > z))
+        def _():
+            for piece in range(len(pieces)):
+                sum_copy(0, q, piece).start()
+
+        @pl.when((z == shards - 1) & (q < z))
+        def _():
+            for piece in range(len(pieces)):
+                sum_copy(1, q, piece).start()
+
+        return carry
+
+    lax.fori_loop(0, shards, do_step, 0)
+
+    def do_forward(turn, carry):
+        up = turn
+        down = shards - 1 - turn
+        for piece in range(len(pieces)):
+
+            @pl.when((up > z) & (z > 0))
+            def _():
+                take_sum(up, up, piece)
+                sum_copy(0, up, piece).start()
+
+            @pl.when((down < z) & (z < shards - 1))
+            def _():
+                take_sum(down, down, piece)
+                sum_copy(1, down, piece).start()
+
+        return carry
+
+    lax.fori_loop(1, shards, do_forward, 0)
+    for piece in range(len(pieces)):
+
+        @pl.when(line.has_below)
+        def _():
+            take_sum(z, z, piece)
+
+        @pl.when(line.has_above)
+        def _():
+            take_sum(shards, z, piece)
+
+    finals = [
+        pltpu.make_async_copy(part_in_ref.at[z], sum_in_ref, final_sem.at[0]),
+        pltpu.make_async_copy(part_out_ref.at[z], sum_out_ref, final_sem.at[1]),
     ]
-    operands = [received, received, win, wout]
-    if not first:
-        in_specs += [pl.BlockSpec((total, width), lambda s, r: (0, 0), pipeline_mode=pl.Buffered(1))] * 2
-        operands += list(carried)
-    if last:
-        out_shape = [jax.ShapeDtypeStruct(received.shape, BF)]
-        out_specs = [
-            pl.BlockSpec(
-                (group, batches, 2, cap_pad, width),
-                lambda s, r: (jnp.where(s == final, r, 0), 0, 0, 0, 0),
-            )
-        ]
-    else:
-        out_shape = [jax.ShapeDtypeStruct((total, width), F32)] * 2
-        out_specs = [pl.BlockSpec((rows, width), lambda s, r: (jnp.where(s == final, r, 0), 0))] * 2
-    out_shape += [
-        jax.ShapeDtypeStruct(win.shape, BF),
-        jax.ShapeDtypeStruct(wout.shape, BF),
-    ]
-    out_specs += [
-        pl.BlockSpec((1, tall, span), lambda s, r: (s, 0, 0)),
-        pl.BlockSpec((1, span, width), lambda s, r: (s, 0, 0)),
-    ]
+    for copy in finals:
+        copy.start()
+
+    def finish_sum(q, carry):
+        @pl.when((q > z) & line.has_above)
+        def _():
+            for piece in range(len(pieces)):
+                sum_copy(0, q, piece).wait_send()
+
+        @pl.when((q < z) & line.has_below)
+        def _():
+            for piece in range(len(pieces)):
+                sum_copy(1, q, piece).wait_send()
+
+        return carry
+
+    lax.fori_loop(0, shards, finish_sum, 0)
+    for round_id in range(early, shards - 1):
+        line.drain(round_id, own, spread, weight_send, arrived)
+    for k in range(groups):
+        source = lax.rem(me + k, groups)
+        if k:
+            back_copy(source).wait_send()
+        view = back_ref.at[source]
+        pltpu.make_async_copy(view, view, back_recv.at[source]).wait()
+    for copy in finals:
+        copy.wait()
+
+
+def run_moe(received, own_in, own_out, spread_in, spread_out):
+    groups, batches, _, cap_pad, width = received.shape
+    shards, tall, span = spread_in.shape
+    total = groups * batches * cap_pad
+    count = len(pieces_of(tall, span))
+    anywhere = pl.BlockSpec(memory_space=pl.ANY)
     return pl.pallas_call(
-        functools.partial(expert_kernel, first, last),
-        grid=(shards, blocks),
-        out_shape=tuple(out_shape),
-        in_specs=in_specs,
-        out_specs=tuple(out_specs),
+        functools.partial(moe_kernel, shards, groups),
+        out_shape=(
+            jax.ShapeDtypeStruct(received.shape, BF),
+            jax.ShapeDtypeStruct((tall, span), BF),
+            jax.ShapeDtypeStruct((span, width), BF),
+        ),
+        in_specs=[anywhere] * 5,
+        out_specs=(anywhere,) * 3,
         scratch_shapes=[
+            pltpu.VMEM(received.shape, BF),
+            pltpu.VMEM((shards, tall, span), BF),
+            pltpu.VMEM((shards, span, width), BF),
             pltpu.VMEM((total, width), F32),
             pltpu.VMEM((total, width), F32),
-            pltpu.VMEM((tall, span), F32),
+            pltpu.VMEM((ceil_to(width + 1, 8), span), F32),
             pltpu.VMEM((span, width), F32),
+            pltpu.VMEM((shards, tall, span), BF),
+            pltpu.VMEM((shards, span, width), BF),
+            pltpu.VMEM((shards + 1, tall, span), BF),
+            pltpu.VMEM((shards + 1, span, width), BF),
+            pltpu.SemaphoreType.DMA((groups,)),
+            pltpu.SemaphoreType.DMA((2, shards, 2)),
+            pltpu.SemaphoreType.DMA((shards, 2)),
+            pltpu.SemaphoreType.DMA((2, shards, count)),
+            pltpu.SemaphoreType.DMA((shards + 1, count)),
+            pltpu.SemaphoreType.DMA((groups,)),
+            pltpu.SemaphoreType.DMA((groups,)),
+            pltpu.SemaphoreType.DMA((2,)),
         ],
-        compiler_params=params(2),
+        compiler_params=pltpu.CompilerParams(
+            vmem_limit_bytes=VMEM_MAX, collective_id=2, has_side_effects=True
+        ),
         cost_estimate=pl.CostEstimate(
             flops=12 * total * width * span * shards,
-            bytes_accessed=40000000,
+            bytes_accessed=60000000,
             transcendentals=2 * total * span * shards,
         ),
-        name="expert",
-    )(*operands)
+        name="moe",
+    )(received, own_in, own_out, spread_in, spread_out)
 
 
 def tail_kernel(
@@ -597,16 +963,9 @@
     pack = lax.dynamic_slice_in_dim(pack, mine * slice_rows, slice_rows, axis=0)
     weight = lax.all_gather(pack, both, axis=0, tiled=True)
 
-    hidden_units = expert_out.shape[1]
-    cuts = 3
-    span = hidden_units // cuts
     bias_rows = jnp.pad(expert_bias, ((0, BIAS_ROWS - 1), (0, 0)))
-    tall_in = jnp.concatenate([expert_in[0], bias_rows], axis=0)
-    gathered = []
-    for cut in range(cuts):
-        part_in = lax.all_gather(tall_in[:, cut * span : (cut + 1) * span], "dp", axis=0)
-        part_out = lax.all_gather(expert_out[0, cut * span : (cut + 1) * span], "dp", axis=0)
-        gathered.append((part_in, part_out))
+    own_in = jnp.concatenate([expert_in[0], bias_rows], axis=0)
+    own_out = expert_out[0]
 
     extra = SEQ_PAD - SEQ
     x = jnp.pad(inputs.reshape(batches, SEQ, width), ((0, 0), (0, extra), (0, 0)))
@@ -617,24 +976,17 @@
     cols = jnp.pad(cols, ((0, 0), (0, extra), (0, 0)), constant_values=-1)
     rows = jnp.swapaxes(cols, 1, 2)
     slot_rows, slot_cols = run_route(cols, rows, capacity, cap_pad)
-    send, *saved = run_front(x, grad, weight, cols, slot_rows, experts, cap_pad)
-    received = lax.all_to_all(send, "expert", split_axis=0, concat_axis=0, tiled=True)
-    carried = None
-    expert_sums = []
-    for cut in range(cuts):
-        last = cut == cuts - 1
-        *carried, sum_in, sum_out = run_expert(received, *gathered[cut], carried, last)
-        sum_in = lax.psum_scatter(sum_in, "dp", scatter_dimension=0, tiled=False)
-        sum_out = lax.psum_scatter(sum_out, "dp", scatter_dimension=0, tiled=False)
-        expert_sums.append((sum_in, sum_out))
-    back = lax.all_to_all(carried[0], "expert", split_axis=0, concat_axis=0, tiled=True)
+    received, *saved, spread_in, spread_out = run_front(
+        x, grad, weight, cols, slot_rows, own_in, own_out, experts, cap_pad
+    )
+    back, grad_in, grad_out = run_moe(received, own_in, own_out, spread_in, spread_out)
     outputs, inputs_grad, dense = run_tail(
         x, grad, weight, cols, slot_cols, back, saved, experts
     )
     dense = lax.psum_scatter(dense, both, scatter_dimension=0, tiled=True)
     dense = lax.all_gather(dense, "expert", axis=0, tiled=True).astype(F32)
-    grad_in = jnp.concatenate([part[0] for part in expert_sums], axis=1).astype(F32)
-    grad_out = jnp.concatenate([part[1] for part in expert_sums], axis=0).astype(F32)
+    grad_in = grad_in.astype(F32)
+    grad_out = grad_out.astype(F32)
     spot = 4 * width
     return (
         outputs[:, :SEQ].reshape(batches * SEQ, width),

time: 833 us -> 606 us (0.73)
  waiting for transfers between devices: 503 us -> 161 us
  Pallas kernels: 195 us -> 390 us
  blocking collectives: 76.9 us -> 0 us
    reduce_scatter x6 -> x0, waiting for transfers between devices: 221 us -> none  [the longest x3 111 us: per_device(): sum_out = lax.psum_scatter(sum_out, 'dp', scatter_dimension=0, tiled=False)]
    pallas_call x4 -> x2, Pallas kernels: 151 us -> 346 us  [the longest x1 232 us: run_moe(): pl.pallas_call(functools.partial(moe_kernel, shards, groups), out_shape=(...]
    all_gather x6 -> x0, waiting for transfers between devices: 91.1 us -> none  [the longest x3 83.8 us: per_device(): lax.all_gather(tall_in[:, cut * span:(cut + 1) * span], 'dp', axis=0)]
    all_to_all x1 -> x0, blocking collectives: 76.9 us -> none  [per_device(): lax.all_to_all(carried[0], 'expert', split_axis=0, concat_axis=0, tiled=T...]
    all_to_all x1 -> x0, waiting for transfers between devices: 23.6 us -> none  [per_device(): lax.all_to_all(send, 'expert', split_axis=0, concat_axis=0, tiled=True)]
    unnamed x16 -> x4, waiting for transfers between devices: 103 us -> 101 us
  transfers between devices with their start and end apart: 16 -> 3, of which waited for: 14 -> 3; matrix products, arithmetic and copies ran while one was open for 3% -> 5% of each run, Pallas kernels for 13% -> 1%
where the time goes in v2:
time: 606 us
  Pallas kernels  390 us (64%)
  waiting for transfers between devices  161 us (27%)
  local copies, waits for them, and re-layouts  29.8 us (5%)
  between operations  13.9 us (2%)
  other arithmetic  10.3 us (2%)
    pallas_call x1, Pallas kernels, run_moe(): pl.pallas_call(functools.partial(moe_kernel, shards, groups), out_shape=(...  232 us
    pallas_call x1, Pallas kernels, run_front(): pl.pallas_call(functools.partial(front_kernel, experts, shards), grid=(ba...  114 us
    unnamed x4, waiting for transfers between devices  101 us
    all_gather x1, waiting for transfers between devices, per_device(): weight = lax.all_gather(pack, both, axis=0, tiled=True)  48.3 us
    pallas_call x1, Pallas kernels, run_tail(): pl.pallas_call(functools.partial(tail_kernel, experts), grid=(batches,),...  40.2 us
  transfers between devices with their start and end apart: 3, of which 3 were waited for; matrix products, arithmetic and copies ran while one was open for 5% of the time, Pallas kernels for 1%

profile of v2, /device:TPU:0, one launch (start us, length us, event | category | flops | bytes accessed | tf_op | source)
XLA Modules:
  0.0 605.6 jit_solution(12609984385475809978)
XLA Ops:
  7.2 0.0 all-gather.3.cloned.1.call-start
  7.2 0.7 stack.12
  7.9 0.7 stack.13
  8.5 0.7 stack.14
  9.2 0.7 stack.15
  9.9 0.8 concatenate.12
  10.7 0.1 copy.45
  10.8 0.0 copy-start.2
  10.8 1.7 fusion.4
  12.6 0.0 all-gather.3.cloned.1.call-update
  12.6 0.0 reduce-scatter.4.cloned.1.call-start
  12.6 0.8 reshape.44
  13.4 0.2 copy.46
  13.6 0.9 reshape.45
  14.5 0.2 pad_add_fusion
  14.7 0.8 pad_bitcast_fusion
  15.5 0.8 copy.47.rows_ref
  16.3 0.0 copy-done.2
  16.3 1.7 reshape.42
  18.0 2.0 reshape.43
  20.0 3.4 pad.19.x_ref
  23.4 0.0 copy-start.4
  23.4 1.7 pad.20.grad_ref
  25.1 4.1 route.1
  29.1 0.0 copy-done.4
  29.1 2.4 fusion.1.own_in_ref
  31.5 48.3 %all-gather.3.cloned.1.call-done.weight_ref = bf16[768,3200]{1,0:T(8,128)(2,1)} async-done(((bf16[24,3200]{1,0:T(8,128)(2,1)}), bf16[768,3200]{1,0:T(8,128)(2,1)}) %all-gather.3.cloned.1.call-update) | async-done | bytes 4915216 | tf_op jit(solution)/shard_map/all_gather | solution.py:964
  79.8 114.1 %front.1 = (bf16[8,4,2,64,768]{4,3,2,1,0:T(8,128)(2,1)}, bf16[4,208,2304]{2,1,0:T(8,128)(2,1)}, bf16[4,208,768]{2,1,0:T(8,128)(2,1)}, f32[4,208,128]{2,1,0:T(8,1...) custom-call(f32[4,208,768]{2,1,0:T(8,128)} %pad.19.x_ref, ...), custom_call_target="tpu_custom_call" | custom-call | flops 8000000000 | bytes 40000000 | tf_op jit(solution)/shard_map/front/pallas_call | solution.py:330
  194.0 232.0 %moe.1 = (bf16[8,4,2,64,768]{4,3,2,1,0:T(8,128)(2,1)}, bf16[784,768]{1,0:T(8,128)(2,1)}, bf16[768,768]{1,0:T(8,128)(2,1)}) custom-call(bf16[8,4,2,64,768]{4,3,2,1,0:T(8,128)(2,1)} %get-tuple-element.32.x_hbm, bf16[784,768]{1,0:T(8,128)(2,1)} %fusion.1.own_in_ref, bf16[768,768]{1,0:T(8,128)(2,1)} %bitcast.13, ...), custom_call_target="tpu_custom_call" | custom-call | flops 57982058496 | bytes 60000000 | tf_op jit(solution)/shard_map/moe/pallas_call | solution.py:696
  426.0 40.2 %tail.1 = (f32[4,208,768]{2,1,0:T(8,128)}, f32[4,208,768]{2,1,0:T(8,128)}, bf16[768,3200]{1,0:T(8,128)(2,1)}) custom-call(f32[4,208,768]{2,1,0:T(8,128)} %pad.19.x_ref, f32[4,208,768]{2,1,0:T(8,128)} %pad.20.grad_ref, bf16[768,3200]{1,0:T(8,128)(2,1)} %all-gather.3.cloned.1.call-done.weight_ref, s32[4,208,4]{2,1,0:T(8,128)} %get-tuple-element.101.cols_ref, ...), custom_call_target="tpu_custom_call" | custom-call | flops 16000000000 | bytes 50000000 | tf_op jit(solution)/shard_map/tail/pallas_call | solution.py:885
  466.2 0.0 copy-start.3
  466.2 0.0 reduce-scatter.4.cloned.1.call-update
  466.2 0.0 all-gather.5.cloned.1.call-start
  466.2 101.3 %reduce-scatter.4.cloned.1.call-done = bf16[24,3200]{1,0:T(8,128)(2,1)} async-done(((bf16[768,3200]{1,0:T(8,128)(2,1)}), bf16[24,3200]{1,0:T(8,128)(2,1)}) %reduce-scatter.4.cloned.1.call-update) | async-done | bytes 153616
  567.5 0.0 all-gather.5.cloned.1.call-update
  567.5 0.0 copy-done.3
  567.5 0.6 slice.52
  568.1 1.6 convert_element_type.15
  569.7 1.9 slice.33
  571.6 1.7 reshape.46
  573.3 1.9 slice.34
  575.2 1.7 reshape.47
  576.9 0.0 copy-start.1
  576.9 3.0 bitcast_convert_fusion
  579.9 0.0 copy-done.1
  579.9 1.6 slice_bitcast_fusion
  581.4 11.4 %all-gather.5.cloned.1.call-done = bf16[192,3200]{1,0:T(8,128)(2,1)} async-done(((bf16[24,3200]{1,0:T(8,128)(2,1)}), bf16[192,3200]{1,0:T(8,128)(2,1)}) %all-gather.5.cloned.1.call-update) | async-done | bytes 1228816 | tf_op jit(solution)/shard_map/all_gather | solution.py:987
  592.9 0.0 copy-start
  592.9 1.0 slice.50
  593.8 0.7 copy.48
  594.5 1.4 convert_element_type.14
  596.0 0.9 slice_reduce_fusion
  596.9 0.0 copy-done
  596.9 0.9 slice.47
  597.7 1.3 slice.46
Async XLA Ops:
  7.2 72.6 %all-gather.3.cloned.1.call-start = ((), (), s32[]{:S(2)}) async-start(), calls=%async_computation.1 | async-start | bytes 5068800 | tf_op jit(solution)/shard_map/all_gather | solution.py:964
  10.8 5.5 copy-start.2
  12.6 554.9 %reduce-scatter.4.cloned.1.call-start = ((), (), s32[]{:S(2)}) async-start(), calls=%async_computation.3 | async-start | bytes 5068800
  23.4 5.7 copy-start.4
  466.2 101.4 %copy-start.3 = (bf16[784,768]{1,0:T(8,128)(2,1)S(1)}, bf16[784,768]{1,0:T(8,128)(2,1)}, u32[]{:S(2)}) copy-start(bf16[784,768]{1,0:T(8,128)(2,1)} %get-tuple-element.46) | copy-start | bytes 3612676
  466.2 126.7 %all-gather.5.cloned.1.call-start = ((), (), s32[]{:S(2)}) async-start(), calls=%async_computation.2 | async-start | bytes 1382400 | tf_op jit(solution)/shard_map/all_gather | solution.py:987
  576.9 3.0 copy-start.1
  592.9 4.0 copy-start
Sparse Core Ops, SparseCore 0:
  12.7 67.0 all-gather.2
  466.3 101.1 reduce-scatter.3
  569.6 23.2 all-gather.4

commit v3 on v2

--- a/solution.py
+++ b/solution.py
@@ -928,6 +928,506 @@
     )(x, grad, weight, cols, slot_cols, back, qkv, mixed, lse, hidden, one, two, probs)
 
 
+TILE = 128
+PLANE = 8
+
+
+def reduce_kernel(
+    experts,
+    shards,
+    cols_ref,
+    slot_cols_ref,
+    lse_ref,
+    probs_ref,
+    x_hbm,
+    grad_hbm,
+    weight_hbm,
+    back_hbm,
+    qkv_hbm,
+    mixed_hbm,
+    hidden_hbm,
+    one_hbm,
+    two_hbm,
+    out_hbm,
+    dx_hbm,
+    qkv_grad_ref,
+    proj_grad_ref,
+    small_grad_ref,
+    x_ref,
+    grad_ref,
+    weight_ref,
+    back_ref,
+    qkv_ref,
+    mixed_ref,
+    hidden_ref,
+    one_ref,
+    two_ref,
+    small_ref,
+    sums_ref,
+    one_flip,
+    d_qkv_ref,
+    d_branch_ref,
+    d_mixed_ref,
+    d_logits_ref,
+    tiles_ref,
+    near_ref,
+    plane_land,
+    plane_ref,
+    line_land,
+    final_ref,
+    small_land,
+    small_far,
+    load_sem,
+    store_sem,
+    near_send,
+    near_recv,
+    plane_send,
+    plane_recv,
+    line_send,
+    line_recv,
+    final_send,
+    final_recv,
+    small_send,
+    small_recv,
+):
+    batches, rows, width = x_ref.shape
+    z = lax.axis_index("dp")
+    me = lax.axis_index("expert")
+    core = lax.rem(me, 2)
+    sibling = me + 1 - 2 * core
+    chip = me // 2
+    chips = PLANE // 2
+    pairs = HEADS // 2
+    depth = width // shards
+    head_tiles = width // TILE
+    own_tiles = (4 * width // TILE) // PLANE
+
+    def loads(kind, image):
+        pair = {
+            0: (back_hbm.at[:, image], back_ref.at[:, image]),
+            1: (hidden_hbm.at[image], hidden_ref.at[image]),
+            2: (grad_hbm.at[image], grad_ref.at[image]),
+            3: (mixed_hbm.at[image], mixed_ref.at[pl.ds(image * rows, rows)]),
+            4: (two_hbm.at[image], two_ref.at[pl.ds(image * rows, rows)]),
+            5: (one_hbm.at[image], one_ref.at[pl.ds(image * rows, rows)]),
+            6: (qkv_hbm.at[image], qkv_ref.at[image]),
+            7: (x_hbm.at[image], x_ref.at[image]),
+        }[kind]
+        return pltpu.make_async_copy(pair[0], pair[1], load_sem.at[kind, image])
+
+    weight_load = pltpu.make_async_copy(weight_hbm, weight_ref, load_sem.at[8, 0])
+    for kind in range(3):
+        loads(kind, 0).start()
+    weight_load.start()
+    for image in range(1, batches):
+        for kind in range(3):
+            loads(kind, image).start()
+    for kind in range(3, 8):
+        for image in range(batches):
+            loads(kind, image).start()
+
+    barrier = pltpu.get_barrier_semaphore()
+    for k in range(1, PLANE):
+        pl.semaphore_signal(
+            barrier, inc=1, device_id={"expert": lax.rem(me + k, PLANE)}, device_id_type=MESH
+        )
+    for k in range(1, shards):
+        pl.semaphore_signal(
+            barrier, inc=1, device_id={"dp": lax.rem(z + k, shards)}, device_id_type=MESH
+        )
+    pl.semaphore_wait(barrier, PLANE - 1 + shards - 1)
+
+    def remote(source, target, send_sem, recv_sem, peer):
+        return pltpu.make_async_remote_copy(
+            src_ref=source,
+            dst_ref=target,
+            send_sem=send_sem,
+            recv_sem=recv_sem,
+            device_id=peer,
+            device_id_type=MESH,
+        )
+
+    def landed(view, sem):
+        pltpu.make_async_copy(view, view, sem).wait()
+
+    def near_copy(tile):
+        return remote(
+            tiles_ref.at[tile],
+            near_ref.at[tile],
+            near_send.at[tile],
+            near_recv.at[tile],
+            {"expert": sibling},
+        )
+
+    def plane_copy(tile):
+        return remote(
+            tiles_ref.at[tile],
+            plane_land.at[tile // PLANE, chip],
+            plane_send.at[tile],
+            plane_recv.at[tile // PLANE, chip],
+            {"expert": lax.rem(tile, PLANE)},
+        )
+
+    def line_copy(k, far):
+        return remote(
+            plane_ref.at[k, pl.ds(pl.multiple_of(far * depth, depth), depth)],
+            line_land.at[k, z],
+            line_send.at[k, far],
+            line_recv.at[k, z],
+            {"dp": far},
+        )
+
+    def final_copy(k, peer):
+        tile = me + PLANE * k
+        return remote(
+            final_ref.at[tile],
+            final_ref.at[tile],
+            final_send.at[k, peer],
+            final_recv.at[tile],
+            {"expert": peer},
+        )
+
+    def leave(tile):
+        @pl.when(lax.rem(tile, 2) != core)
+        def _():
+            near_copy(tile).start()
+
+    def combine(tile):
+        @pl.when(lax.rem(tile, 2) == core)
+        def _():
+            landed(near_ref.at[tile], near_recv.at[tile])
+            tiles_ref[tile] = (
+                tiles_ref[tile].astype(F32) + near_ref[tile].astype(F32)
+            ).astype(BF)
+
+            @pl.when(lax.rem(tile, PLANE) != me)
+            def _():
+                plane_copy(tile).start()
+
+    def plane_sum(k):
+        total = tiles_ref[me + PLANE * k].astype(F32)
+        for j in range(1, chips):
+            far = lax.rem(chip + j, chips)
+            landed(plane_land.at[k, far], plane_recv.at[k, far])
+            total = total + plane_land[k, far].astype(F32)
+        plane_ref[k] = total.astype(BF)
+        for j in range(1, shards):
+            line_copy(k, lax.rem(z + j, shards)).start()
+
+    def line_sum(k):
+        mine = pl.ds(pl.multiple_of(z * depth, depth), depth)
+        total = plane_ref[k, mine].astype(F32)
+        for j in range(1, shards):
+            far = lax.rem(z + j, shards)
+            landed(line_land.at[k, far], line_recv.at[k, far])
+            total = total + line_land[k, far].astype(F32)
+        final_ref[me + PLANE * k] = total.astype(BF)
+        for j in range(1, PLANE):
+            final_copy(k, lax.rem(me + j, PLANE)).start()
+
+    lane = lax.broadcasted_iota(jnp.int32, (1, 128), 1)
+    groups, _, _, cap_pad, _ = back_ref.shape
+    slots = groups * cap_pad
+    slot = lax.broadcasted_iota(jnp.int32, (1, slots), 1)
+    sums_ref[...] = jnp.zeros_like(sums_ref)
+
+    def phase_one(image, carry):
+        here = pl.ds(pl.multiple_of(image * rows, rows), rows)
+        for kind in range(3):
+            view = (back_ref.at[:, image], hidden_ref.at[image], grad_ref.at[image])[kind]
+            landed(view, load_sem.at[kind, image])
+
+        @pl.when(image == 0)
+        def _():
+            weight_load.wait()
+            small_ref[...] = weight_ref[:, 4 * width :].astype(F32).T
+
+        out_grad = grad_ref[image]
+        hidden = hidden_ref[image]
+        probs = probs_ref[image]
+        answers = back_ref[:, image, 0].reshape(slots, width)
+        answer_grads = back_ref[:, image, 1].reshape(slots, width)
+        result = hidden
+        d_probs = jnp.zeros_like(probs)
+        both = None
+        for j in range(2):
+            pick = (slot == slot_cols_ref[image, :, j : j + 1]).astype(F32)
+            both = pick if both is None else both + pick
+            chosen = lane - 4 == cols_ref[image, :, j : j + 1]
+            gate = jnp.sum(jnp.where(chosen, probs, 0.0), axis=-1, keepdims=True)
+            picked = dot(pick.astype(BF), answers)
+            result = result + gate * picked
+            d_gate = jnp.sum(picked * out_grad, axis=-1, keepdims=True)
+            d_probs = jnp.where(chosen, d_gate, d_probs)
+        d_logits = probs * (d_probs - jnp.sum(d_probs * probs, axis=-1, keepdims=True))
+        d_logits = d_logits.astype(BF)
+        d_logits_ref[here, :] = d_logits
+        d_two = dot(both.astype(BF), answer_grads) + dot_nt(d_logits, weight_ref[:, 4 * width :])
+        hat, inverse = norm_stats(hidden)
+        sums_ref[2:3, :] += jnp.sum(d_two * hat, axis=0, keepdims=True)
+        sums_ref[3:4, :] += jnp.sum(d_two, axis=0, keepdims=True)
+        d_hat = d_two * small_ref[2:3, :]
+        d_hidden = out_grad + inverse * (
+            d_hat
+            - jnp.mean(d_hat, axis=-1, keepdims=True)
+            - hat * jnp.mean(d_hat * hat, axis=-1, keepdims=True)
+        )
+        d_branch = d_hidden.astype(BF)
+        d_branch_ref[here, :] = d_branch
+        d_mixed_ref[here, :] = dot_nt(d_branch, weight_ref[:, 3 * width : 4 * width]).astype(BF)
+        grad_ref[image] = d_hidden
+        hidden_ref[image] = result
+        pltpu.make_async_copy(hidden_ref.at[image], out_hbm.at[image], store_sem.at[0, image]).start()
+        return carry
+
+    lax.fori_loop(0, batches, phase_one, 0)
+    for kind, view in ((3, mixed_ref), (4, two_ref), (5, one_ref)):
+        for image in range(batches):
+            landed(view.at[pl.ds(image * rows, rows)], load_sem.at[kind, image])
+    proj = dot_tn(mixed_ref[...], d_branch_ref[...]).astype(BF)
+    for tile in range(head_tiles):
+        tiles_ref[tile] = proj[:, tile * TILE : (tile + 1) * TILE]
+    for tile in range(head_tiles):
+        leave(tile)
+    one_flip[...] = one_ref[...].T
+    flipped = dot_tn(d_logits_ref[...], two_ref[...])
+    for image in range(batches):
+        landed(qkv_ref.at[image], load_sem.at[6, image])
+
+    key_ok = lax.broadcasted_iota(jnp.int32, (1, rows), 1) < SEQ
+    scale = HEAD ** (-0.5)
+
+    def phase_two(pair, carry):
+        low = pl.multiple_of(pair * TILE, TILE)
+        spots = [pl.ds(pl.multiple_of(part * width + low, TILE), TILE) for part in range(3)]
+        for image in range(batches):
+            here = pl.ds(image * rows, rows)
+            query, keys, values = (qkv_ref[image, :, spot] for spot in spots)
+            d_mixed = d_mixed_ref[here, pl.ds(low, TILE)]
+            total = [None, None, None]
+            for side in range(2):
+                mine = (lane // HEAD) == side
+
+                def own(array):
+                    return jnp.where(mine, array, jnp.zeros_like(array))
+
+                my_query = own(query)
+                my_d_mixed = own(d_mixed)
+                scores = dot_nt(my_query, keys) * scale
+                scores = jnp.where(key_ok, scores, NEG)
+                log_total = jnp.sum(
+                    jnp.where(lane == 2 * pair + side, lse_ref[image], 0.0), axis=-1, keepdims=True
+                )
+                probs_h = jnp.exp(scores - log_total)
+                d_weights = dot_nt(my_d_mixed, values)
+                row_terms = jnp.sum(d_weights * probs_h, axis=-1, keepdims=True)
+                d_scores = (probs_h * (d_weights - row_terms) * scale).astype(BF)
+                fresh = (
+                    dot(d_scores, own(keys)),
+                    dot_tn(d_scores, my_query),
+                    dot_tn(probs_h.astype(BF), my_d_mixed),
+                )
+                total = [new if old is None else old + new for old, new in zip(total, fresh)]
+            for part in range(3):
+                d_qkv_ref[here, spots[part]] = total[part].astype(BF)
+        first = head_tiles + 3 * pair
+        for part in range(3):
+            tiles_ref[first + part] = dot(one_flip[...], d_qkv_ref[:, spots[part]]).astype(BF)
+        for part in range(3):
+            leave(first + part)
+
+        @pl.when(pair == 0)
+        def _():
+            for tile in range(head_tiles):
+                combine(tile)
+
+        @pl.when(pair > 0)
+        def _():
+            for part in range(3):
+                combine(first - 3 + part)
+
+        @pl.when(pair == pairs - 3)
+        def _():
+            plane_sum(0)
+
+        @pl.when(pair == pairs - 1)
+        def _():
+            line_sum(0)
+            plane_sum(1)
+
+        return carry
+
+    lax.fori_loop(0, pairs, phase_two, 0)
+    for part in range(3):
+        combine(head_tiles + 3 * (pairs - 1) + part)
+
+    for image in range(batches):
+        landed(x_ref.at[image], load_sem.at[7, image])
+
+    def phase_three(image, carry):
+        here = pl.ds(pl.multiple_of(image * rows, rows), rows)
+        d_one = dot_nt(d_qkv_ref[here, :], weight_ref[:, : 3 * width])
+        hat, inverse = norm_stats(x_ref[image])
+        sums_ref[0:1, :] += jnp.sum(d_one * hat, axis=0, keepdims=True)
+        sums_ref[1:2, :] += jnp.sum(d_one, axis=0, keepdims=True)
+        d_hat = d_one * small_ref[0:1, :]
+        x_ref[image] = grad_ref[image] + inverse * (
+            d_hat
+            - jnp.mean(d_hat, axis=-1, keepdims=True)
+            - hat * jnp.mean(d_hat * hat, axis=-1, keepdims=True)
+        )
+        pltpu.make_async_copy(x_ref.at[image], dx_hbm.at[image], store_sem.at[1, image]).start()
+
+        @pl.when(image == batches // 2 - 1)
+        def _():
+            line_sum(1)
+            plane_sum(2)
+
+        return carry
+
+    lax.fori_loop(0, batches, phase_three, 0)
+
+    def small_copy(k):
+        peer = lax.rem(me + k, PLANE)
+        return remote(
+            sums_ref, small_land.at[me], small_send.at[peer], small_recv.at[me], {"expert": peer}
+        )
+
+    def small_far_copy(k):
+        peer = lax.rem(z + k, shards)
+        return remote(
+            small_land.at[me],
+            small_far.at[z],
+            small_send.at[PLANE + peer],
+            small_recv.at[PLANE + z],
+            {"dp": peer},
+        )
+
+    sums_ref[...] += flipped[: sums_ref.shape[0]]
+    for k in range(1, PLANE):
+        small_copy(k).start()
+    line_sum(2)
+    total = sums_ref[...]
+    for k in range(1, PLANE):
+        peer = lax.rem(me + k, PLANE)
+        landed(small_land.at[peer], small_recv.at[peer])
+        total = total + small_land[peer]
+    small_land[me] = total
+    for k in range(1, shards):
+        small_far_copy(k).start()
+    for k in range(1, shards):
+        peer = lax.rem(z + k, shards)
+        landed(small_far.at[peer], small_recv.at[PLANE + peer])
+        total = total + small_far[peer]
+    small_grad_ref[...] = total
+
+    def finish(tile, carry):
+        @pl.when(lax.rem(tile, PLANE) != me)
+        def _():
+            landed(final_ref.at[tile], final_recv.at[tile])
+
+        @pl.when(lax.rem(tile, 2) != core)
+        def _():
+            near_copy(tile).wait_send()
+
+        @pl.when((lax.rem(tile, 2) == core) & (lax.rem(tile, PLANE) != me))
+        def _():
+            plane_copy(tile).wait_send()
+
+        return carry
+
+    lax.fori_loop(0, 4 * head_tiles, finish, 0)
+    for tile in range(head_tiles):
+        proj_grad_ref[:, tile * TILE : (tile + 1) * TILE] = final_ref[tile].astype(F32)
+    for pair in range(pairs):
+        for part in range(3):
+            low = part * width + pair * TILE
+            qkv_grad_ref[:, low : low + TILE] = final_ref[head_tiles + 3 * pair + part].astype(F32)
+    for k in range(own_tiles):
+        for j in range(1, shards):
+            line_copy(k, lax.rem(z + j, shards)).wait_send()
+        for j in range(1, PLANE):
+            final_copy(k, lax.rem(me + j, PLANE)).wait_send()
+    for k in range(1, PLANE):
+        small_copy(k).wait_send()
+    for k in range(1, shards):
+        small_far_copy(k).wait_send()
+    for image in range(batches):
+        pltpu.make_async_copy(hidden_ref.at[image], out_hbm.at[image], store_sem.at[0, image]).wait()
+        pltpu.make_async_copy(x_ref.at[image], dx_hbm.at[image], store_sem.at[1, image]).wait()
+
+
+def run_reduce(x, grad, weight, cols, slot_cols, back, saved, experts):
+    batches, rows, width = x.shape
+    total = weight.shape[1]
+    shards = lax.axis_size("dp")
+    qkv, mixed, lse, hidden, one, two, probs = saved
+    depth = width // shards
+    tiles = 4 * width // TILE
+    own_tiles = tiles // PLANE
+    small_rows = ceil_to(4 + experts, 8)
+    anywhere = pl.BlockSpec(memory_space=pl.ANY)
+    inside = pl.BlockSpec(memory_space=pltpu.VMEM)
+    dma = pltpu.SemaphoreType.DMA
+    return pl.pallas_call(
+        functools.partial(reduce_kernel, experts, shards),
+        out_shape=(
+            jax.ShapeDtypeStruct(x.shape, F32),
+            jax.ShapeDtypeStruct(x.shape, F32),
+            jax.ShapeDtypeStruct((depth, 3 * width), F32),
+            jax.ShapeDtypeStruct((depth, width), F32),
+            jax.ShapeDtypeStruct((small_rows, width), F32),
+        ),
+        in_specs=[inside] * 4 + [anywhere] * 9,
+        out_specs=(anywhere, anywhere, inside, inside, inside),
+        scratch_shapes=[
+            pltpu.VMEM(x.shape, F32),
+            pltpu.VMEM(x.shape, F32),
+            pltpu.VMEM(weight.shape, BF),
+            pltpu.VMEM(back.shape, BF),
+            pltpu.VMEM(qkv.shape, BF),
+            pltpu.VMEM((batches * rows, width), BF),
+            pltpu.VMEM(x.shape, F32),
+            pltpu.VMEM((batches * rows, width), BF),
+            pltpu.VMEM((batches * rows, width), BF),
+            pltpu.VMEM((SMALL, width), F32),
+            pltpu.VMEM((small_rows, width), F32),
+            pltpu.VMEM((width, batches * rows), BF),
+            pltpu.VMEM((batches * rows, 3 * width), BF),
+            pltpu.VMEM((batches * rows, width), BF),
+            pltpu.VMEM((batches * rows, width), BF),
+            pltpu.VMEM((batches * rows, SMALL), BF),
+            pltpu.VMEM((tiles, width, TILE), BF),
+            pltpu.VMEM((tiles, width, TILE), BF),
+            pltpu.VMEM((own_tiles, PLANE // 2, width, TILE), BF),
+            pltpu.VMEM((own_tiles, width, TILE), BF),
+            pltpu.VMEM((own_tiles, shards, depth, TILE), BF),
+            pltpu.VMEM((tiles, depth, TILE), BF),
+            pltpu.VMEM((PLANE, small_rows, width), F32),
+            pltpu.VMEM((shards, small_rows, width), F32),
+            dma((9, batches)),
+            dma((2, batches)),
+            dma((tiles,)),
+            dma((tiles,)),
+            dma((tiles,)),
+            dma((own_tiles, PLANE // 2)),
+            dma((own_tiles, shards)),
+            dma((own_tiles, shards)),
+            dma((own_tiles, PLANE)),
+            dma((tiles,)),
+            dma((PLANE + shards,)),
+            dma((PLANE + shards,)),
+        ],
+        compiler_params=pltpu.CompilerParams(
+            vmem_limit_bytes=VMEM_MAX, collective_id=3, has_side_effects=True
+        ),
+        cost_estimate=pl.CostEstimate(
+            flops=16000000000, bytes_accessed=50000000, transcendentals=2000000
+        ),
+        name="tail",
+    )(cols, slot_cols, lse, probs, x, grad, weight, back, qkv, mixed, hidden, one, two)
+
+
 def per_device(
     inputs,
     gain_one,
@@ -980,24 +1480,38 @@
         x, grad, weight, cols, slot_rows, own_in, own_out, experts, cap_pad
     )
     back, grad_in, grad_out = run_moe(received, own_in, own_out, spread_in, spread_out)
-    outputs, inputs_grad, dense = run_tail(
-        x, grad, weight, cols, slot_cols, back, saved, experts
-    )
-    dense = lax.psum_scatter(dense, both, scatter_dimension=0, tiled=True)
-    dense = lax.all_gather(dense, "expert", axis=0, tiled=True).astype(F32)
+    spot = 4 * width
+    if groups == PLANE:
+        outputs, inputs_grad, qkv_grad, proj_grad, small_grad = run_reduce(
+            x, grad, weight, cols, slot_cols, back, saved, experts
+        )
+        small_grad = lax.dynamic_slice_in_dim(
+            small_grad, lax.axis_index("dp") * depth, depth, axis=1
+        )
+        vectors = [small_grad[k] for k in range(4)]
+        router_grad = small_grad[4 : 4 + experts].T
+    else:
+        outputs, inputs_grad, dense = run_tail(
+            x, grad, weight, cols, slot_cols, back, saved, experts
+        )
+        dense = lax.psum_scatter(dense, both, scatter_dimension=0, tiled=True)
+        dense = lax.all_gather(dense, "expert", axis=0, tiled=True).astype(F32)
+        qkv_grad = dense[:, : 3 * width]
+        proj_grad = dense[:, 3 * width : spot]
+        vectors = [dense[:, spot + k] for k in range(4)]
+        router_grad = dense[:, spot + 4 : spot + 4 + experts]
     grad_in = grad_in.astype(F32)
     grad_out = grad_out.astype(F32)
-    spot = 4 * width
     return (
         outputs[:, :SEQ].reshape(batches * SEQ, width),
         inputs_grad[:, :SEQ].reshape(batches * SEQ, width),
-        dense[:, spot],
-        dense[:, spot + 1],
-        dense[:, : 3 * width],
-        dense[:, 3 * width : spot],
-        dense[:, spot + 2],
-        dense[:, spot + 3],
-        dense[:, spot + 4 : spot + 4 + experts],
+        vectors[0],
+        vectors[1],
+        qkv_grad,
+        proj_grad,
+        vectors[2],
+        vectors[3],
+        router_grad,
         grad_in[None, :width],
         grad_in[None, width],
         grad_out[None],

time: 606 us -> 528 us (0.87)
  waiting for transfers between devices: 161 us -> 48.2 us
  Pallas kernels: 390 us -> 422 us
    unnamed x4 -> x1, waiting for transfers between devices: 101 us -> 0.02 us
    pallas_call x1, Pallas kernels: 40.2 us -> 71.8 us  [run_reduce(): pl.pallas_call(functools.partial(reduce_kernel, experts, shards), out_sha...]
    all_gather x1 -> x0, waiting for transfers between devices: 11.4 us -> none  [per_device(): dense = lax.all_gather(dense, 'expert', axis=0, tiled=True).astype(F32)]
  transfers between devices with their start and end apart: 3 -> 1, of which waited for: 3 -> 1; matrix products, arithmetic and copies ran while one was open for 5% -> 3% of each run, Pallas kernels for 1% -> 1%
where the time goes in v3:
time: 528 us; the launch traced here: 526 us
  Pallas kernels  422 us (80%)
  waiting for transfers between devices  48.2 us (9%)
  local copies, waits for them, and re-layouts  32.7 us (6%)
  between operations  14.1 us (3%)
  other arithmetic  8.83 us (2%)
    pallas_call x1, Pallas kernels, run_moe(): pl.pallas_call(functools.partial(moe_kernel, shards, groups), out_shape=(...  232 us
    pallas_call x1, Pallas kernels, run_front(): pl.pallas_call(functools.partial(front_kernel, experts, shards), grid=(ba...  114 us
    pallas_call x1, Pallas kernels, run_reduce(): pl.pallas_call(functools.partial(reduce_kernel, experts, shards), out_sha...  71.8 us
    all_gather x1, waiting for transfers between devices, per_device(): weight = lax.all_gather(pack, both, axis=0, tiled=True)  48.2 us
  transfers between devices with their start and end apart: 1, of which 1 were waited for; matrix products, arithmetic and copies ran while one was open for 3% of the time, Pallas kernels for 1%

profile of v3, /device:TPU:0, one launch (start us, length us, event | category | flops | bytes accessed | tf_op | source)
XLA Modules:
  0.0 525.9 jit_solution(2540264055734266930)
XLA Ops:
  7.2 0.0 all-gather.2.cloned.1.call-start
  7.2 0.7 stack.12
  7.9 0.7 stack.13
  8.5 0.7 stack.14
  9.2 0.7 stack.15
  9.9 0.8 concatenate.13
  10.7 0.1 copy.44
  10.8 0.0 copy-start
  10.8 1.7 fusion.4
  12.6 0.0 all-gather.2.cloned.1.call-update
  12.6 0.9 reshape.43
  13.5 0.8 reshape.42
  14.3 0.2 copy.42
  14.5 0.2 pad_add_fusion
  14.7 0.8 pad_bitcast_fusion
  15.5 0.8 copy.43.rows_ref
  16.3 0.0 copy-done
  16.3 1.8 reshape.44
  18.0 2.0 reshape.45
  20.0 3.5 pad.20.x_ref.x_hbm
  23.4 0.0 copy-start.4
  23.4 1.8 pad.21.grad_ref.grad_hbm
  25.2 4.1 route.1
  29.3 0.0 copy-done.4
  29.3 2.4 fusion.1.own_in_ref
  31.6 48.2 %all-gather.2.cloned.1.call-done.weight_ref.weight_hbm = bf16[768,3200]{1,0:T(8,128)(2,1)} async-done(((bf16[24,3200]{1,0:T(8,128)(2,1)}), bf16[768,3200]{1,0:T(8,128)(2,1)}) %all-gather.2.cloned.1.call-update) | async-done | bytes 4915216 | tf_op jit(solution)/shard_map/all_gather | solution.py:1464
  79.8 114.1 %front.1 = (bf16[8,4,2,64,768]{4,3,2,1,0:T(8,128)(2,1)}, bf16[4,208,2304]{2,1,0:T(8,128)(2,1)}, bf16[4,208,768]{2,1,0:T(8,128)(2,1)}, f32[4,208,128]{2,1,0:T(8,1...) custom-call(f32[4,208,768]{2,1,0:T(8,128)} %pad.20.x_ref.x_hbm, ...), custom_call_target="tpu_custom_call" | custom-call | flops 8000000000 | bytes 40000000 | tf_op jit(solution)/shard_map/front/pallas_call | solution.py:330
  193.9 232.1 %moe.1 = (bf16[8,4,2,64,768]{4,3,2,1,0:T(8,128)(2,1)}, bf16[784,768]{1,0:T(8,128)(2,1)}, bf16[768,768]{1,0:T(8,128)(2,1)}) custom-call(bf16[8,4,2,64,768]{4,3,2,1,0:T(8,128)(2,1)} %get-tuple-element.36.x_hbm, bf16[784,768]{1,0:T(8,128)(2,1)} %fusion.1.own_in_ref, bf16[768,768]{1,0:T(8,128)(2,1)} %bitcast.23, ...), custom_call_target="tpu_custom_call" | custom-call | flops 57982058496 | bytes 60000000 | tf_op jit(solution)/shard_map/moe/pallas_call | solution.py:696
  426.0 3.0 convert_element_type.11
  428.9 1.3 slice.37
  430.2 71.8 %tail.1 = (f32[4,208,768]{2,1,0:T(8,128)}, f32[4,208,768]{2,1,0:T(8,128)}, f32[192,2304]{1,0:T(8,128)}, f32[192,768]{1,0:T(8,128)}, f32[16,768]{1,0:T(8,128)}) custom-call(s32[4,208,4]{2,1,0:T(8,128)} %get-tuple-element.53.cols_ref, s32[4,208,8]{2,1,0:T(8,128)} %get-tuple-element.32.slot_cols_ref, f32[4,208,128]{2,1,0:T(8,128)} %get-tuple-element.34.lse_ref, ...), custom_call_target="tpu_custom_call" | custom-call | flops 16000000000 | bytes 50000000 | tf_op jit(solution)/shard_map/tail/pallas_call | solution.py:1372
  502.1 1.9 slice.27
  503.9 1.7 reshape.46
  505.6 1.9 slice.28
  507.5 1.7 reshape.47
  509.2 0.0 copy-start.2
  509.2 3.3 slice_bitcast_fusion
  512.5 0.0 copy-start.1
  512.5 0.0 copy-done.2
  512.5 1.6 bitcast_convert_fusion
  514.1 0.0 copy-start.3
  514.1 1.5 dynamic-slice_bitcast_fusion
  515.6 1.5 fusion.5
  517.1 0.0 copy-done.1
  517.1 1.2 copy.47
  518.3 0.0 copy-done.3
  518.3 0.8 copy.48
Async XLA Ops:
  7.2 72.6 %all-gather.2.cloned.1.call-start = ((), (), s32[]{:S(2)}) async-start(), calls=%async_computation | async-start | bytes 5068800 | tf_op jit(solution)/shard_map/all_gather | solution.py:1464
  10.8 5.5 %copy-start = (f32[788,768]{1,0:T(8,128)S(1)}, f32[788,768]{1,0:T(8,128)}, u32[]{:S(2)}) copy-start(f32[788,768]{1,0:T(8,128)} %param.15) | copy-start | bytes 7262212
  23.4 5.8 %copy-start.4 = (bf16[1,768]{1,0:T(2,128)(2,1)S(1)}, bf16[1,768]{1,0:T(2,128)(2,1)}, u32[]{:S(2)}) copy-start(bf16[1,768]{1,0:T(2,128)(2,1)} %param.24) | copy-start | bytes 4612
  509.2 3.3 copy-start.2
  512.5 4.6 copy-start.1
  514.1 4.2 copy-start.3
Sparse Core Ops, SparseCore 0:
  12.7 67.0 all-gather.1

commit v4 on v3

--- a/solution.py
+++ b/solution.py
@@ -17,6 +17,8 @@
 SMALL = 128
 MESH = pl.DeviceIdType.MESH
 EARLY = 2
+TILE = 128
+PLANE = 8
 BIAS_ROWS = 16
 NEG = -1e30
 VMEM_LIMIT = 60 * 1024 * 1024
@@ -58,35 +60,39 @@
             pl.semaphore_signal(
                 barrier, inc=1, device_id={"expert": lax.rem(me + k, groups)}, device_id_type=MESH
             )
-
-        @pl.when(self.has_below)
-        def _():
-            pl.semaphore_signal(barrier, inc=1, device_id={"dp": self.me - 1}, device_id_type=MESH)
-
-        @pl.when(self.has_above)
-        def _():
-            pl.semaphore_signal(barrier, inc=1, device_id={"dp": self.me + 1}, device_id_type=MESH)
-
-        ends = self.has_below.astype(jnp.int32) + self.has_above.astype(jnp.int32)
-        pl.semaphore_wait(barrier, groups - 1 + ends)
+        for k in range(1, self.shards):
+            pl.semaphore_signal(
+                barrier,
+                inc=1,
+                device_id={"dp": lax.rem(self.me + k, self.shards)},
+                device_id_type=MESH,
+            )
+        pl.semaphore_wait(barrier, groups - 1 + self.shards - 1)
 
     def hop(self, way, round_id, source, target, send_sem, arrived):
         step = 1 - 2 * way
         slot = self.me - step * round_id
-        copies = []
-        for part in range(2):
-            origin = source[part] if round_id == 0 else source[part].at[slot]
-            copies.append(
-                pltpu.make_async_remote_copy(
-                    src_ref=origin,
-                    dst_ref=target[part].at[slot],
-                    send_sem=send_sem.at[way, round_id, part],
-                    recv_sem=arrived.at[slot, part],
-                    device_id={"dp": self.me + step},
-                    device_id_type=MESH,
-                )
+        if round_id == 0:
+            body, bias, out = source
+            tall = body.shape[0]
+            moves = [
+                (body, target[0].at[slot, pl.ds(0, tall)], 0),
+                (bias, target[0].at[slot, pl.ds(tall, bias.shape[0])], 0),
+                (out, target[1].at[slot], 1),
+            ]
+        else:
+            moves = [(source[part].at[slot], target[part].at[slot], part) for part in range(2)]
+        return [
+            pltpu.make_async_remote_copy(
+                src_ref=origin,
+                dst_ref=place,
+                send_sem=send_sem.at[way, round_id, k],
+                recv_sem=arrived.at[slot, part],
+                device_id={"dp": self.me + step},
+                device_id_type=MESH,
             )
-        return copies
+            for k, (origin, place, part) in enumerate(moves)
+        ]
 
     def sends(self, way, round_id):
         if way == 0:
@@ -128,13 +134,11 @@
             pltpu.make_async_copy(view, view, arrived.at[slot, part]).wait()
 
 
-def route_kernel(cap_pad, cols_ref, rows_ref, limit_ref, slot_rows_ref, slot_cols_ref):
+def route(cap_pad, cols_ref, rows_ref, limit_ref, slot_rows_ref, slot_cols_ref):
     for b in range(cols_ref.shape[0]):
         limit = limit_ref[b]
         col = [cols_ref[b, :, k : k + 1] for k in range(4)]
         row = [rows_ref[b, k : k + 1, :] for k in range(4)]
-        slot_rows_ref[b] = jnp.full(slot_rows_ref.shape[1:], -1, jnp.int32)
-        slot_cols_ref[b] = jnp.full(slot_cols_ref.shape[1:], -1, jnp.int32)
         for j in range(2):
             rank_row = 0
             rank_col = 0
@@ -149,29 +153,6 @@
             slot_cols_ref[b, :, j : j + 1] = jnp.where(keep_col, col[j] * cap_pad + rank_col, -1)
 
 
-def run_route(cols, rows, limits, cap_pad):
-    batches = cols.shape[0]
-    return pl.pallas_call(
-        functools.partial(route_kernel, cap_pad),
-        out_shape=(
-            jax.ShapeDtypeStruct((batches, 8, SEQ_PAD), jnp.int32),
-            jax.ShapeDtypeStruct((batches, SEQ_PAD, 8), jnp.int32),
-        ),
-        in_specs=[
-            pl.BlockSpec(memory_space=pltpu.VMEM),
-            pl.BlockSpec(memory_space=pltpu.VMEM),
-            pl.BlockSpec(memory_space=pltpu.SMEM),
-        ],
-        out_specs=(
-            pl.BlockSpec(memory_space=pltpu.VMEM),
-            pl.BlockSpec(memory_space=pltpu.VMEM),
-        ),
-        compiler_params=pltpu.CompilerParams(vmem_limit_bytes=VMEM_LIMIT),
-        cost_estimate=pl.CostEstimate(flops=4000000, bytes_accessed=1000000, transcendentals=0),
-        name="route",
-    )(cols, rows, limits)
-
-
 def norm_stats(values):
     average = jnp.mean(values, axis=-1, keepdims=True)
     centered = values - average
@@ -183,205 +164,372 @@
 def front_kernel(
     experts,
     shards,
+    limit_ref,
+    cols_ref,
+    rows_ref,
+    raw_hbm,
+    raw_grad_hbm,
+    qkv_own,
+    proj_own,
+    small_own,
+    own_body,
+    own_bias,
+    own_out,
+    received_ref,
+    x_hbm,
+    grad_hbm,
+    weight_hbm,
+    qkv_hbm,
+    mixed_hbm,
+    hidden_hbm,
+    one_hbm,
+    two_hbm,
+    lse_ref,
+    probs_ref,
+    slot_cols_ref,
+    spread_in_ref,
+    spread_out_ref,
+    raw_ref,
+    raw_grad_ref,
     x_ref,
     grad_ref,
     weight_ref,
-    cols_ref,
-    slot_rows_ref,
-    own_in_ref,
-    own_out_ref,
-    received_ref,
     qkv_ref,
     mixed_ref,
-    lse_ref,
     hidden_ref,
     one_ref,
     two_ref,
-    probs_ref,
-    spread_in_ref,
-    spread_out_ref,
     small_ref,
+    slot_rows_ref,
     send_ref,
+    load_sem,
+    store_sem,
     send_sem,
     arrived,
     rows_send,
     rows_recv,
+    small_send,
+    small_recv,
+    line_send,
+    piece_recv,
+    plane_send,
+    near_send,
 ):
-    index = pl.program_id(0)
+    batches, rows, width = x_ref.shape
+    groups = received_ref.shape[0]
+    cap_pad = received_ref.shape[3]
     me = lax.axis_index("expert")
-    groups = received_ref.shape[0]
-    width = x_ref.shape[-1]
-    rows = x_ref.shape[1]
     line = Line(shards)
-    own = (own_in_ref, own_out_ref)
+    z = line.me
+    own = (own_body, own_bias, own_out)
     spread = (spread_in_ref, spread_out_ref)
-
-    @pl.when(pl.program_id(0) == 0)
-    def _():
-        line.greet(me, groups)
-        small_ref[...] = weight_ref[:, 4 * width :].astype(F32).T
-        line.push(0, own, spread, send_sem, arrived)
-
-    x = x_ref[0]
-    hat, _ = norm_stats(x)
-    one = (hat * small_ref[0:1, :] + small_ref[1:2, :]).astype(BF)
-    one_ref[0] = one
-    qkv_ref[0] = dot(one, weight_ref[:, : 3 * width]).astype(BF)
+    depth = width // shards
+    piece_width = 4 * width // PLANE
+    base = me // PLANE * PLANE
+    spot = me - base
+    core = lax.rem(me, 2)
+    sibling = me + 1 - 2 * core
+    chip = spot // 2
+    chips = PLANE // 2
+    cut = 3 * width // piece_width
+
+    def remote(source, target, send, recv, peer):
+        return pltpu.make_async_remote_copy(
+            src_ref=source,
+            dst_ref=target,
+            send_sem=send,
+            recv_sem=recv,
+            device_id=peer,
+            device_id_type=MESH,
+        )
+
+    def landed(view, sem):
+        pltpu.make_async_copy(view, view, sem).wait()
+
+    def rows_of(shard):
+        return pl.ds(pl.multiple_of(shard * depth, depth), depth)
+
+    def piece(shard, index):
+        low = pl.multiple_of(index * piece_width, piece_width)
+        return weight_ref.at[rows_of(shard), pl.ds(low, piece_width)]
+
+    small_cols = pl.ds(4 * width, SMALL)
+
+    raws = [
+        pltpu.make_async_copy(raw_hbm, raw_ref, load_sem.at[0]),
+        pltpu.make_async_copy(raw_grad_hbm, raw_grad_ref, load_sem.at[1]),
+    ]
+    mine = [
+        pltpu.make_async_copy(
+            qkv_own, weight_ref.at[rows_of(z), pl.ds(0, 3 * width)], load_sem.at[2]
+        ),
+        pltpu.make_async_copy(
+            proj_own, weight_ref.at[rows_of(z), pl.ds(3 * width, width)], load_sem.at[3]
+        ),
+        pltpu.make_async_copy(small_own, weight_ref.at[rows_of(z), small_cols], load_sem.at[4]),
+    ]
+    for copy in mine:
+        copy.start()
+    for copy in raws:
+        copy.start()
+    line.greet(me, groups)
+    for copy in mine:
+        copy.wait()
+
+    def small_copy(far):
+        view = weight_ref.at[rows_of(z), small_cols]
+        return remote(view, view, small_send.at[far], small_recv.at[z], {"dp": far})
+
+    def line_copy(far):
+        view = piece(z, spot)
+        return remote(view, view, line_send.at[far], piece_recv.at[z, spot], {"dp": far})
+
+    def plane_copy(shard, other):
+        view = piece(shard, spot)
+        peer = base + 2 * other + core
+        return remote(
+            view, view, plane_send.at[shard, other], piece_recv.at[shard, spot], {"expert": peer}
+        )
+
+    def near_copy(shard, other):
+        index = 2 * other + core
+        view = piece(shard, index)
+        return remote(
+            view, view, near_send.at[shard, other], piece_recv.at[shard, index], {"expert": sibling}
+        )
+
+    peers = [lax.rem(z + k, shards) for k in range(1, shards)]
+    others = [lax.rem(chip + k, chips) for k in range(1, chips)]
+    for far in peers:
+        line_copy(far).start()
+    for far in peers:
+        small_copy(far).start()
+    zero_rows = jnp.zeros((rows - SEQ, width), F32)
+
+    def pad_image(image):
+        x_ref[image, :SEQ] = raw_ref[image * SEQ : (image + 1) * SEQ]
+        x_ref[image, SEQ:] = zero_rows
+        pltpu.make_async_copy(x_ref.at[image], x_hbm.at[image], store_sem.at[0, image]).start()
+        grad_ref[image, :SEQ] = raw_grad_ref[image * SEQ : (image + 1) * SEQ]
+        grad_ref[image, SEQ:] = zero_rows
+        pltpu.make_async_copy(
+            grad_ref.at[image], grad_hbm.at[image], store_sem.at[1, image]
+        ).start()
+
+    for copy in raws:
+        copy.wait()
+    pad_image(0)
+    for far in peers:
+        landed(piece(far, spot), piece_recv.at[far, spot])
+        for other in others:
+            plane_copy(far, other).start()
+        near_copy(far, chip).start()
+    line.push(0, own, spread, send_sem, arrived)
+    for image in range(1, batches):
+        pad_image(image)
+    slot_rows_ref[...] = jnp.full(slot_rows_ref.shape, -1, jnp.int32)
+    slot_cols_ref[...] = jnp.full(slot_cols_ref.shape, -1, jnp.int32)
+    route(cap_pad, cols_ref, rows_ref, limit_ref, slot_rows_ref, slot_cols_ref)
+    for far in peers:
+        for other in others:
+            index = 2 * other + core
+            landed(piece(far, index), piece_recv.at[far, index])
+            near_copy(far, other).start()
+    for far in peers:
+        landed(weight_ref.at[rows_of(far), small_cols], small_recv.at[far])
+        for k in range(chips):
+            index = 2 * k + 1 - core
+            landed(piece(far, index), piece_recv.at[far, index])
+    weight_store = pltpu.make_async_copy(weight_ref, weight_hbm, load_sem.at[5])
+    weight_store.start()
+    small_ref[...] = weight_ref[:, 4 * width :].astype(F32).T
+
+    def rows_copy(image, target):
+        return remote(
+            send_ref.at[image, target],
+            received_ref.at[me, image],
+            rows_send.at[image, target],
+            rows_recv.at[me, image],
+            {"expert": target},
+        )
+
+    saves = (
+        (qkv_ref, qkv_hbm),
+        (mixed_ref, mixed_hbm),
+        (hidden_ref, hidden_hbm),
+        (one_ref, one_hbm),
+        (two_ref, two_hbm),
+    )
     lane = lax.broadcasted_iota(jnp.int32, (1, 128), 1)
     key_ok = lax.broadcasted_iota(jnp.int32, (1, rows), 1) < SEQ
-    lse = jnp.zeros((rows, 128), F32)
+    slot = lax.broadcasted_iota(jnp.int32, (groups * cap_pad, 1), 0)
     scale = HEAD ** (-0.5)
-    for pair in range(HEADS // 2):
-        low = pair * 128
-        query = qkv_ref[0, :, low : low + 128]
-        keys = qkv_ref[0, :, width + low : width + low + 128]
-        values = qkv_ref[0, :, 2 * width + low : 2 * width + low + 128]
-        total = None
-        for side in range(2):
-            mine = (lane // HEAD) == side
-            scores = dot_nt(jnp.where(mine, query, jnp.zeros_like(query)), keys) * scale
-            scores = jnp.where(key_ok, scores, NEG)
-            highest = jnp.max(scores, axis=-1, keepdims=True)
-            expo = jnp.exp(scores - highest)
-            denom = jnp.sum(expo, axis=-1, keepdims=True)
-            weights = (expo / denom).astype(BF)
-            lse = jnp.where(lane == 2 * pair + side, highest + jnp.log(denom), lse)
-            part = dot(weights, jnp.where(mine, values, jnp.zeros_like(values)))
-            total = part if total is None else total + part
-        mixed_ref[0, :, low : low + 128] = total.astype(BF)
-    lse_ref[0] = lse
-    hidden = x + dot(mixed_ref[0], weight_ref[:, 3 * width : 4 * width])
-    hidden_ref[0] = hidden
-    hat, _ = norm_stats(hidden)
-    two = (hat * small_ref[2:3, :] + small_ref[3:4, :]).astype(BF)
-    two_ref[0] = two
-    logits = dot(two, weight_ref[:, 4 * width :])
-    in_router = (lane >= 4) & (lane < 4 + experts)
-    logits = jnp.where(in_router, logits, NEG)
-    expo = jnp.exp(logits - jnp.max(logits, axis=-1, keepdims=True))
-    probs = expo / jnp.sum(expo, axis=-1, keepdims=True)
-    probs_ref[0] = probs
-    out_grad = grad_ref[0]
-    cap_pad = send_ref.shape[3]
-    slot = lax.broadcasted_iota(jnp.int32, (groups * cap_pad, 1), 0)
-    both = None
-    grads = None
-    for j in range(2):
-        gate = jnp.sum(
-            jnp.where(lane - 4 == cols_ref[0, :, j : j + 1], probs, 0.0), axis=-1, keepdims=True
-        )
-        pick = (slot == slot_rows_ref[0, j : j + 1, :]).astype(F32)
-        both = pick if both is None else both + pick
-        part = dot(pick.astype(BF), (gate * out_grad).astype(BF))
-        grads = part if grads is None else grads + part
-    sent = dot(both.astype(BF), two).astype(BF)
-    send_ref[index, :, 0] = sent.reshape(groups, cap_pad, width)
-    send_ref[index, :, 1] = grads.astype(BF).reshape(groups, cap_pad, width)
-
-    def rows_copy(image, target):
-        return pltpu.make_async_remote_copy(
-            src_ref=send_ref.at[image, target],
-            dst_ref=received_ref.at[me, image],
-            send_sem=rows_send.at[image, target],
-            recv_sem=rows_recv.at[me, image],
-            device_id={"expert": target},
-            device_id_type=MESH,
-        )
-
-    for k in range(1, groups):
-        rows_copy(index, lax.rem(me + k, groups)).start()
-    pltpu.make_async_copy(
-        send_ref.at[index, me], received_ref.at[me, index], rows_recv.at[me, index]
-    ).start()
-
-    @pl.when(index == pl.num_programs(0) - 1)
-    def _():
-        rounds = min(EARLY, shards - 1)
-        for round_id in range(1, rounds):
-            line.receive(round_id - 1, spread, arrived)
-            line.push(round_id, own, spread, send_sem, arrived)
-
-        def finish(image, carry):
-            for k in range(groups):
-                source = lax.rem(me + k, groups)
-                if k:
-                    rows_copy(image, source).wait_send()
-                view = received_ref.at[source, image]
-                pltpu.make_async_copy(view, view, rows_recv.at[source, image]).wait()
-            return carry
-
-        lax.fori_loop(0, send_ref.shape[0], finish, 0)
-        line.receive(rounds - 1, spread, arrived)
-        for round_id in range(rounds):
-            line.drain(round_id, own, spread, send_sem, arrived)
-
-
-def run_front(x, grad, weight, cols, slot_rows, own_in, own_out, experts, cap_pad):
-    batches, rows, width = x.shape
+
+    def do_image(index, carry):
+        x = x_ref[index]
+        hat, _ = norm_stats(x)
+        one = (hat * small_ref[0:1, :] + small_ref[1:2, :]).astype(BF)
+        one_ref[index] = one
+        qkv_ref[index] = dot(one, weight_ref[:, : 3 * width]).astype(BF)
+        lse = jnp.zeros((rows, 128), F32)
+        for pair in range(HEADS // 2):
+            low = pair * 128
+            query = qkv_ref[index, :, low : low + 128]
+            keys = qkv_ref[index, :, width + low : width + low + 128]
+            values = qkv_ref[index, :, 2 * width + low : 2 * width + low + 128]
+            total = None
+            for side in range(2):
+                part_of = (lane // HEAD) == side
+                scores = dot_nt(jnp.where(part_of, query, jnp.zeros_like(query)), keys) * scale
+                scores = jnp.where(key_ok, scores, NEG)
+                highest = jnp.max(scores, axis=-1, keepdims=True)
+                expo = jnp.exp(scores - highest)
+                denom = jnp.sum(expo, axis=-1, keepdims=True)
+                weights = (expo / denom).astype(BF)
+                lse = jnp.where(lane == 2 * pair + side, highest + jnp.log(denom), lse)
+                part = dot(weights, jnp.where(part_of, values, jnp.zeros_like(values)))
+                total = part if total is None else total + part
+            mixed_ref[index, :, low : low + 128] = total.astype(BF)
+        lse_ref[index] = lse
+        hidden = x + dot(mixed_ref[index], weight_ref[:, 3 * width : 4 * width])
+        hidden_ref[index] = hidden
+        hat, _ = norm_stats(hidden)
+        two = (hat * small_ref[2:3, :] + small_ref[3:4, :]).astype(BF)
+        two_ref[index] = two
+        logits = dot(two, weight_ref[:, 4 * width :])
+        in_router = (lane >= 4) & (lane < 4 + experts)
+        logits = jnp.where(in_router, logits, NEG)
+        expo = jnp.exp(logits - jnp.max(logits, axis=-1, keepdims=True))
+        probs = expo / jnp.sum(expo, axis=-1, keepdims=True)
+        probs_ref[index] = probs
+        out_grad = grad_ref[index]
+        both = None
+        grads = None
+        for j in range(2):
+            gate = jnp.sum(
+                jnp.where(lane - 4 == cols_ref[index, :, j : j + 1], probs, 0.0),
+                axis=-1,
+                keepdims=True,
+            )
+            pick = (slot == slot_rows_ref[index, j : j + 1, :]).astype(F32)
+            both = pick if both is None else both + pick
+            part = dot(pick.astype(BF), (gate * out_grad).astype(BF))
+            grads = part if grads is None else grads + part
+        sent = dot(both.astype(BF), two).astype(BF)
+        send_ref[index, :, 0] = sent.reshape(groups, cap_pad, width)
+        send_ref[index, :, 1] = grads.astype(BF).reshape(groups, cap_pad, width)
+        for k in range(1, groups):
+            rows_copy(index, lax.rem(me + k, groups)).start()
+        pltpu.make_async_copy(
+            send_ref.at[index, me], received_ref.at[me, index], rows_recv.at[me, index]
+        ).start()
+        for k, (here, there) in enumerate(saves):
+            pltpu.make_async_copy(here.at[index], there.at[index], store_sem.at[2 + k, index]).start()
+        return carry
+
+    lax.fori_loop(0, batches, do_image, 0)
+
+    rounds = min(EARLY, shards - 1)
+    for round_id in range(1, rounds):
+        line.receive(round_id - 1, spread, arrived)
+        line.push(round_id, own, spread, send_sem, arrived)
+
+    def finish(image, carry):
+        for k in range(groups):
+            source = lax.rem(me + k, groups)
+            if k:
+                rows_copy(image, source).wait_send()
+            landed(received_ref.at[source, image], rows_recv.at[source, image])
+        pltpu.make_async_copy(x_ref.at[image], x_hbm.at[image], store_sem.at[0, image]).wait()
+        pltpu.make_async_copy(grad_ref.at[image], grad_hbm.at[image], store_sem.at[1, image]).wait()
+        for k, (here, there) in enumerate(saves):
+            pltpu.make_async_copy(here.at[image], there.at[image], store_sem.at[2 + k, image]).wait()
+        return carry
+
+    lax.fori_loop(0, batches, finish, 0)
+    weight_store.wait()
+    for far in peers:
+        line_copy(far).wait_send()
+        small_copy(far).wait_send()
+        for other in others:
+            plane_copy(far, other).wait_send()
+        for k in range(chips):
+            near_copy(far, k).wait_send()
+    line.receive(rounds - 1, spread, arrived)
+    for round_id in range(rounds):
+        line.drain(round_id, own, spread, send_sem, arrived)
+
+
+def run_front(raw, raw_grad, dense, own, cols, rows_first, limits, experts, cap_pad):
+    batches, rows = cols.shape[:2]
+    width = raw.shape[1]
     shards = lax.axis_size("dp")
-    total = weight.shape[1]
-
-    def block(*shape):
-        return pl.BlockSpec((1,) + shape, lambda i: (i,) + (0,) * len(shape))
-
-    def out(shape, dtype):
-        return jax.ShapeDtypeStruct((batches,) + shape, dtype)
+    groups = lax.axis_size("expert")
+    body, bias, out = own
+    tall = body.shape[0] + bias.shape[0]
+    anywhere = pl.BlockSpec(memory_space=pl.ANY)
+    inside = pl.BlockSpec(memory_space=pltpu.VMEM)
+    dma = pltpu.SemaphoreType.DMA
+    chips = PLANE // 2
+
+    def shape(*dims, dtype=BF):
+        return jax.ShapeDtypeStruct((batches, rows) + dims, dtype)
 
     return pl.pallas_call(
         functools.partial(front_kernel, experts, shards),
-        grid=(batches,),
         out_shape=(
-            jax.ShapeDtypeStruct((experts, batches, 2, cap_pad, width), BF),
-            out((rows, 3 * width), BF),
-            out((rows, width), BF),
-            out((rows, 128), F32),
-            out((rows, width), F32),
-            out((rows, width), BF),
-            out((rows, width), BF),
-            out((rows, SMALL), F32),
-            jax.ShapeDtypeStruct((shards,) + own_in.shape, BF),
-            jax.ShapeDtypeStruct((shards,) + own_out.shape, BF),
+            jax.ShapeDtypeStruct((groups, batches, 2, cap_pad, width), BF),
+            shape(width, dtype=F32),
+            shape(width, dtype=F32),
+            jax.ShapeDtypeStruct((width, 4 * width + SMALL), BF),
+            shape(3 * width),
+            shape(width),
+            shape(width, dtype=F32),
+            shape(width),
+            shape(width),
+            shape(128, dtype=F32),
+            shape(SMALL, dtype=F32),
+            shape(8, dtype=jnp.int32),
+            jax.ShapeDtypeStruct((shards, tall, body.shape[1]), BF),
+            jax.ShapeDtypeStruct((shards,) + out.shape, BF),
         ),
-        in_specs=[
-            block(rows, width),
-            block(rows, width),
-            pl.BlockSpec((width, total), lambda i: (0, 0), pipeline_mode=pl.Buffered(1)),
-            block(rows, 4),
-            block(8, rows),
-            pl.BlockSpec(memory_space=pl.ANY),
-            pl.BlockSpec(memory_space=pl.ANY),
-        ],
-        out_specs=(
-            pl.BlockSpec(memory_space=pl.ANY),
-            block(rows, 3 * width),
-            block(rows, width),
-            block(rows, 128),
-            block(rows, width),
-            block(rows, width),
-            block(rows, width),
-            block(rows, SMALL),
-            pl.BlockSpec(memory_space=pl.ANY),
-            pl.BlockSpec(memory_space=pl.ANY),
-        ),
+        in_specs=[pl.BlockSpec(memory_space=pltpu.SMEM), inside, inside] + [anywhere] * 8,
+        out_specs=(anywhere,) * 9 + (inside,) * 3 + (anywhere,) * 2,
         scratch_shapes=[
+            pltpu.VMEM(raw.shape, F32),
+            pltpu.VMEM(raw.shape, F32),
+            pltpu.VMEM((batches, rows, width), F32),
+            pltpu.VMEM((batches, rows, width), F32),
+            pltpu.VMEM((width, 4 * width + SMALL), BF),
+            pltpu.VMEM((batches, rows, 3 * width), BF),
+            pltpu.VMEM((batches, rows, width), BF),
+            pltpu.VMEM((batches, rows, width), F32),
+            pltpu.VMEM((batches, rows, width), BF),
+            pltpu.VMEM((batches, rows, width), BF),
             pltpu.VMEM((SMALL, width), F32),
-            pltpu.VMEM((batches, experts, 2, cap_pad, width), BF),
-            pltpu.SemaphoreType.DMA((2, EARLY, 2)),
-            pltpu.SemaphoreType.DMA((shards, 2)),
-            pltpu.SemaphoreType.DMA((batches, experts)),
-            pltpu.SemaphoreType.DMA((experts, batches)),
+            pltpu.VMEM((batches, 8, rows), jnp.int32),
+            pltpu.VMEM((batches, groups, 2, cap_pad, width), BF),
+            dma((6,)),
+            dma((7, batches)),
+            dma((2, EARLY, 3)),
+            dma((shards, 2)),
+            dma((batches, groups)),
+            dma((groups, batches)),
+            dma((shards,)),
+            dma((shards,)),
+            dma((shards,)),
+            dma((shards, PLANE)),
+            dma((shards, chips)),
+            dma((shards, chips)),
         ],
         compiler_params=pltpu.CompilerParams(
-            dimension_semantics=("arbitrary",),
-            vmem_limit_bytes=VMEM_LIMIT,
-            collective_id=1,
-            has_side_effects=True,
+            vmem_limit_bytes=VMEM_LIMIT, collective_id=1, has_side_effects=True
         ),
         cost_estimate=pl.CostEstimate(
             flops=8000000000, bytes_accessed=40000000, transcendentals=3000000
         ),
         name="front",
-    )(x, grad, weight, cols, slot_rows, own_in, own_out)
+    )(limits, cols, rows_first, raw, raw_grad, *dense, *own)
 
 
 def pieces_of(tall, span):
@@ -394,8 +542,9 @@
     shards,
     groups,
     x_hbm,
-    own_in_ref,
-    own_out_ref,
+    own_body,
+    own_bias,
+    own_out,
     spread_in_ref,
     spread_out_ref,
     back_ref,
@@ -425,7 +574,7 @@
     z = line.me
     me = lax.axis_index("expert")
     _, batches, _, cap_pad, width = rows_ref.shape
-    tall, span = own_in_ref.shape
+    _, tall, span = spread_in_ref.shape
     group = max(1, 512 // (batches * cap_pad))
     while groups % group:
         group -= 1
@@ -434,7 +583,7 @@
     early = min(EARLY, shards - 1)
     spread = (win_ref, wout_ref)
     early_spread = (spread_in_ref, spread_out_ref)
-    own = (own_in_ref, own_out_ref)
+    own = (own_body, own_bias, own_out)
     parts = (part_in_ref, part_out_ref)
     lands = (land_in_ref, land_out_ref)
     pieces = pieces_of(tall, span)
@@ -442,8 +591,13 @@
     for k in range(groups):
         source = lax.rem(me + k, groups)
         pltpu.make_async_copy(x_hbm.at[source], rows_ref.at[source], rows_sem.at[source]).start()
-    for part in range(2):
-        pltpu.make_async_copy(own[part], spread[part].at[z], arrived.at[z, part]).start()
+    mine = (
+        (own_body, win_ref.at[z, pl.ds(0, width)], 0),
+        (own_bias, win_ref.at[z, pl.ds(width, tall - width)], 0),
+        (own_out, wout_ref.at[z], 1),
+    )
+    for here, there, part in mine:
+        pltpu.make_async_copy(here, there, arrived.at[z, part]).start()
     for far in range(1, early + 1):
         for sign in (-1, 1):
             slot = z + sign * far
@@ -687,7 +841,7 @@
         copy.wait()
 
 
-def run_moe(received, own_in, own_out, spread_in, spread_out):
+def run_moe(received, own, spread_in, spread_out):
     groups, batches, _, cap_pad, width = received.shape
     shards, tall, span = spread_in.shape
     total = groups * batches * cap_pad
@@ -700,7 +854,7 @@
             jax.ShapeDtypeStruct((tall, span), BF),
             jax.ShapeDtypeStruct((span, width), BF),
         ),
-        in_specs=[anywhere] * 5,
+        in_specs=[anywhere] * 6,
         out_specs=(anywhere,) * 3,
         scratch_shapes=[
             pltpu.VMEM(received.shape, BF),
@@ -732,7 +886,7 @@
             transcendentals=2 * total * span * shards,
         ),
         name="moe",
-    )(received, own_in, own_out, spread_in, spread_out)
+    )(received, *own, spread_in, spread_out)
 
 
 def tail_kernel(
@@ -926,10 +1080,6 @@
         ),
         name="tail",
     )(x, grad, weight, cols, slot_cols, back, qkv, mixed, lse, hidden, one, two, probs)
-
-
-TILE = 128
-PLANE = 8
 
 
 def reduce_kernel(
@@ -1457,29 +1607,17 @@
     vectors = jnp.stack([gain_one, shift_one, gain_two, shift_two], axis=1)
     small = jnp.concatenate([vectors, router_weight], axis=1)
     small = jnp.pad(small, ((0, 0), (0, SMALL - small.shape[1])))
-    pack = jnp.concatenate([qkv_weight, proj_weight, small], axis=1)
-    slice_rows = depth // groups
-    mine = lax.axis_index("expert")
-    pack = lax.dynamic_slice_in_dim(pack, mine * slice_rows, slice_rows, axis=0)
-    weight = lax.all_gather(pack, both, axis=0, tiled=True)
-
-    bias_rows = jnp.pad(expert_bias, ((0, BIAS_ROWS - 1), (0, 0)))
-    own_in = jnp.concatenate([expert_in[0], bias_rows], axis=0)
-    own_out = expert_out[0]
-
-    extra = SEQ_PAD - SEQ
-    x = jnp.pad(inputs.reshape(batches, SEQ, width), ((0, 0), (0, extra), (0, 0)))
-    grad = jnp.pad(out_grad.reshape(batches, SEQ, width), ((0, 0), (0, extra), (0, 0)))
-    cols = jnp.concatenate(
-        [routes.reshape(batches, SEQ, 2), priority.reshape(batches, SEQ, 2)], axis=2
+    dense = (qkv_weight, proj_weight, small)
+    own = (expert_in[0], jnp.pad(expert_bias, ((0, BIAS_ROWS - 1), (0, 0))), expert_out[0])
+    cols = jnp.concatenate([routes, priority.reshape(batches * SEQ, 2)], axis=1)
+    cols = cols.reshape(batches, SEQ, 4)
+    cols = jnp.pad(cols, ((0, 0), (0, SEQ_PAD - SEQ), (0, 0)), constant_values=-1)
+    rows_first = jnp.swapaxes(cols, 1, 2)
+    received, x, grad, weight, qkv, mixed, hidden, one, two, lse, probs, slot_cols, *spread = run_front(
+        inputs, out_grad, dense, own, cols, rows_first, capacity, experts, cap_pad
     )
-    cols = jnp.pad(cols, ((0, 0), (0, extra), (0, 0)), constant_values=-1)
-    rows = jnp.swapaxes(cols, 1, 2)
-    slot_rows, slot_cols = run_route(cols, rows, capacity, cap_pad)
-    received, *saved, spread_in, spread_out = run_front(
-        x, grad, weight, cols, slot_rows, own_in, own_out, experts, cap_pad
-    )
-    back, grad_in, grad_out = run_moe(received, own_in, own_out, spread_in, spread_out)
+    saved = (qkv, mixed, lse, hidden, one, two, probs)
+    back, grad_in, grad_out = run_moe(received, own, *spread)
     spot = 4 * width
     if groups == PLANE:
         outputs, inputs_grad, qkv_grad, proj_grad, small_grad = run_reduce(

time: 528 us -> 460 us (0.87)
  waiting for transfers between devices: 48.2 us -> 0 us
  between operations: 14.1 us -> 0.82 us
  Pallas kernels: 422 us -> 435 us
  local copies, waits for them, and re-layouts: 32.7 us -> 20.4 us
  other arithmetic: 8.83 us -> 3.2 us
    all_gather x1 -> x0, waiting for transfers between devices: 48.2 us -> none  [per_device(): weight = lax.all_gather(pack, both, axis=0, tiled=True)]
    pallas_call x2 -> x1, Pallas kernels: 118 us -> 132 us  [run_front(): pl.pallas_call(functools.partial(front_kernel, experts, shards), out_shap...]
    reshape x5 -> x0, local copies, waits for them, and re-layouts: 5.59 us -> none  [the longest x1 1.96 us: per_device(): out_grad.reshape(batches, SEQ, width)]
  transfers between devices with their start and end apart: 1 -> 0, of which waited for: 1 -> 0; matrix products, arithmetic and copies ran while one was open for 3% -> 0% of each run, Pallas kernels for 1% -> 0%
where the time goes in v4:
time: 460 us; the launch traced here: 459 us
  Pallas kernels  435 us (95%)
  local copies, waits for them, and re-layouts  20.4 us (4%)
    pallas_call x1, Pallas kernels, run_moe(): pl.pallas_call(functools.partial(moe_kernel, shards, groups), out_shape=(...  232 us
    pallas_call x1, Pallas kernels, run_front(): pl.pallas_call(functools.partial(front_kernel, experts, shards), out_shap...  132 us
    pallas_call x1, Pallas kernels, run_reduce(): pl.pallas_call(functools.partial(reduce_kernel, experts, shards), out_sha...  71.2 us

profile of v4, /device:TPU:0, one launch (start us, length us, event | category | flops | bytes accessed | tf_op | source)
XLA Modules:
  0.0 459.2 jit_solution(9433812117353974408)
XLA Ops:
  0.6 0.0 copy-start.4
  0.7 0.0 copy-start.5
  0.7 0.0 copy-start.6
  0.7 0.0 copy-start.7
  0.7 0.0 copy-start.8
  0.7 0.0 copy-start.3
  0.7 0.8 concatenate.11
  1.5 0.2 copy.42
  1.7 0.9 concatenate.12
  2.6 0.2 pad_add_fusion
  2.8 0.8 pad_bitcast_fusion
  3.6 0.8 copy.44.rows_ref
  4.4 0.0 copy-done.4
  4.4 0.6 pad.14.own_bias
  5.0 0.0 copy-done.5
  5.0 0.0 copy-done.6
  5.1 0.0 copy-done.7
  5.1 0.0 copy-done.8
  5.1 0.0 copy-done.3
  5.1 0.1 concatenate.14
  5.2 0.1 copy.43
  5.4 0.6 pad.13.small_own
  6.0 131.9 %front.1 = (bf16[8,4,2,64,768]{4,3,2,1,0:T(8,128)(2,1)}, f32[4,208,768]{2,1,0:T(8,128)}, f32[4,208,768]{2,1,0:T(8,128)}, bf16[768,3200]{1,0:T(8,128)(2,1)}, bf16...) custom-call(s32[4]{0:T(128)} %limit_ref.1, ...), custom_call_target="tpu_custom_call" | custom-call | flops 8000000000 | bytes 40000000 | tf_op jit(solution)/shard_map/front/pallas_call | solution.py:478
  137.9 231.8 %moe.1 = (bf16[8,4,2,64,768]{4,3,2,1,0:T(8,128)(2,1)}, bf16[784,768]{1,0:T(8,128)(2,1)}, bf16[768,768]{1,0:T(8,128)(2,1)}) custom-call(bf16[8,4,2,64,768]{4,3,2,1,0:T(8,128)(2,1)} %get-tuple-element.40.x_hbm, bf16[768,768]{1,0:T(8,128)(2,1)} %bitcast.22, bf16[16,768]{1,0:T(8,128)(2,1)} %pad.14.own_bias, bf16[768,768]{1,0:T(8,128)(2,1)} %bitcast.24, ...), custom_call_target="tpu_custom_call" | custom-call | flops 57982058496 | bytes 60000000 | tf_op jit(solution)/shard_map/moe/pallas_call | solution.py:850
  369.7 71.2 %tail.1 = (f32[4,208,768]{2,1,0:T(8,128)}, f32[4,208,768]{2,1,0:T(8,128)}, f32[192,2304]{1,0:T(8,128)}, f32[192,768]{1,0:T(8,128)}, f32[16,768]{1,0:T(8,128)}) custom-call(s32[4,208,4]{2,1,0:T(8,128)} %get-tuple-element.57.cols_ref, s32[4,208,8]{2,1,0:T(8,128)} %get-tuple-element.34.slot_cols_ref, f32[4,208,128]{2,1,0:T(8,128)} %get-tuple-element.35.lse_ref, ...), custom_call_target="tpu_custom_call" | custom-call | flops 16000000000 | bytes 50000000 | tf_op jit(solution)/shard_map/tail/pallas_call | solution.py:1522
  440.9 1.9 slice.27
  442.7 1.7 reshape.35
  444.4 1.9 slice.28
  446.3 1.7 reshape.36
  448.0 1.4 dynamic-slice_bitcast_fusion
  449.4 1.5 fusion
  450.9 1.4 convert_element_type.8
  452.4 0.0 copy-start.1
  452.4 1.6 slice_bitcast_fusion
  453.9 0.0 copy-start
  453.9 1.4 slice.37
  455.3 0.0 copy-done.1
  455.3 1.6 bitcast_convert_fusion
  456.9 0.0 copy-done
  456.9 0.0 copy-start.2
  456.9 1.2 copy.47
  458.1 0.3 copy-done.2
  458.4 0.8 copy.48
  (4 shorter events, 0.0 us)
Async XLA Ops:
  0.6 3.8 copy-start.4
  0.7 4.4 copy-start.5
  0.7 4.4 copy-start.6
  0.7 4.4 copy-start.7
  0.7 4.4 copy-start.8
  0.7 4.4 copy-start.3
  452.4 3.0 copy-start.1
  453.9 3.0 copy-start
  456.9 1.5 copy-start.2

commit v5 on v4

--- a/solution.py
+++ b/solution.py
@@ -17,6 +17,20 @@
 SMALL = 128
 MESH = pl.DeviceIdType.MESH
 EARLY = 2
+FAR_CUTS = 4
+FAR_TURNS = (
+    (0, True, 1),
+    (0, True, 2),
+    (1, True, 3),
+    (1, False, 0),
+    (2, True, 4),
+    (2, False, 1),
+    (3, False, 2),
+    (4, True, 5),
+    (4, False, 3),
+    (5, True, 6),
+    (5, False, 4),
+)
 TILE = 128
 PLANE = 8
 BIAS_ROWS = 16
@@ -532,10 +546,13 @@
     )(limits, cols, rows_first, raw, raw_grad, *dense, *own)
 
 
-def pieces_of(tall, span):
-    half = ceil_to(tall // 2, 16)
-    mid = ceil_to(span // 2, 16)
-    return ((0, 0, half), (0, half, tall - half), (1, 0, mid), (1, mid, span - mid))
+def pieces_of(tall, span, cuts=2):
+    pieces = []
+    for kind, extent in enumerate((tall, span)):
+        size = ceil_to(-(-extent // cuts), 16)
+        for low in range(0, extent, size):
+            pieces.append((kind, low, min(size, extent - low)))
+    return tuple(pieces)
 
 
 def moe_kernel(
@@ -550,6 +567,8 @@
     back_ref,
     sum_in_ref,
     sum_out_ref,
+    far_in_ref,
+    far_out_ref,
     rows_ref,
     win_ref,
     wout_ref,
@@ -616,7 +635,7 @@
     table = []
     for at in range(shards):
         near = sorted(range(shards), key=lambda q: (abs(q - at), q))
-        table.append(near[1:] + near[:1])
+        table.append(near[1:-1] + near[:1] + near[-1:])
 
     def quarter(step):
         total = 0
@@ -629,10 +648,10 @@
     def sum_copy(way, q, piece):
         kind, low, size = pieces[piece]
         if way == 0:
-            slot = q
+            slot = q - 1
             peer = z + 1
         else:
-            slot = jnp.where(q == z - 1, shards, q)
+            slot = jnp.where(q == z - 1, shards - 2, q - 1)
             peer = z - 1
         cut = pl.ds(low, size)
         return pltpu.make_async_remote_copy(
@@ -680,105 +699,122 @@
     def block_first(block):
         return lax.rem(me // group + 1 + block, blocks) * group
 
-    def do_step(step, carry):
+    plain = (shards - 2) * blocks
+    inner = (z > 0) & (z < shards - 1)
+
+    def do_item(item, carry):
+        late = item >= plain
+        rest = item - plain
+        step = jnp.where(late, shards - 2 + lax.rem(rest + 2 * blocks, 2), item // blocks)
+        block = jnp.where(late, (rest + 2 * blocks) // 2 - blocks, lax.rem(item, blocks))
         q = quarter(step)
-        line.wait_slot(q, spread, arrived)
-        for round_id in range(early, shards - 2):
-            for way in range(2):
-                forward = 1 - 2 * way
-
-                @pl.when((q == z - forward * (round_id + 1)) & line.sends(way, round_id + 1))
-                def _():
-                    for copy in line.hop(way, round_id + 1, spread, spread, weight_send, arrived):
-                        copy.start()
-
-        def do_block(block, inner):
-            lead = block_first(block)
-            low = pl.multiple_of(lead * (batches * cap_pad), rows)
-            here = pl.ds(low, rows)
-            mine = pl.ds(lead, group)
-
-            @pl.when(step == 0)
+        bank = jnp.where(step == shards - 1, 1, 0)
+
+        @pl.when(block == 0)
+        def _():
+            line.wait_slot(q, spread, arrived)
+            for round_id in range(early, shards - 2):
+                for way in range(2):
+                    forward = 1 - 2 * way
+
+                    @pl.when((q == z - forward * (round_id + 1)) & line.sends(way, round_id + 1))
+                    def _():
+                        for copy in line.hop(
+                            way, round_id + 1, spread, spread, weight_send, arrived
+                        ):
+                            copy.start()
+
+        @pl.when((step == shards - 2) & (block > 0))
+        def _():
+            back_start(block_first(block - 1))
+
+        lead = block_first(block)
+        low = pl.multiple_of(lead * (batches * cap_pad), rows)
+        here = pl.ds(low, rows)
+        mine = pl.ds(lead, group)
+
+        @pl.when(step == 0)
+        def _():
+            for k in range(group):
+                view = rows_ref.at[lead + k]
+                pltpu.make_async_copy(view, view, rows_sem.at[lead + k]).wait()
+
+        x = rows_ref[mine, :, 0].reshape(rows, width)
+        grad = rows_ref[mine, :, 1].reshape(rows, width)
+        win = win_ref[q, :width, :]
+        wout = wout_ref[q]
+        pre = dot(x, win) + win_ref[q, width : width + 1, :].astype(F32)
+        cdf = 0.5 * lax.erf(pre * (0.5**0.5)) + 0.5
+        active = (pre * cdf).astype(BF)
+        slope = cdf + pre * (jnp.exp(-0.5 * pre * pre) * 0.3989422804014327)
+        d_pre = (dot_nt(grad, wout) * slope).astype(BF)
+        y_part = dot(active, wout)
+        dx_part = dot_nt(d_pre, win)
+
+        @pl.when(step == 0)
+        def _():
+            y_acc[here, :] = y_part
+            dx_acc[here, :] = dx_part
+
+        @pl.when(step > 0)
+        def _():
+            y_acc[here, :] += y_part
+            dx_acc[here, :] += dx_part
+
+        gout = dot_tn(active, grad)
+        gin = dot_tn(x, d_pre)
+        gbias = jnp.sum(d_pre.astype(F32), axis=0, keepdims=True)
+
+        @pl.when(block == 0)
+        def _():
+            gout_acc[bank] = gout
+            gin_acc[bank, :width, :] = gin
+            gin_acc[bank, width : width + 1, :] = gbias
+
+        @pl.when(block > 0)
+        def _():
+            gout_acc[bank] += gout
+            gin_acc[bank, :width, :] += gin
+            gin_acc[bank, width : width + 1, :] += gbias
+
+        @pl.when(step == shards - 1)
+        def _():
+            shape = (group, batches, cap_pad, width)
+            rows_ref[mine, :, 0] = y_acc[here, :].astype(BF).reshape(shape)
+            rows_ref[mine, :, 1] = dx_acc[here, :].astype(BF).reshape(shape)
+
+        @pl.when(block == blocks - 1)
+        def _():
+            part_in_ref[q, :width, :] = gin_acc[bank, :width, :].astype(BF)
+            part_in_ref[q, width:, :] = jnp.broadcast_to(
+                gin_acc[bank, width : width + 1, :].astype(BF), (tall - width, span)
+            )
+            part_out_ref[q] = gout_acc[bank].astype(BF)
+
+            @pl.when((z == 0) & (q > z) & (q < shards - 1))
             def _():
-                for k in range(group):
-                    view = rows_ref.at[lead + k]
-                    pltpu.make_async_copy(view, view, rows_sem.at[lead + k]).wait()
-
-            x = rows_ref[mine, :, 0].reshape(rows, width)
-            grad = rows_ref[mine, :, 1].reshape(rows, width)
-            win = win_ref[q, :width, :]
-            wout = wout_ref[q]
-            pre = dot(x, win) + win_ref[q, width : width + 1, :].astype(F32)
-            cdf = 0.5 * lax.erf(pre * (0.5**0.5)) + 0.5
-            active = (pre * cdf).astype(BF)
-            slope = cdf + pre * (jnp.exp(-0.5 * pre * pre) * 0.3989422804014327)
-            d_pre = (dot_nt(grad, wout) * slope).astype(BF)
-            y_part = dot(active, wout)
-            dx_part = dot_nt(d_pre, win)
-
-            @pl.when(step == 0)
+                for piece in range(len(pieces)):
+                    sum_copy(0, q, piece).start()
+
+            @pl.when((z == shards - 1) & (q < z) & (q > 0))
             def _():
-                y_acc[here, :] = y_part
-                dx_acc[here, :] = dx_part
-
-            @pl.when(step > 0)
-            def _():
-                y_acc[here, :] += y_part
-                dx_acc[here, :] += dx_part
-
-            gout = dot_tn(active, grad)
-            gin = dot_tn(x, d_pre)
-            gbias = jnp.sum(d_pre.astype(F32), axis=0, keepdims=True)
-
-            @pl.when(block == 0)
-            def _():
-                gout_acc[...] = gout
-                gin_acc[:width, :] = gin
-                gin_acc[width : width + 1, :] = gbias
-
-            @pl.when(block > 0)
-            def _():
-                gout_acc[...] += gout
-                gin_acc[:width, :] += gin
-                gin_acc[width : width + 1, :] += gbias
-
-            @pl.when(step == shards - 1)
-            def _():
-                shape = (group, batches, cap_pad, width)
-                rows_ref[mine, :, 0] = y_acc[here, :].astype(BF).reshape(shape)
-                rows_ref[mine, :, 1] = dx_acc[here, :].astype(BF).reshape(shape)
-
-                @pl.when(block > 0)
-                def _():
-                    back_start(block_first(block - 1))
-
-            return inner
-
-        lax.fori_loop(0, blocks, do_block, 0)
-
-        @pl.when(step == shards - 1)
-        def _():
-            back_start(block_first(blocks - 1))
-
-        part_in_ref[q, :width, :] = gin_acc[:width, :].astype(BF)
-        part_in_ref[q, width:, :] = jnp.broadcast_to(
-            gin_acc[width : width + 1, :].astype(BF), (tall - width, span)
-        )
-        part_out_ref[q] = gout_acc[...].astype(BF)
-
-        @pl.when((z == 0) & (q > z))
-        def _():
-            for piece in range(len(pieces)):
-                sum_copy(0, q, piece).start()
-
-        @pl.when((z == shards - 1) & (q < z))
-        def _():
-            for piece in range(len(pieces)):
-                sum_copy(1, q, piece).start()
+                for piece in range(len(pieces)):
+                    sum_copy(1, q, piece).start()
 
         return carry
 
-    lax.fori_loop(0, shards, do_step, 0)
+    lax.fori_loop(0, shards * blocks, do_item, 0)
+    back_start(block_first(blocks - 1))
+    finals = [
+        pltpu.make_async_copy(part_in_ref.at[0], far_in_ref.at[0], final_sem.at[0]),
+        pltpu.make_async_copy(part_out_ref.at[0], far_out_ref.at[0], final_sem.at[1]),
+        pltpu.make_async_copy(part_in_ref.at[shards - 1], far_in_ref.at[1], final_sem.at[2]),
+        pltpu.make_async_copy(part_out_ref.at[shards - 1], far_out_ref.at[1], final_sem.at[3]),
+        pltpu.make_async_copy(part_in_ref.at[z], sum_in_ref, final_sem.at[4]),
+        pltpu.make_async_copy(part_out_ref.at[z], sum_out_ref, final_sem.at[5]),
+    ]
+    for copy in finals[:4]:
+        copy.start()
 
     def do_forward(turn, carry):
         up = turn
@@ -787,32 +823,25 @@
 
             @pl.when((up > z) & (z > 0))
             def _():
-                take_sum(up, up, piece)
+                take_sum(up - 1, up, piece)
                 sum_copy(0, up, piece).start()
 
             @pl.when((down < z) & (z < shards - 1))
             def _():
-                take_sum(down, down, piece)
+                take_sum(down - 1, down, piece)
                 sum_copy(1, down, piece).start()
 
         return carry
 
-    lax.fori_loop(1, shards, do_forward, 0)
+    lax.fori_loop(1, shards - 1, do_forward, 0)
     for piece in range(len(pieces)):
 
-        @pl.when(line.has_below)
-        def _():
-            take_sum(z, z, piece)
-
-        @pl.when(line.has_above)
-        def _():
-            take_sum(shards, z, piece)
-
-    finals = [
-        pltpu.make_async_copy(part_in_ref.at[z], sum_in_ref, final_sem.at[0]),
-        pltpu.make_async_copy(part_out_ref.at[z], sum_out_ref, final_sem.at[1]),
-    ]
-    for copy in finals:
+        @pl.when(inner)
+        def _():
+            take_sum(z - 1, z, piece)
+            take_sum(shards - 2, z, piece)
+
+    for copy in finals[4:]:
         copy.start()
 
     def finish_sum(q, carry):
@@ -828,7 +857,7 @@
 
         return carry
 
-    lax.fori_loop(0, shards, finish_sum, 0)
+    lax.fori_loop(1, shards - 1, finish_sum, 0)
     for round_id in range(early, shards - 1):
         line.drain(round_id, own, spread, weight_send, arrived)
     for k in range(groups):
@@ -853,29 +882,31 @@
             jax.ShapeDtypeStruct(received.shape, BF),
             jax.ShapeDtypeStruct((tall, span), BF),
             jax.ShapeDtypeStruct((span, width), BF),
+            jax.ShapeDtypeStruct((2, tall, span), BF),
+            jax.ShapeDtypeStruct((2, span, width), BF),
         ),
         in_specs=[anywhere] * 6,
-        out_specs=(anywhere,) * 3,
+        out_specs=(anywhere,) * 5,
         scratch_shapes=[
             pltpu.VMEM(received.shape, BF),
             pltpu.VMEM((shards, tall, span), BF),
             pltpu.VMEM((shards, span, width), BF),
             pltpu.VMEM((total, width), F32),
             pltpu.VMEM((total, width), F32),
-            pltpu.VMEM((ceil_to(width + 1, 8), span), F32),
-            pltpu.VMEM((span, width), F32),
+            pltpu.VMEM((2, ceil_to(width + 1, 8), span), F32),
+            pltpu.VMEM((2, span, width), F32),
             pltpu.VMEM((shards, tall, span), BF),
             pltpu.VMEM((shards, span, width), BF),
-            pltpu.VMEM((shards + 1, tall, span), BF),
-            pltpu.VMEM((shards + 1, span, width), BF),
+            pltpu.VMEM((shards - 1, tall, span), BF),
+            pltpu.VMEM((shards - 1, span, width), BF),
             pltpu.SemaphoreType.DMA((groups,)),
             pltpu.SemaphoreType.DMA((2, shards, 2)),
             pltpu.SemaphoreType.DMA((shards, 2)),
             pltpu.SemaphoreType.DMA((2, shards, count)),
-            pltpu.SemaphoreType.DMA((shards + 1, count)),
+            pltpu.SemaphoreType.DMA((shards - 1, count)),
             pltpu.SemaphoreType.DMA((groups,)),
             pltpu.SemaphoreType.DMA((groups,)),
-            pltpu.SemaphoreType.DMA((2,)),
+            pltpu.SemaphoreType.DMA((6,)),
         ],
         compiler_params=pltpu.CompilerParams(
             vmem_limit_bytes=VMEM_MAX, collective_id=2, has_side_effects=True
@@ -1098,8 +1129,12 @@
     hidden_hbm,
     one_hbm,
     two_hbm,
+    far_in_hbm,
+    far_out_hbm,
     out_hbm,
     dx_hbm,
+    end_in_hbm,
+    end_out_hbm,
     qkv_grad_ref,
     proj_grad_ref,
     small_grad_ref,
@@ -1127,6 +1162,10 @@
     final_ref,
     small_land,
     small_far,
+    far_in_ref,
+    far_out_ref,
+    far_in_land,
+    far_out_land,
     load_sem,
     store_sem,
     near_send,
@@ -1139,6 +1178,9 @@
     final_recv,
     small_send,
     small_recv,
+    far_load,
+    far_send,
+    far_recv,
 ):
     batches, rows, width = x_ref.shape
     z = lax.axis_index("dp")
@@ -1160,18 +1202,38 @@
             3: (mixed_hbm.at[image], mixed_ref.at[pl.ds(image * rows, rows)]),
             4: (two_hbm.at[image], two_ref.at[pl.ds(image * rows, rows)]),
             5: (one_hbm.at[image], one_ref.at[pl.ds(image * rows, rows)]),
-            6: (qkv_hbm.at[image], qkv_ref.at[image]),
+            6: (qkv_hbm.at[image], qkv_ref.at[pl.ds(image * rows, rows)]),
             7: (x_hbm.at[image], x_ref.at[image]),
         }[kind]
         return pltpu.make_async_copy(pair[0], pair[1], load_sem.at[kind, image])
 
     weight_load = pltpu.make_async_copy(weight_hbm, weight_ref, load_sem.at[8, 0])
+    far_parts = (far_in_ref, far_out_ref)
+    far_lands = (far_in_land, far_out_land)
+    far_loads = [
+        pltpu.make_async_copy(source.at[k], target.at[k], far_load.at[k, part])
+        for k in range(2)
+        for part, (source, target) in enumerate(
+            ((far_in_hbm, far_in_ref), (far_out_hbm, far_out_ref))
+        )
+    ]
+
+    @pl.when((z == 0) | (z == shards - 1))
+    def _():
+        for copy in far_loads:
+            copy.start()
+
     for kind in range(3):
         loads(kind, 0).start()
     weight_load.start()
     for image in range(1, batches):
         for kind in range(3):
             loads(kind, image).start()
+    @pl.when((z > 0) & (z < shards - 1))
+    def _():
+        for copy in far_loads:
+            copy.start()
+
     for kind in range(3, 8):
         for image in range(batches):
             loads(kind, image).start()
@@ -1200,10 +1262,60 @@
     def landed(view, sem):
         pltpu.make_async_copy(view, view, sem).wait()
 
+    pieces = pieces_of(far_in_ref.shape[1], far_out_ref.shape[1], FAR_CUTS)
+    inner = (z > 0) & (z < shards - 1)
+    low_half = 2 * z < shards
+
+    def far_copy(k, piece):
+        kind, low, size = pieces[piece]
+        cut = pl.ds(low, size)
+        return remote(
+            far_parts[kind].at[k, cut],
+            far_lands[kind].at[k, cut],
+            far_send.at[k, piece],
+            far_recv.at[k, piece],
+            {"dp": z + 2 * k - 1},
+        )
+
+    def far_take(k, piece):
+        kind, low, size = pieces[piece]
+        cut = pl.ds(low, size)
+        landed(far_lands[kind].at[k, cut], far_recv.at[k, piece])
+        far_parts[kind][k, cut] = (
+            far_parts[kind][k, cut].astype(F32) + far_lands[kind][k, cut].astype(F32)
+        ).astype(BF)
+
+    def far_forward(k, piece):
+        far_take(k, piece)
+        far_copy(k, piece).start()
+
+    def pass_on(first, piece):
+        @pl.when(inner & low_half)
+        def _():
+            far_forward(1 if first else 0, piece)
+
+        @pl.when(inner & jnp.logical_not(low_half))
+        def _():
+            far_forward(0 if first else 1, piece)
+
+    @pl.when(z == 0)
+    def _():
+        for copy in far_loads:
+            copy.wait()
+        for piece in range(len(pieces)):
+            far_copy(1, piece).start()
+
+    @pl.when(z == shards - 1)
+    def _():
+        for copy in far_loads:
+            copy.wait()
+        for piece in range(len(pieces)):
+            far_copy(0, piece).start()
+
     def near_copy(tile):
         return remote(
             tiles_ref.at[tile],
-            near_ref.at[tile],
+            near_ref.at[tile // 2],
             near_send.at[tile],
             near_recv.at[tile],
             {"expert": sibling},
@@ -1245,9 +1357,9 @@
     def combine(tile):
         @pl.when(lax.rem(tile, 2) == core)
         def _():
-            landed(near_ref.at[tile], near_recv.at[tile])
+            landed(near_ref.at[tile // 2], near_recv.at[tile])
             tiles_ref[tile] = (
-                tiles_ref[tile].astype(F32) + near_ref[tile].astype(F32)
+                tiles_ref[tile].astype(F32) + near_ref[tile // 2].astype(F32)
             ).astype(BF)
 
             @pl.when(lax.rem(tile, PLANE) != me)
@@ -1331,6 +1443,13 @@
         return carry
 
     lax.fori_loop(0, batches, phase_one, 0)
+
+    @pl.when(inner)
+    def _():
+        for copy in far_loads:
+            copy.wait()
+
+    pass_on(True, 0)
     for kind, view in ((3, mixed_ref), (4, two_ref), (5, one_ref)):
         for image in range(batches):
             landed(view.at[pl.ds(image * rows, rows)], load_sem.at[kind, image])
@@ -1342,7 +1461,7 @@
     one_flip[...] = one_ref[...].T
     flipped = dot_tn(d_logits_ref[...], two_ref[...])
     for image in range(batches):
-        landed(qkv_ref.at[image], load_sem.at[6, image])
+        landed(qkv_ref.at[pl.ds(image * rows, rows)], load_sem.at[6, image])
 
     key_ok = lax.broadcasted_iota(jnp.int32, (1, rows), 1) < SEQ
     scale = HEAD ** (-0.5)
@@ -1352,7 +1471,7 @@
         spots = [pl.ds(pl.multiple_of(part * width + low, TILE), TILE) for part in range(3)]
         for image in range(batches):
             here = pl.ds(image * rows, rows)
-            query, keys, values = (qkv_ref[image, :, spot] for spot in spots)
+            query, keys, values = (qkv_ref[here, spot] for spot in spots)
             d_mixed = d_mixed_ref[here, pl.ds(low, TILE)]
             total = [None, None, None]
             for side in range(2):
@@ -1396,6 +1515,12 @@
             for part in range(3):
                 combine(first - 3 + part)
 
+        for turn, first, piece in FAR_TURNS:
+
+            @pl.when(pair == turn)
+            def _():
+                pass_on(first, piece)
+
         @pl.when(pair == pairs - 3)
         def _():
             plane_sum(0)
@@ -1430,6 +1555,8 @@
 
         @pl.when(image == batches // 2 - 1)
         def _():
+            pass_on(True, 7)
+            pass_on(False, 5)
             line_sum(1)
             plane_sum(2)
 
@@ -1456,6 +1583,7 @@
     sums_ref[...] += flipped[: sums_ref.shape[0]]
     for k in range(1, PLANE):
         small_copy(k).start()
+    pass_on(False, 6)
     line_sum(2)
     total = sums_ref[...]
     for k in range(1, PLANE):
@@ -1470,6 +1598,7 @@
         landed(small_far.at[peer], small_recv.at[PLANE + peer])
         total = total + small_far[peer]
     small_grad_ref[...] = total
+    pass_on(False, 7)
 
     def finish(tile, carry):
         @pl.when(lax.rem(tile, PLANE) != me)
@@ -1502,12 +1631,41 @@
         small_copy(k).wait_send()
     for k in range(1, shards):
         small_far_copy(k).wait_send()
+    for piece in range(len(pieces)):
+
+        @pl.when(z == 0)
+        def _():
+            far_take(0, piece)
+
+        @pl.when(z == shards - 1)
+        def _():
+            far_take(1, piece)
+
+    mine = jnp.where(z == shards - 1, 1, 0)
+    ends = [
+        pltpu.make_async_copy(far_in_ref.at[mine], end_in_hbm, far_load.at[0, 0]),
+        pltpu.make_async_copy(far_out_ref.at[mine], end_out_hbm, far_load.at[0, 1]),
+    ]
+    for copy in ends:
+        copy.start()
+    for piece in range(len(pieces)):
+
+        @pl.when(z < shards - 1)
+        def _():
+            far_copy(1, piece).wait_send()
+
+        @pl.when(z > 0)
+        def _():
+            far_copy(0, piece).wait_send()
+
+    for copy in ends:
+        copy.wait()
     for image in range(batches):
         pltpu.make_async_copy(hidden_ref.at[image], out_hbm.at[image], store_sem.at[0, image]).wait()
         pltpu.make_async_copy(x_ref.at[image], dx_hbm.at[image], store_sem.at[1, image]).wait()
 
 
-def run_reduce(x, grad, weight, cols, slot_cols, back, saved, experts):
+def run_reduce(x, grad, weight, cols, slot_cols, back, saved, far, experts):
     batches, rows, width = x.shape
     total = weight.shape[1]
     shards = lax.axis_size("dp")
@@ -1516,6 +1674,7 @@
     tiles = 4 * width // TILE
     own_tiles = tiles // PLANE
     small_rows = ceil_to(4 + experts, 8)
+    count = len(pieces_of(far[0].shape[1], far[1].shape[1], FAR_CUTS))
     anywhere = pl.BlockSpec(memory_space=pl.ANY)
     inside = pl.BlockSpec(memory_space=pltpu.VMEM)
     dma = pltpu.SemaphoreType.DMA
@@ -1524,18 +1683,20 @@
         out_shape=(
             jax.ShapeDtypeStruct(x.shape, F32),
             jax.ShapeDtypeStruct(x.shape, F32),
+            jax.ShapeDtypeStruct(far[0].shape[1:], BF),
+            jax.ShapeDtypeStruct(far[1].shape[1:], BF),
             jax.ShapeDtypeStruct((depth, 3 * width), F32),
             jax.ShapeDtypeStruct((depth, width), F32),
             jax.ShapeDtypeStruct((small_rows, width), F32),
         ),
-        in_specs=[inside] * 4 + [anywhere] * 9,
-        out_specs=(anywhere, anywhere, inside, inside, inside),
+        in_specs=[inside] * 4 + [anywhere] * 11,
+        out_specs=(anywhere,) * 4 + (inside,) * 3,
         scratch_shapes=[
             pltpu.VMEM(x.shape, F32),
             pltpu.VMEM(x.shape, F32),
             pltpu.VMEM(weight.shape, BF),
             pltpu.VMEM(back.shape, BF),
-            pltpu.VMEM(qkv.shape, BF),
+            pltpu.VMEM((batches * rows, 3 * width), BF),
             pltpu.VMEM((batches * rows, width), BF),
             pltpu.VMEM(x.shape, F32),
             pltpu.VMEM((batches * rows, width), BF),
@@ -1548,13 +1709,17 @@
             pltpu.VMEM((batches * rows, width), BF),
             pltpu.VMEM((batches * rows, SMALL), BF),
             pltpu.VMEM((tiles, width, TILE), BF),
-            pltpu.VMEM((tiles, width, TILE), BF),
+            pltpu.VMEM((tiles // 2, width, TILE), BF),
             pltpu.VMEM((own_tiles, PLANE // 2, width, TILE), BF),
             pltpu.VMEM((own_tiles, width, TILE), BF),
             pltpu.VMEM((own_tiles, shards, depth, TILE), BF),
             pltpu.VMEM((tiles, depth, TILE), BF),
             pltpu.VMEM((PLANE, small_rows, width), F32),
             pltpu.VMEM((shards, small_rows, width), F32),
+            pltpu.VMEM(far[0].shape, BF),
+            pltpu.VMEM(far[1].shape, BF),
+            pltpu.VMEM(far[0].shape, BF),
+            pltpu.VMEM(far[1].shape, BF),
             dma((9, batches)),
             dma((2, batches)),
             dma((tiles,)),
@@ -1567,6 +1732,9 @@
             dma((tiles,)),
             dma((PLANE + shards,)),
             dma((PLANE + shards,)),
+            dma((2, 2)),
+            dma((2, count)),
+            dma((2, count)),
         ],
         compiler_params=pltpu.CompilerParams(
             vmem_limit_bytes=VMEM_MAX, collective_id=3, has_side_effects=True
@@ -1575,7 +1743,12 @@
             flops=16000000000, bytes_accessed=50000000, transcendentals=2000000
         ),
         name="tail",
-    )(cols, slot_cols, lse, probs, x, grad, weight, back, qkv, mixed, hidden, one, two)
+    )(cols, slot_cols, lse, probs, x, grad, weight, back, qkv, mixed, hidden, one, two, *far)
+
+
+def last_turn(far_in, far_out):
+    at = lax.axis_index("dp") // (lax.axis_size("dp") - 1)
+    return [lax.psum(far.astype(F32), "dp").astype(BF)[at] for far in (far_in, far_out)]
 
 
 def per_device(
@@ -1617,11 +1790,13 @@
         inputs, out_grad, dense, own, cols, rows_first, capacity, experts, cap_pad
     )
     saved = (qkv, mixed, lse, hidden, one, two, probs)
-    back, grad_in, grad_out = run_moe(received, own, *spread)
+    back, sum_in, sum_out, far_in, far_out = run_moe(received, own, *spread)
+    z = lax.axis_index("dp")
+    at_end = (z == 0) | (z == lax.axis_size("dp") - 1)
     spot = 4 * width
     if groups == PLANE:
-        outputs, inputs_grad, qkv_grad, proj_grad, small_grad = run_reduce(
-            x, grad, weight, cols, slot_cols, back, saved, experts
+        outputs, inputs_grad, end_in, end_out, qkv_grad, proj_grad, small_grad = run_reduce(
+            x, grad, weight, cols, slot_cols, back, saved, (far_in, far_out), experts
         )
         small_grad = lax.dynamic_slice_in_dim(
             small_grad, lax.axis_index("dp") * depth, depth, axis=1
@@ -1632,14 +1807,15 @@
         outputs, inputs_grad, dense = run_tail(
             x, grad, weight, cols, slot_cols, back, saved, experts
         )
+        end_in, end_out = last_turn(far_in, far_out)
         dense = lax.psum_scatter(dense, both, scatter_dimension=0, tiled=True)
         dense = lax.all_gather(dense, "expert", axis=0, tiled=True).astype(F32)
         qkv_grad = dense[:, : 3 * width]
         proj_grad = dense[:, 3 * width : spot]
         vectors = [dense[:, spot + k] for k in range(4)]
         router_grad = dense[:, spot + 4 : spot + 4 + experts]
-    grad_in = grad_in.astype(F32)
-    grad_out = grad_out.astype(F32)
+    grad_in = jnp.where(at_end, end_in, sum_in).astype(F32)
+    grad_out = jnp.where(at_end, end_out, sum_out).astype(F32)
     return (
         outputs[:, :SEQ].reshape(batches * SEQ, width),
         inputs_grad[:, :SEQ].reshape(batches * SEQ, width),

time: 460 us -> 403 us (0.88)
  Pallas kernels: 435 us -> 379 us
    pallas_call x1, Pallas kernels: 232 us -> 127 us  [run_moe(): pl.pallas_call(functools.partial(moe_kernel, shards, groups), out_shape=(...]
    pallas_call x1, Pallas kernels: 71.2 us -> 120 us  [run_reduce(): pl.pallas_call(functools.partial(reduce_kernel, experts, shards), out_sha...]
where the time goes in v5:
time: 403 us
  Pallas kernels  379 us (94%)
  local copies, waits for them, and re-layouts  19.7 us (5%)
    pallas_call x1, Pallas kernels, run_front(): pl.pallas_call(functools.partial(front_kernel, experts, shards), out_shap...  132 us
    pallas_call x1, Pallas kernels, run_moe(): pl.pallas_call(functools.partial(moe_kernel, shards, groups), out_shape=(...  127 us
    pallas_call x1, Pallas kernels, run_reduce(): pl.pallas_call(functools.partial(reduce_kernel, experts, shards), out_sha...  120 us

profile of v5, /device:TPU:0, one launch (start us, length us, event | category | flops | bytes accessed | tf_op | source)
XLA Modules:
  0.0 402.8 jit_solution(6534366396910575784)
XLA Ops:
  0.6 0.0 copy-start.5
  0.7 0.0 copy-start.6
  0.7 0.0 copy-start.7
  0.7 0.0 copy-start.8
  0.7 0.0 copy-start.9
  0.7 0.0 copy-start.4
  0.7 0.8 concatenate.11
  1.5 0.2 copy.42
  1.7 0.9 concatenate.12
  2.6 0.2 pad_add_fusion
  2.8 0.8 pad_bitcast_fusion
  3.6 0.8 copy.44.rows_ref
  4.4 0.0 copy-done.5
  4.4 0.6 pad.14.own_bias
  5.0 0.0 copy-done.6
  5.0 0.0 copy-done.7
  5.1 0.0 copy-done.8
  5.1 0.0 copy-done.9
  5.1 0.0 copy-done.4
  5.1 0.1 concatenate.14
  5.2 0.1 copy.43
  5.4 0.6 pad.13.small_own
  6.0 131.9 %front.1 = (bf16[8,4,2,64,768]{4,3,2,1,0:T(8,128)(2,1)}, f32[4,208,768]{2,1,0:T(8,128)}, f32[4,208,768]{2,1,0:T(8,128)}, bf16[768,3200]{1,0:T(8,128)(2,1)}, bf16...) custom-call(s32[4]{0:T(128)} %limit_ref.1, ...), custom_call_target="tpu_custom_call" | custom-call | flops 8000000000 | bytes 40000000 | tf_op jit(solution)/shard_map/front/pallas_call | solution.py:492
  138.0 127.0 %moe.1 = (bf16[8,4,2,64,768]{4,3,2,1,0:T(8,128)(2,1)}, bf16[784,768]{1,0:T(8,128)(2,1)}, bf16[768,768]{1,0:T(8,128)(2,1)}, bf16[2,784,768]{2,1,0:T(8,128)(2,1)}, bf16[2,768,768]{2,1,0:T(8,128)(2,1)}) custom-call(bf16[8,4,2,64,768]{4,3,2,1,0:T(8,128)(2,1)} %get-tuple-element.44.x_hbm, bf16[768,768]{1,0:T(8,128)(2,1)} %bitcast.22, ...), custom_call_target="tpu_custom_call" | custom-call | flops 57982058496 | bytes 60000000 | tf_op jit(solution)/shard_map/moe/pallas_call | solution.py:879
  264.9 120.0 %tail.1 = (f32[4,208,768]{2,1,0:T(8,128)}, f32[4,208,768]{2,1,0:T(8,128)}, bf16[784,768]{1,0:T(8,128)(2,1)}, bf16[768,768]{1,0:T(8,128)(2,1)}, f32[192,2304]{1,0...) custom-call(s32[4,208,4]{2,1,0:T(8,128)} %get-tuple-element.65.cols_ref, s32[4,208,8]{2,1,0:T(8,128)} %get-tuple-element.38.slot_cols_ref, ...), custom_call_target="tpu_custom_call" | custom-call | flops 16000000000 | bytes 50000000 | tf_op jit(solution)/shard_map/tail/pallas_call | solution.py:1681
  385.0 0.0 copy-start.1
  385.0 0.0 copy-start.2
  385.0 3.0 bitcast_convert_fusion
  388.0 0.0 copy-done.1
  388.0 0.0 copy-done.2
  388.0 0.2 select_convert_fusion
  388.2 0.0 copy-start
  388.2 1.6 slice_bitcast_fusion
  389.7 0.6 slice.37
  390.3 0.4 copy-done
  390.7 0.2 slice.27
  391.0 1.7 reshape.35
  392.7 1.9 slice.28
  394.5 1.7 reshape.36
  396.2 0.0 copy-start.3
  396.2 1.5 dynamic-slice_bitcast_fusion
  397.7 1.5 fusion
  399.2 2.8 copy.47
  402.0 0.0 copy-done.3
  402.0 0.8 copy.48
  (4 shorter events, 0.0 us)
Async XLA Ops:
  0.6 3.8 copy-start.5
  0.7 4.4 %copy-start.6 = (bf16[192]{0:T(256)(128)(2,1)S(1)}, bf16[192]{0:T(256)(128)(2,1)}, u32[]{:S(2)}) copy-start(bf16[192]{0:T(256)(128)(2,1)} %param.16) | copy-start | bytes 1156
  0.7 4.4 %copy-start.7 = (bf16[192]{0:T(256)(128)(2,1)S(1)}, bf16[192]{0:T(256)(128)(2,1)}, u32[]{:S(2)}) copy-start(bf16[192]{0:T(256)(128)(2,1)} %param.17) | copy-start | bytes 1156
  0.7 4.4 %copy-start.8 = (bf16[192]{0:T(256)(128)(2,1)S(1)}, bf16[192]{0:T(256)(128)(2,1)}, u32[]{:S(2)}) copy-start(bf16[192]{0:T(256)(128)(2,1)} %param.20) | copy-start | bytes 1156
  0.7 4.4 %copy-start.9 = (bf16[192]{0:T(256)(128)(2,1)S(1)}, bf16[192]{0:T(256)(128)(2,1)}, u32[]{:S(2)}) copy-start(bf16[192]{0:T(256)(128)(2,1)} %param.21) | copy-start | bytes 1156
  0.7 4.4 %copy-start.4 = (bf16[192,8]{0,1:T(8,128)(2,1)S(1)}, bf16[192,8]{0,1:T(8,128)(2,1)}, u32[]{:S(2)}) copy-start(bf16[192,8]{0,1:T(8,128)(2,1)} %param.22) | copy-start | bytes 9220
  385.0 3.0 copy-start.1
  385.0 3.0 copy-start.2
  388.2 2.6 copy-start
  396.2 5.8 %copy-start.3 = (f32[192,768]{1,0:T(8,128)S(1)}, f32[192,768]{1,0:T(8,128)}, u32[]{:S(2)}) copy-start(f32[192,768]{1,0:T(8,128)} %get-tuple-element.87) | copy-start | bytes 1769476

commit v6 on v5

--- a/solution.py
+++ b/solution.py
@@ -16,20 +16,19 @@
 F32 = jnp.float32
 SMALL = 128
 MESH = pl.DeviceIdType.MESH
-EARLY = 2
+EARLY_PIECES = range(3)
+LATE_PIECES = range(3, 4)
+EARLY_FAR = 2
 FAR_CUTS = 4
 FAR_TURNS = (
-    (0, True, 1),
-    (0, True, 2),
-    (1, True, 3),
-    (1, False, 0),
-    (2, True, 4),
-    (2, False, 1),
-    (3, False, 2),
-    (4, True, 5),
-    (4, False, 3),
-    (5, True, 6),
-    (5, False, 4),
+    (0, True, 4),
+    (0, False, 2),
+    (1, True, 5),
+    (1, False, 3),
+    (3, True, 6),
+    (3, False, 4),
+    (4, True, 7),
+    (4, False, 5),
 )
 TILE = 128
 PLANE = 8
@@ -83,29 +82,39 @@
             )
         pl.semaphore_wait(barrier, groups - 1 + self.shards - 1)
 
-    def hop(self, way, round_id, source, target, send_sem, arrived):
+    def views(self, pair, slot):
+        tall, span = pair[0].shape[1:]
+        return [
+            pair[kind].at[slot, pl.ds(low, size)] for kind, low, size in pieces_of(tall, span)
+        ]
+
+    def hop(self, way, round_id, source, target, send_sem, arrived, some=range(4)):
         step = 1 - 2 * way
         slot = self.me - step * round_id
+        places = self.views(target, slot)
         if round_id == 0:
             body, bias, out = source
-            tall = body.shape[0]
-            moves = [
-                (body, target[0].at[slot, pl.ds(0, tall)], 0),
-                (bias, target[0].at[slot, pl.ds(tall, bias.shape[0])], 0),
-                (out, target[1].at[slot], 1),
-            ]
+            tall, span = target[0].shape[1:]
+            moves = []
+            for piece, (kind, low, size) in enumerate(pieces_of(tall, span)):
+                own = out if kind else body
+                here = min(size, own.shape[0] - low)
+                moves.append((own.at[pl.ds(low, here)], target[kind].at[slot, pl.ds(low, here)], piece))
+                if here < size:
+                    moves.append((bias, target[kind].at[slot, pl.ds(low + here, size - here)], piece))
         else:
-            moves = [(source[part].at[slot], target[part].at[slot], part) for part in range(2)]
+            origins = self.views(source, slot)
+            moves = [(origins[piece], places[piece], piece) for piece in some]
         return [
             pltpu.make_async_remote_copy(
                 src_ref=origin,
                 dst_ref=place,
-                send_sem=send_sem.at[way, round_id, k],
-                recv_sem=arrived.at[slot, part],
+                send_sem=send_sem.at[way, round_id, k if round_id == 0 else piece],
+                recv_sem=arrived.at[slot, piece],
                 device_id={"dp": self.me + step},
                 device_id_type=MESH,
             )
-            for k, (origin, place, part) in enumerate(moves)
+            for k, (origin, place, piece) in enumerate(moves)
         ]
 
     def sends(self, way, round_id):
@@ -113,39 +122,37 @@
             return (self.me >= round_id) & self.has_above
         return (self.me + round_id < self.shards) & self.has_below
 
-    def push(self, round_id, own, spread, send_sem, arrived, source=None):
-        source = own if round_id == 0 else (source or spread)
+    def push(self, round_id, source, target, send_sem, arrived, some=range(4)):
         for way in range(2):
 
             @pl.when(self.sends(way, round_id))
             def _():
-                for copy in self.hop(way, round_id, source, spread, send_sem, arrived):
+                for copy in self.hop(way, round_id, source, target, send_sem, arrived, some):
                     copy.start()
 
-    def drain(self, round_id, own, spread, send_sem, arrived, source=None):
-        source = own if round_id == 0 else (source or spread)
+    def drain(self, round_id, source, target, send_sem, arrived, some=range(4)):
         for way in range(2):
 
             @pl.when(self.sends(way, round_id))
             def _():
-                for copy in self.hop(way, round_id, source, spread, send_sem, arrived):
+                for copy in self.hop(way, round_id, source, target, send_sem, arrived, some):
                     copy.wait_send()
 
-    def receive(self, round_id, spread, arrived):
+    def receive(self, round_id, target, arrived, some=range(4)):
         far = round_id + 1
 
         @pl.when(self.me >= far)
         def _():
-            self.wait_slot(self.me - far, spread, arrived)
+            self.wait_slot(self.me - far, target, arrived, some)
 
         @pl.when(self.me + far < self.shards)
         def _():
-            self.wait_slot(self.me + far, spread, arrived)
-
-    def wait_slot(self, slot, spread, arrived):
-        for part in range(2):
-            view = spread[part].at[slot]
-            pltpu.make_async_copy(view, view, arrived.at[slot, part]).wait()
+            self.wait_slot(self.me + far, target, arrived, some)
+
+    def wait_slot(self, slot, target, arrived, some=range(4)):
+        places = self.views(target, slot)
+        for piece in some:
+            pltpu.make_async_copy(places[piece], places[piece], arrived.at[slot, piece]).wait()
 
 
 def route(cap_pad, cols_ref, rows_ref, limit_ref, slot_rows_ref, slot_cols_ref):
@@ -201,6 +208,7 @@
     lse_ref,
     probs_ref,
     slot_cols_ref,
+    vectors_ref,
     spread_in_ref,
     spread_out_ref,
     raw_ref,
@@ -213,7 +221,7 @@
     hidden_ref,
     one_ref,
     two_ref,
-    small_ref,
+    small_land,
     slot_rows_ref,
     send_ref,
     load_sem,
@@ -267,8 +275,6 @@
         low = pl.multiple_of(index * piece_width, piece_width)
         return weight_ref.at[rows_of(shard), pl.ds(low, piece_width)]
 
-    small_cols = pl.ds(4 * width, SMALL)
-
     raws = [
         pltpu.make_async_copy(raw_hbm, raw_ref, load_sem.at[0]),
         pltpu.make_async_copy(raw_grad_hbm, raw_grad_ref, load_sem.at[1]),
@@ -280,7 +286,7 @@
         pltpu.make_async_copy(
             proj_own, weight_ref.at[rows_of(z), pl.ds(3 * width, width)], load_sem.at[3]
         ),
-        pltpu.make_async_copy(small_own, weight_ref.at[rows_of(z), small_cols], load_sem.at[4]),
+        pltpu.make_async_copy(small_own, small_land.at[z], load_sem.at[4]),
     ]
     for copy in mine:
         copy.start()
@@ -291,7 +297,7 @@
         copy.wait()
 
     def small_copy(far):
-        view = weight_ref.at[rows_of(z), small_cols]
+        view = small_land.at[z]
         return remote(view, view, small_send.at[far], small_recv.at[z], {"dp": far})
 
     def line_copy(far):
@@ -318,6 +324,7 @@
         line_copy(far).start()
     for far in peers:
         small_copy(far).start()
+    line.push(0, own, spread, send_sem, arrived)
     zero_rows = jnp.zeros((rows - SEQ, width), F32)
 
     def pad_image(image):
@@ -338,25 +345,31 @@
         for other in others:
             plane_copy(far, other).start()
         near_copy(far, chip).start()
-    line.push(0, own, spread, send_sem, arrived)
     for image in range(1, batches):
         pad_image(image)
     slot_rows_ref[...] = jnp.full(slot_rows_ref.shape, -1, jnp.int32)
     slot_cols_ref[...] = jnp.full(slot_cols_ref.shape, -1, jnp.int32)
     route(cap_pad, cols_ref, rows_ref, limit_ref, slot_rows_ref, slot_cols_ref)
+    slot_cols_ref[:, :, 2:4] = cols_ref[:, :, 0:2]
     for far in peers:
         for other in others:
             index = 2 * other + core
             landed(piece(far, index), piece_recv.at[far, index])
             near_copy(far, other).start()
     for far in peers:
-        landed(weight_ref.at[rows_of(far), small_cols], small_recv.at[far])
+        landed(small_land.at[far], small_recv.at[far])
         for k in range(chips):
             index = 2 * k + 1 - core
             landed(piece(far, index), piece_recv.at[far, index])
     weight_store = pltpu.make_async_copy(weight_ref, weight_hbm, load_sem.at[5])
     weight_store.start()
-    small_ref[...] = weight_ref[:, 4 * width :].astype(F32).T
+    used = small_land.shape[1]
+    small_rows = jnp.concatenate(
+        [small_land[shard, :, :depth].astype(F32) for shard in range(shards)], axis=1
+    )
+    vectors_ref[...] = jnp.zeros_like(vectors_ref)
+    vectors_ref[:used] = small_rows.astype(BF)
+    gain_one, shift_one, gain_two, shift_two = (small_rows[k : k + 1] for k in range(4))
 
     def rows_copy(image, target):
         return remote(
@@ -382,7 +395,7 @@
     def do_image(index, carry):
         x = x_ref[index]
         hat, _ = norm_stats(x)
-        one = (hat * small_ref[0:1, :] + small_ref[1:2, :]).astype(BF)
+        one = (hat * gain_one + shift_one).astype(BF)
         one_ref[index] = one
         qkv_ref[index] = dot(one, weight_ref[:, : 3 * width]).astype(BF)
         lse = jnp.zeros((rows, 128), F32)
@@ -408,9 +421,9 @@
         hidden = x + dot(mixed_ref[index], weight_ref[:, 3 * width : 4 * width])
         hidden_ref[index] = hidden
         hat, _ = norm_stats(hidden)
-        two = (hat * small_ref[2:3, :] + small_ref[3:4, :]).astype(BF)
+        two = (hat * gain_two + shift_two).astype(BF)
         two_ref[index] = two
-        logits = dot(two, weight_ref[:, 4 * width :])
+        logits = dot_nt(two, vectors_ref[...])
         in_router = (lane >= 4) & (lane < 4 + experts)
         logits = jnp.where(in_router, logits, NEG)
         expo = jnp.exp(logits - jnp.max(logits, axis=-1, keepdims=True))
@@ -443,10 +456,8 @@
 
     lax.fori_loop(0, batches, do_image, 0)
 
-    rounds = min(EARLY, shards - 1)
-    for round_id in range(1, rounds):
-        line.receive(round_id - 1, spread, arrived)
-        line.push(round_id, own, spread, send_sem, arrived)
+    line.receive(0, spread, arrived)
+    line.push(1, spread, spread, send_sem, arrived, EARLY_PIECES)
 
     def finish(image, carry):
         for k in range(groups):
@@ -469,9 +480,9 @@
             plane_copy(far, other).wait_send()
         for k in range(chips):
             near_copy(far, k).wait_send()
-    line.receive(rounds - 1, spread, arrived)
-    for round_id in range(rounds):
-        line.drain(round_id, own, spread, send_sem, arrived)
+    line.receive(1, spread, arrived, EARLY_PIECES)
+    line.drain(0, own, spread, send_sem, arrived)
+    line.drain(1, spread, spread, send_sem, arrived, EARLY_PIECES)
 
 
 def run_front(raw, raw_grad, dense, own, cols, rows_first, limits, experts, cap_pad):
@@ -495,7 +506,7 @@
             jax.ShapeDtypeStruct((groups, batches, 2, cap_pad, width), BF),
             shape(width, dtype=F32),
             shape(width, dtype=F32),
-            jax.ShapeDtypeStruct((width, 4 * width + SMALL), BF),
+            jax.ShapeDtypeStruct((width, 4 * width), BF),
             shape(3 * width),
             shape(width),
             shape(width, dtype=F32),
@@ -504,29 +515,30 @@
             shape(128, dtype=F32),
             shape(SMALL, dtype=F32),
             shape(8, dtype=jnp.int32),
+            jax.ShapeDtypeStruct((SMALL, width), BF),
             jax.ShapeDtypeStruct((shards, tall, body.shape[1]), BF),
             jax.ShapeDtypeStruct((shards,) + out.shape, BF),
         ),
         in_specs=[pl.BlockSpec(memory_space=pltpu.SMEM), inside, inside] + [anywhere] * 8,
-        out_specs=(anywhere,) * 9 + (inside,) * 3 + (anywhere,) * 2,
+        out_specs=(anywhere,) * 9 + (inside,) * 4 + (anywhere,) * 2,
         scratch_shapes=[
             pltpu.VMEM(raw.shape, F32),
             pltpu.VMEM(raw.shape, F32),
             pltpu.VMEM((batches, rows, width), F32),
             pltpu.VMEM((batches, rows, width), F32),
-            pltpu.VMEM((width, 4 * width + SMALL), BF),
+            pltpu.VMEM((width, 4 * width), BF),
             pltpu.VMEM((batches, rows, 3 * width), BF),
             pltpu.VMEM((batches, rows, width), BF),
             pltpu.VMEM((batches, rows, width), F32),
             pltpu.VMEM((batches, rows, width), BF),
             pltpu.VMEM((batches, rows, width), BF),
-            pltpu.VMEM((SMALL, width), F32),
+            pltpu.VMEM((shards,) + dense[2].shape, BF),
             pltpu.VMEM((batches, 8, rows), jnp.int32),
             pltpu.VMEM((batches, groups, 2, cap_pad, width), BF),
             dma((6,)),
             dma((7, batches)),
-            dma((2, EARLY, 3)),
-            dma((shards, 2)),
+            dma((2, 2, 5)),
+            dma((shards, 4)),
             dma((batches, groups)),
             dma((groups, batches)),
             dma((shards,)),
@@ -580,7 +592,11 @@
     part_out_ref,
     land_in_ref,
     land_out_ref,
+    far_land,
     rows_sem,
+    own_sem,
+    far_send,
+    far_recv,
     weight_send,
     arrived,
     sum_send,
@@ -599,38 +615,47 @@
         group -= 1
     blocks = groups // group
     rows = group * batches * cap_pad
-    early = min(EARLY, shards - 1)
     spread = (win_ref, wout_ref)
     early_spread = (spread_in_ref, spread_out_ref)
     own = (own_body, own_bias, own_out)
     parts = (part_in_ref, part_out_ref)
     lands = (land_in_ref, land_out_ref)
     pieces = pieces_of(tall, span)
+    far_pieces = pieces_of(tall, span, FAR_CUTS)
 
     for k in range(groups):
         source = lax.rem(me + k, groups)
         pltpu.make_async_copy(x_hbm.at[source], rows_ref.at[source], rows_sem.at[source]).start()
-    mine = (
+    own_places = (
         (own_body, win_ref.at[z, pl.ds(0, width)], 0),
-        (own_bias, win_ref.at[z, pl.ds(width, tall - width)], 0),
-        (own_out, wout_ref.at[z], 1),
+        (own_bias, win_ref.at[z, pl.ds(width, tall - width)], 1),
+        (own_out, wout_ref.at[z], 2),
     )
-    for here, there, part in mine:
-        pltpu.make_async_copy(here, there, arrived.at[z, part]).start()
-    for far in range(1, early + 1):
+    own_loads = [
+        pltpu.make_async_copy(here, there, own_sem.at[k]) for here, there, k in own_places
+    ]
+
+    def fetch(far, some):
         for sign in (-1, 1):
             slot = z + sign * far
 
             @pl.when((slot >= 0) & (slot < shards))
             def _():
-                for part in range(2):
+                origins = line.views(early_spread, slot)
+                places = line.views(spread, slot)
+                for piece in some:
                     pltpu.make_async_copy(
-                        early_spread[part].at[slot], spread[part].at[slot], arrived.at[slot, part]
+                        origins[piece], places[piece], arrived.at[slot, piece]
                     ).start()
 
+    fetch(1, range(4))
+    fetch(2, EARLY_PIECES)
+    for copy in own_loads:
+        copy.start()
+
     line.greet(me, groups)
-    if early < shards - 1:
-        line.push(early, own, spread, weight_send, arrived, early_spread)
+    line.push(1, early_spread, spread, weight_send, arrived, LATE_PIECES)
+    line.push(2, early_spread, spread, weight_send, arrived, EARLY_PIECES)
 
     table = []
     for at in range(shards):
@@ -697,9 +722,17 @@
                 ).start()
 
     def block_first(block):
-        return lax.rem(me // group + 1 + block, blocks) * group
+        lead = me // group
+        if blocks == 4:
+            order = (3 - lead, lead + 1 - 2 * lax.rem(lead, 2), lax.rem(lead + 2, 4), lead)
+            picked = 0
+            for k in range(4):
+                picked = picked + jnp.where(block == k, order[k], 0)
+            return picked * group
+        return lax.rem(lead + 1 + block, blocks) * group
 
     plain = (shards - 2) * blocks
+    late_item = max(1, blocks - 1)
     inner = (z > 0) & (z < shards - 1)
 
     def do_item(item, carry):
@@ -712,17 +745,34 @@
 
         @pl.when(block == 0)
         def _():
-            line.wait_slot(q, spread, arrived)
-            for round_id in range(early, shards - 2):
+            far = jnp.abs(q - z)
+
+            @pl.when(far == 0)
+            def _():
+                for copy in own_loads:
+                    copy.wait()
+
+            @pl.when(far == 2)
+            def _():
+                line.wait_slot(q, spread, arrived, EARLY_PIECES)
+
+            @pl.when((far == 1) | (far > 2))
+            def _():
+                line.wait_slot(q, spread, arrived)
+
+            for distance in range(3, shards - 1):
                 for way in range(2):
                     forward = 1 - 2 * way
 
-                    @pl.when((q == z - forward * (round_id + 1)) & line.sends(way, round_id + 1))
+                    @pl.when((q == z - forward * distance) & line.sends(way, distance))
                     def _():
-                        for copy in line.hop(
-                            way, round_id + 1, spread, spread, weight_send, arrived
-                        ):
+                        for copy in line.hop(way, distance, spread, spread, weight_send, arrived):
                             copy.start()
+
+        @pl.when(item == late_item)
+        def _():
+            line.receive(1, spread, arrived, LATE_PIECES)
+            line.push(2, spread, spread, weight_send, arrived, LATE_PIECES)
 
         @pl.when((step == shards - 2) & (block > 0))
         def _():
@@ -805,6 +855,38 @@
 
     lax.fori_loop(0, shards * blocks, do_item, 0)
     back_start(block_first(blocks - 1))
+
+    def early_far(k, piece):
+        _, low, size = far_pieces[piece]
+        cut = pl.ds(low, size)
+        return pltpu.make_async_remote_copy(
+            src_ref=part_in_ref.at[(shards - 1) * k, cut],
+            dst_ref=far_land.at[k, cut],
+            send_sem=far_send.at[piece],
+            recv_sem=far_recv.at[piece],
+            device_id={"dp": z + 2 * k - 1},
+            device_id_type=MESH,
+        )
+
+    def early_add(k, piece):
+        _, low, size = far_pieces[piece]
+        cut = pl.ds(low, size)
+        view = far_land.at[k, cut]
+        pltpu.make_async_copy(view, view, far_recv.at[piece]).wait()
+        part_in_ref[(shards - 1) * k, cut] = (
+            part_in_ref[(shards - 1) * k, cut].astype(F32) + far_land[k, cut].astype(F32)
+        ).astype(BF)
+
+    for piece in range(EARLY_FAR):
+
+        @pl.when(z == 0)
+        def _():
+            early_far(1, piece).start()
+
+        @pl.when(z == shards - 1)
+        def _():
+            early_far(0, piece).start()
+
     finals = [
         pltpu.make_async_copy(part_in_ref.at[0], far_in_ref.at[0], final_sem.at[0]),
         pltpu.make_async_copy(part_out_ref.at[0], far_out_ref.at[0], final_sem.at[1]),
@@ -813,9 +895,6 @@
         pltpu.make_async_copy(part_in_ref.at[z], sum_in_ref, final_sem.at[4]),
         pltpu.make_async_copy(part_out_ref.at[z], sum_out_ref, final_sem.at[5]),
     ]
-    for copy in finals[:4]:
-        copy.start()
-
     def do_forward(turn, carry):
         up = turn
         down = shards - 1 - turn
@@ -843,6 +922,18 @@
 
     for copy in finals[4:]:
         copy.start()
+    for piece in range(EARLY_FAR):
+
+        @pl.when(z == 1)
+        def _():
+            early_add(1, piece)
+
+        @pl.when(z == shards - 2)
+        def _():
+            early_add(0, piece)
+
+    for copy in finals[:4]:
+        copy.start()
 
     def finish_sum(q, carry):
         @pl.when((q > z) & line.has_above)
@@ -858,8 +949,19 @@
         return carry
 
     lax.fori_loop(1, shards - 1, finish_sum, 0)
-    for round_id in range(early, shards - 1):
-        line.drain(round_id, own, spread, weight_send, arrived)
+    line.drain(1, spread, spread, weight_send, arrived, LATE_PIECES)
+    for round_id in range(2, shards - 1):
+        line.drain(round_id, spread, spread, weight_send, arrived)
+    for piece in range(EARLY_FAR):
+
+        @pl.when(z == 0)
+        def _():
+            early_far(1, piece).wait_send()
+
+        @pl.when(z == shards - 1)
+        def _():
+            early_far(0, piece).wait_send()
+
     for k in range(groups):
         source = lax.rem(me + k, groups)
         if k:
@@ -875,6 +977,7 @@
     shards, tall, span = spread_in.shape
     total = groups * batches * cap_pad
     count = len(pieces_of(tall, span))
+    early_rows = sum(pieces_of(tall, span, FAR_CUTS)[EARLY_FAR - 1][1:])
     anywhere = pl.BlockSpec(memory_space=pl.ANY)
     return pl.pallas_call(
         functools.partial(moe_kernel, shards, groups),
@@ -899,9 +1002,13 @@
             pltpu.VMEM((shards, span, width), BF),
             pltpu.VMEM((shards - 1, tall, span), BF),
             pltpu.VMEM((shards - 1, span, width), BF),
+            pltpu.VMEM((2, early_rows, span), BF),
             pltpu.SemaphoreType.DMA((groups,)),
-            pltpu.SemaphoreType.DMA((2, shards, 2)),
-            pltpu.SemaphoreType.DMA((shards, 2)),
+            pltpu.SemaphoreType.DMA((3,)),
+            pltpu.SemaphoreType.DMA((EARLY_FAR,)),
+            pltpu.SemaphoreType.DMA((EARLY_FAR,)),
+            pltpu.SemaphoreType.DMA((2, shards, 4)),
+            pltpu.SemaphoreType.DMA((shards, 4)),
             pltpu.SemaphoreType.DMA((2, shards, count)),
             pltpu.SemaphoreType.DMA((shards - 1, count)),
             pltpu.SemaphoreType.DMA((groups,)),
@@ -1116,10 +1223,10 @@
 def reduce_kernel(
     experts,
     shards,
-    cols_ref,
     slot_cols_ref,
     lse_ref,
     probs_ref,
+    vectors_ref,
     x_hbm,
     grad_hbm,
     weight_hbm,
@@ -1147,7 +1254,7 @@
     hidden_ref,
     one_ref,
     two_ref,
-    small_ref,
+    raw_ref,
     sums_ref,
     one_flip,
     d_qkv_ref,
@@ -1218,22 +1325,14 @@
         )
     ]
 
-    @pl.when((z == 0) | (z == shards - 1))
-    def _():
-        for copy in far_loads:
-            copy.start()
-
+    for copy in far_loads:
+        copy.start()
     for kind in range(3):
         loads(kind, 0).start()
     weight_load.start()
     for image in range(1, batches):
         for kind in range(3):
             loads(kind, image).start()
-    @pl.when((z > 0) & (z < shards - 1))
-    def _():
-        for copy in far_loads:
-            copy.start()
-
     for kind in range(3, 8):
         for image in range(batches):
             loads(kind, image).start()
@@ -1286,7 +1385,13 @@
         ).astype(BF)
 
     def far_forward(k, piece):
-        far_take(k, piece)
+        if piece < EARLY_FAR:
+            @pl.when(z != (1 if k else shards - 2))
+            def _():
+                far_take(k, piece)
+
+        else:
+            far_take(k, piece)
         far_copy(k, piece).start()
 
     def pass_on(first, piece):
@@ -1298,18 +1403,17 @@
         def _():
             far_forward(0 if first else 1, piece)
 
+    for copy in far_loads:
+        copy.wait()
+
     @pl.when(z == 0)
     def _():
-        for copy in far_loads:
-            copy.wait()
-        for piece in range(len(pieces)):
+        for piece in range(EARLY_FAR, len(pieces)):
             far_copy(1, piece).start()
 
     @pl.when(z == shards - 1)
     def _():
-        for copy in far_loads:
-            copy.wait()
-        for piece in range(len(pieces)):
+        for piece in range(EARLY_FAR, len(pieces)):
             far_copy(0, piece).start()
 
     def near_copy(tile):
@@ -1322,11 +1426,13 @@
         )
 
     def plane_copy(tile):
+        owner = lax.rem(tile, PLANE) // 2
+        place = lax.rem(chip - owner + 2 * chips - 1, chips)
         return remote(
             tiles_ref.at[tile],
-            plane_land.at[tile // PLANE, chip],
+            plane_land.at[tile // PLANE, place],
             plane_send.at[tile],
-            plane_recv.at[tile // PLANE, chip],
+            plane_recv.at[tile // PLANE, place],
             {"expert": lax.rem(tile, PLANE)},
         )
 
@@ -1369,9 +1475,8 @@
     def plane_sum(k):
         total = tiles_ref[me + PLANE * k].astype(F32)
         for j in range(1, chips):
-            far = lax.rem(chip + j, chips)
-            landed(plane_land.at[k, far], plane_recv.at[k, far])
-            total = total + plane_land[k, far].astype(F32)
+            landed(plane_land.at[k, j - 1], plane_recv.at[k, j - 1])
+            total = total + plane_land[k, j - 1].astype(F32)
         plane_ref[k] = total.astype(BF)
         for j in range(1, shards):
             line_copy(k, lax.rem(z + j, shards)).start()
@@ -1387,11 +1492,17 @@
         for j in range(1, PLANE):
             final_copy(k, lax.rem(me + j, PLANE)).start()
 
+    pass_on(True, 0)
+    pass_on(True, 1)
+
     lane = lax.broadcasted_iota(jnp.int32, (1, 128), 1)
     groups, _, _, cap_pad, _ = back_ref.shape
     slots = groups * cap_pad
     slot = lax.broadcasted_iota(jnp.int32, (1, slots), 1)
     sums_ref[...] = jnp.zeros_like(sums_ref)
+    small_rows = vectors_ref[:8].astype(F32)
+    gain_one = small_rows[0:1]
+    gain_two = small_rows[2:3]
 
     def phase_one(image, carry):
         here = pl.ds(pl.multiple_of(image * rows, rows), rows)
@@ -1402,7 +1513,6 @@
         @pl.when(image == 0)
         def _():
             weight_load.wait()
-            small_ref[...] = weight_ref[:, 4 * width :].astype(F32).T
 
         out_grad = grad_ref[image]
         hidden = hidden_ref[image]
@@ -1415,7 +1525,7 @@
         for j in range(2):
             pick = (slot == slot_cols_ref[image, :, j : j + 1]).astype(F32)
             both = pick if both is None else both + pick
-            chosen = lane - 4 == cols_ref[image, :, j : j + 1]
+            chosen = lane - 4 == slot_cols_ref[image, :, 2 + j : 3 + j]
             gate = jnp.sum(jnp.where(chosen, probs, 0.0), axis=-1, keepdims=True)
             picked = dot(pick.astype(BF), answers)
             result = result + gate * picked
@@ -1424,11 +1534,11 @@
         d_logits = probs * (d_probs - jnp.sum(d_probs * probs, axis=-1, keepdims=True))
         d_logits = d_logits.astype(BF)
         d_logits_ref[here, :] = d_logits
-        d_two = dot(both.astype(BF), answer_grads) + dot_nt(d_logits, weight_ref[:, 4 * width :])
+        d_two = dot(both.astype(BF), answer_grads) + dot(d_logits, vectors_ref[...])
         hat, inverse = norm_stats(hidden)
         sums_ref[2:3, :] += jnp.sum(d_two * hat, axis=0, keepdims=True)
         sums_ref[3:4, :] += jnp.sum(d_two, axis=0, keepdims=True)
-        d_hat = d_two * small_ref[2:3, :]
+        d_hat = d_two * gain_two
         d_hidden = out_grad + inverse * (
             d_hat
             - jnp.mean(d_hat, axis=-1, keepdims=True)
@@ -1439,17 +1549,16 @@
         d_mixed_ref[here, :] = dot_nt(d_branch, weight_ref[:, 3 * width : 4 * width]).astype(BF)
         grad_ref[image] = d_hidden
         hidden_ref[image] = result
-        pltpu.make_async_copy(hidden_ref.at[image], out_hbm.at[image], store_sem.at[0, image]).start()
         return carry
 
     lax.fori_loop(0, batches, phase_one, 0)
-
-    @pl.when(inner)
-    def _():
-        for copy in far_loads:
-            copy.wait()
-
-    pass_on(True, 0)
+    for image in range(batches):
+        raw_ref[image * SEQ : (image + 1) * SEQ] = hidden_ref[image, :SEQ]
+    out_store = pltpu.make_async_copy(raw_ref, out_hbm, store_sem.at[0, 0])
+    out_store.start()
+    pass_on(True, 2)
+    pass_on(True, 3)
+    pass_on(False, 0)
     for kind, view in ((3, mixed_ref), (4, two_ref), (5, one_ref)):
         for image in range(batches):
             landed(view.at[pl.ds(image * rows, rows)], load_sem.at[kind, image])
@@ -1462,6 +1571,8 @@
     flipped = dot_tn(d_logits_ref[...], two_ref[...])
     for image in range(batches):
         landed(qkv_ref.at[pl.ds(image * rows, rows)], load_sem.at[6, image])
+
+    pass_on(False, 1)
 
     key_ok = lax.broadcasted_iota(jnp.int32, (1, rows), 1) < SEQ
     scale = HEAD ** (-0.5)
@@ -1545,24 +1656,27 @@
         hat, inverse = norm_stats(x_ref[image])
         sums_ref[0:1, :] += jnp.sum(d_one * hat, axis=0, keepdims=True)
         sums_ref[1:2, :] += jnp.sum(d_one, axis=0, keepdims=True)
-        d_hat = d_one * small_ref[0:1, :]
+        d_hat = d_one * gain_one
         x_ref[image] = grad_ref[image] + inverse * (
             d_hat
             - jnp.mean(d_hat, axis=-1, keepdims=True)
             - hat * jnp.mean(d_hat * hat, axis=-1, keepdims=True)
         )
-        pltpu.make_async_copy(x_ref.at[image], dx_hbm.at[image], store_sem.at[1, image]).start()
 
         @pl.when(image == batches // 2 - 1)
         def _():
-            pass_on(True, 7)
-            pass_on(False, 5)
+            pass_on(False, 6)
             line_sum(1)
             plane_sum(2)
 
         return carry
 
     lax.fori_loop(0, batches, phase_three, 0)
+    out_store.wait()
+    for image in range(batches):
+        raw_ref[image * SEQ : (image + 1) * SEQ] = x_ref[image, :SEQ]
+    dx_store = pltpu.make_async_copy(raw_ref, dx_hbm, store_sem.at[1, 0])
+    dx_store.start()
 
     def small_copy(k):
         peer = lax.rem(me + k, PLANE)
@@ -1583,7 +1697,7 @@
     sums_ref[...] += flipped[: sums_ref.shape[0]]
     for k in range(1, PLANE):
         small_copy(k).start()
-    pass_on(False, 6)
+    pass_on(False, 7)
     line_sum(2)
     total = sums_ref[...]
     for k in range(1, PLANE):
@@ -1598,7 +1712,6 @@
         landed(small_far.at[peer], small_recv.at[PLANE + peer])
         total = total + small_far[peer]
     small_grad_ref[...] = total
-    pass_on(False, 7)
 
     def finish(tile, carry):
         @pl.when(lax.rem(tile, PLANE) != me)
@@ -1650,24 +1763,23 @@
         copy.start()
     for piece in range(len(pieces)):
 
-        @pl.when(z < shards - 1)
+        first = 1 if piece < EARLY_FAR else 0
+
+        @pl.when((z < shards - 1) & (z >= first))
         def _():
             far_copy(1, piece).wait_send()
 
-        @pl.when(z > 0)
+        @pl.when((z > 0) & (z < shards - first))
         def _():
             far_copy(0, piece).wait_send()
 
     for copy in ends:
         copy.wait()
-    for image in range(batches):
-        pltpu.make_async_copy(hidden_ref.at[image], out_hbm.at[image], store_sem.at[0, image]).wait()
-        pltpu.make_async_copy(x_ref.at[image], dx_hbm.at[image], store_sem.at[1, image]).wait()
-
-
-def run_reduce(x, grad, weight, cols, slot_cols, back, saved, far, experts):
+    dx_store.wait()
+
+
+def run_reduce(x, grad, weight, vectors, slot_cols, back, saved, far, experts):
     batches, rows, width = x.shape
-    total = weight.shape[1]
     shards = lax.axis_size("dp")
     qkv, mixed, lse, hidden, one, two, probs = saved
     depth = width // shards
@@ -1681,8 +1793,8 @@
     return pl.pallas_call(
         functools.partial(reduce_kernel, experts, shards),
         out_shape=(
-            jax.ShapeDtypeStruct(x.shape, F32),
-            jax.ShapeDtypeStruct(x.shape, F32),
+            jax.ShapeDtypeStruct((batches * SEQ, width), F32),
+            jax.ShapeDtypeStruct((batches * SEQ, width), F32),
             jax.ShapeDtypeStruct(far[0].shape[1:], BF),
             jax.ShapeDtypeStruct(far[1].shape[1:], BF),
             jax.ShapeDtypeStruct((depth, 3 * width), F32),
@@ -1701,7 +1813,7 @@
             pltpu.VMEM(x.shape, F32),
             pltpu.VMEM((batches * rows, width), BF),
             pltpu.VMEM((batches * rows, width), BF),
-            pltpu.VMEM((SMALL, width), F32),
+            pltpu.VMEM((batches * SEQ, width), F32),
             pltpu.VMEM((small_rows, width), F32),
             pltpu.VMEM((width, batches * rows), BF),
             pltpu.VMEM((batches * rows, 3 * width), BF),
@@ -1710,7 +1822,7 @@
             pltpu.VMEM((batches * rows, SMALL), BF),
             pltpu.VMEM((tiles, width, TILE), BF),
             pltpu.VMEM((tiles // 2, width, TILE), BF),
-            pltpu.VMEM((own_tiles, PLANE // 2, width, TILE), BF),
+            pltpu.VMEM((own_tiles, PLANE // 2 - 1, width, TILE), BF),
             pltpu.VMEM((own_tiles, width, TILE), BF),
             pltpu.VMEM((own_tiles, shards, depth, TILE), BF),
             pltpu.VMEM((tiles, depth, TILE), BF),
@@ -1725,7 +1837,7 @@
             dma((tiles,)),
             dma((tiles,)),
             dma((tiles,)),
-            dma((own_tiles, PLANE // 2)),
+            dma((own_tiles, PLANE // 2 - 1)),
             dma((own_tiles, shards)),
             dma((own_tiles, shards)),
             dma((own_tiles, PLANE)),
@@ -1743,7 +1855,7 @@
             flops=16000000000, bytes_accessed=50000000, transcendentals=2000000
         ),
         name="tail",
-    )(cols, slot_cols, lse, probs, x, grad, weight, back, qkv, mixed, hidden, one, two, *far)
+    )(slot_cols, lse, probs, vectors, x, grad, weight, back, qkv, mixed, hidden, one, two, *far)
 
 
 def last_turn(far_in, far_out):
@@ -1777,16 +1889,18 @@
     depth = qkv_weight.shape[0]
     both = ("dp", "expert")
 
-    vectors = jnp.stack([gain_one, shift_one, gain_two, shift_two], axis=1)
-    small = jnp.concatenate([vectors, router_weight], axis=1)
-    small = jnp.pad(small, ((0, 0), (0, SMALL - small.shape[1])))
+    used, wide = 4 + experts, gain_one.shape[0]
+    small = jnp.concatenate(
+        [gain_one, shift_one, gain_two, shift_two, router_weight.T.reshape(-1)]
+    ).reshape(used, wide)
+    small = jnp.pad(small, ((0, ceil_to(used, 16) - used), (0, ceil_to(wide, 128) - wide)))
     dense = (qkv_weight, proj_weight, small)
     own = (expert_in[0], jnp.pad(expert_bias, ((0, BIAS_ROWS - 1), (0, 0))), expert_out[0])
     cols = jnp.concatenate([routes, priority.reshape(batches * SEQ, 2)], axis=1)
     cols = cols.reshape(batches, SEQ, 4)
     cols = jnp.pad(cols, ((0, 0), (0, SEQ_PAD - SEQ), (0, 0)), constant_values=-1)
     rows_first = jnp.swapaxes(cols, 1, 2)
-    received, x, grad, weight, qkv, mixed, hidden, one, two, lse, probs, slot_cols, *spread = run_front(
+    received, x, grad, weight, qkv, mixed, hidden, one, two, lse, probs, slot_cols, rows_small, *spread = run_front(
         inputs, out_grad, dense, own, cols, rows_first, capacity, experts, cap_pad
     )
     saved = (qkv, mixed, lse, hidden, one, two, probs)
@@ -1796,7 +1910,7 @@
     spot = 4 * width
     if groups == PLANE:
         outputs, inputs_grad, end_in, end_out, qkv_grad, proj_grad, small_grad = run_reduce(
-            x, grad, weight, cols, slot_cols, back, saved, (far_in, far_out), experts
+            x, grad, weight, rows_small, slot_cols, back, saved, (far_in, far_out), experts
         )
         small_grad = lax.dynamic_slice_in_dim(
             small_grad, lax.axis_index("dp") * depth, depth, axis=1
@@ -1804,21 +1918,26 @@
         vectors = [small_grad[k] for k in range(4)]
         router_grad = small_grad[4 : 4 + experts].T
     else:
+        weight = jnp.concatenate([weight, rows_small.T], axis=1)
         outputs, inputs_grad, dense = run_tail(
             x, grad, weight, cols, slot_cols, back, saved, experts
         )
         end_in, end_out = last_turn(far_in, far_out)
+        outputs, inputs_grad = (
+            full[:, :SEQ].reshape(batches * SEQ, width) for full in (outputs, inputs_grad)
+        )
         dense = lax.psum_scatter(dense, both, scatter_dimension=0, tiled=True)
         dense = lax.all_gather(dense, "expert", axis=0, tiled=True).astype(F32)
         qkv_grad = dense[:, : 3 * width]
         proj_grad = dense[:, 3 * width : spot]
         vectors = [dense[:, spot + k] for k in range(4)]
         router_grad = dense[:, spot + 4 : spot + 4 + experts]
-    grad_in = jnp.where(at_end, end_in, sum_in).astype(F32)
+    grad_in = jnp.where(at_end, end_in[:width], sum_in[:width]).astype(F32)
+    grad_bias = jnp.where(at_end, end_in[width], sum_in[width]).astype(F32)
     grad_out = jnp.where(at_end, end_out, sum_out).astype(F32)
     return (
-        outputs[:, :SEQ].reshape(batches * SEQ, width),
-        inputs_grad[:, :SEQ].reshape(batches * SEQ, width),
+        outputs,
+        inputs_grad,
         vectors[0],
         vectors[1],
         qkv_grad,
@@ -1826,8 +1945,8 @@
         vectors[2],
         vectors[3],
         router_grad,
-        grad_in[None, :width],
-        grad_in[None, width],
+        grad_in[None],
+        grad_bias[None],
         grad_out[None],
     )
 

time: 403 us -> 388 us (0.963)
  Pallas kernels: 379 us -> 360 us
    pallas_call x1, Pallas kernels: 120 us -> 99.1 us  [run_reduce(): pl.pallas_call(functools.partial(reduce_kernel, experts, shards), out_sha...]
    pallas_call x1, Pallas kernels: 127 us -> 145 us  [run_moe(): pl.pallas_call(functools.partial(moe_kernel, shards, groups), out_shape=(...]
    pallas_call x1, Pallas kernels: 132 us -> 116 us  [run_front(): pl.pallas_call(functools.partial(front_kernel, experts, shards), out_shap...]
where the time goes in v6:
time: 388 us; the launch traced here: 386 us
  Pallas kernels  360 us (93%)
  local copies, waits for them, and re-layouts  19.1 us (5%)
  other arithmetic  5.94 us (2%)
    pallas_call x1, Pallas kernels, run_moe(): pl.pallas_call(functools.partial(moe_kernel, shards, groups), out_shape=(...  145 us
    pallas_call x1, Pallas kernels, run_front(): pl.pallas_call(functools.partial(front_kernel, experts, shards), out_shap...  116 us
    pallas_call x1, Pallas kernels, run_reduce(): pl.pallas_call(functools.partial(reduce_kernel, experts, shards), out_sha...  99.1 us

profile of v6, /device:TPU:0, one launch (start us, length us, event | category | flops | bytes accessed | tf_op | source)
XLA Modules:
  0.0 386.1 jit_solution(7904430085173856679)
XLA Ops:
  0.6 0.9 concatenate.12
  1.5 0.2 copy.29
  1.7 0.8 concatenate.11
  2.6 0.2 copy.31
  2.8 0.8 pad.12.clone.cols_ref
  3.5 0.6 pad_bitcast_fusion.rows_ref
  4.2 1.3 pad.14.own_bias
  5.5 0.8 reshape.35
  6.2 2.8 concatenate.14
  9.0 0.1 reshape.36
  9.1 0.6 pad.13.small_own
  9.7 116.0 %front.1 = (bf16[8,4,2,64,768]{4,3,2,1,0:T(8,128)(2,1)}, f32[4,208,768]{2,1,0:T(8,128)}, f32[4,208,768]{2,1,0:T(8,128)}, bf16[768,3072]{1,0:T(8,128)(2,1)}, bf16...) custom-call(s32[4]{0:T(128)} %limit_ref.1, ...), custom_call_target="tpu_custom_call" | custom-call | flops 8000000000 | bytes 40000000 | tf_op jit(solution)/shard_map/front/pallas_call | solution.py:503
  125.7 145.1 %moe.1 = (bf16[8,4,2,64,768]{4,3,2,1,0:T(8,128)(2,1)}, bf16[784,768]{1,0:T(8,128)(2,1)}, bf16[768,768]{1,0:T(8,128)(2,1)}, bf16[2,784,768]{2,1,0:T(8,128)(2,1)}, bf16[2,768,768]{2,1,0:T(8,128)(2,1)}) custom-call(bf16[8,4,2,64,768]{4,3,2,1,0:T(8,128)(2,1)} %get-tuple-element.46.x_hbm, bf16[768,768]{1,0:T(8,128)(2,1)} %bitcast.25, ...), custom_call_target="tpu_custom_call" | custom-call | flops 57982058496 | bytes 60000000 | tf_op jit(solution)/shard_map/moe/pallas_call | solution.py:982
  270.9 99.1 %tail.1 = (f32[788,768]{1,0:T(8,128)}, f32[788,768]{1,0:T(8,128)}, bf16[784,768]{1,0:T(8,128)(2,1)}, bf16[768,768]{1,0:T(8,128)(2,1)}, f32[192,2304]{1,0:T(8,128...) custom-call(s32[4,208,8]{2,1,0:T(8,128)} %get-tuple-element.39.slot_cols_ref, f32[4,208,128]{2,1,0:T(8,128)} %get-tuple-element.40.lse_ref, ...), custom_call_target="tpu_custom_call" | custom-call | flops 16000000000 | bytes 50000000 | tf_op jit(solution)/shard_map/tail/pallas_call | solution.py:1793
  370.0 1.3 fusion
  371.3 0.0 copy-start.1
  371.3 4.6 %bitcast_convert_fusion = (f32[1,768,768]{2,1,0:T(8,128)}, f32[1,768,768]{2,1,0:T(8,128)}) fusion(bf16[768,768]{1,0:T(8,128)(2,1)} %get-tuple-element.64, bf16[768,768]{1,0:T(8,128)(2,1)} %get-tuple-element.65, pred[]{:T(512)S(6)} %or.3, bf16[784,768]{1,0:T(8,128)(2,1)} %get-tuple-element.63, bf16[784,768]{1,0:T(8,128)(2,1)} %get-tuple-element.62), kind=kLoop, calls=%fused_computation | loop fusion | flops 2359296 | bytes 9437185 | tf_op jit(solution)/shard_map/broadcast_in_dim | solution.py:1950
  376.0 1.4 dynamic-slice_bitcast_fusion
  377.4 1.5 fusion.1
  378.9 0.0 copy-done.1
  378.9 0.0 copy-start
  378.9 1.4 copy.36
  380.3 1.1 copy-done
  381.4 0.0 copy-start.2
  381.4 1.4 copy.37
  382.9 0.9 copy-done.2
  383.8 0.0 copy-start.3
  383.8 1.2 copy.38
  385.0 0.3 copy-done.3
  385.3 0.8 copy.39
  (2 shorter events, 0.0 us)
Async XLA Ops:
  371.3 7.5 %copy-start.1 = (f32[788,768]{1,0:T(8,128)S(1)}, f32[788,768]{1,0:T(8,128)}, u32[]{:S(2)}) copy-start(f32[788,768]{1,0:T(8,128)} %get-tuple-element.84) | copy-start | bytes 7262212
  378.9 2.6 copy-start
  381.4 2.4 copy-start.2
  383.8 1.5 copy-start.3

commit v7 on v6

--- a/solution.py
+++ b/solution.py
@@ -16,19 +16,20 @@
 F32 = jnp.float32
 SMALL = 128
 MESH = pl.DeviceIdType.MESH
-EARLY_PIECES = range(3)
-LATE_PIECES = range(3, 4)
+EARLY_PIECES = range(2)
+LATE_PIECES = range(2, 4)
 EARLY_FAR = 2
 FAR_CUTS = 4
 FAR_TURNS = (
-    (0, True, 4),
-    (0, False, 2),
-    (1, True, 5),
-    (1, False, 3),
-    (3, True, 6),
-    (3, False, 4),
-    (4, True, 7),
-    (4, False, 5),
+    (0, True, 3),
+    (1, True, 4),
+    (1, False, 2),
+    (2, True, 5),
+    (3, False, 3),
+    (4, True, 6),
+    (4, False, 4),
+    (5, True, 7),
+    (5, False, 5),
 )
 TILE = 128
 PLANE = 8
@@ -192,11 +193,12 @@
     raw_grad_hbm,
     qkv_own,
     proj_own,
-    small_own,
+    small_own_ref,
     own_body,
     own_bias,
     own_out,
     received_ref,
+    last_hbm,
     x_hbm,
     grad_hbm,
     weight_hbm,
@@ -286,12 +288,14 @@
         pltpu.make_async_copy(
             proj_own, weight_ref.at[rows_of(z), pl.ds(3 * width, width)], load_sem.at[3]
         ),
-        pltpu.make_async_copy(small_own, small_land.at[z], load_sem.at[4]),
     ]
     for copy in mine:
         copy.start()
     for copy in raws:
         copy.start()
+    small_land[z, :, :depth] = (
+        small_own_ref[...].astype(F32).T[: small_land.shape[1]].astype(BF)
+    )
     line.greet(me, groups)
     for copy in mine:
         copy.wait()
@@ -380,6 +384,8 @@
             {"expert": target},
         )
 
+    last = batches - 1
+    last_store = pltpu.make_async_copy(send_ref.at[last], last_hbm, load_sem.at[4])
     saves = (
         (qkv_ref, qkv_hbm),
         (mixed_ref, mixed_hbm),
@@ -445,11 +451,19 @@
         sent = dot(both.astype(BF), two).astype(BF)
         send_ref[index, :, 0] = sent.reshape(groups, cap_pad, width)
         send_ref[index, :, 1] = grads.astype(BF).reshape(groups, cap_pad, width)
-        for k in range(1, groups):
-            rows_copy(index, lax.rem(me + k, groups)).start()
-        pltpu.make_async_copy(
-            send_ref.at[index, me], received_ref.at[me, index], rows_recv.at[me, index]
-        ).start()
+
+        @pl.when(index < last)
+        def _():
+            for k in range(1, groups):
+                rows_copy(index, lax.rem(me + k, groups)).start()
+            pltpu.make_async_copy(
+                send_ref.at[index, me], received_ref.at[me, index], rows_recv.at[me, index]
+            ).start()
+
+        @pl.when(index == last)
+        def _():
+            last_store.start()
+
         for k, (here, there) in enumerate(saves):
             pltpu.make_async_copy(here.at[index], there.at[index], store_sem.at[2 + k, index]).start()
         return carry
@@ -460,11 +474,14 @@
     line.push(1, spread, spread, send_sem, arrived, EARLY_PIECES)
 
     def finish(image, carry):
-        for k in range(groups):
-            source = lax.rem(me + k, groups)
-            if k:
-                rows_copy(image, source).wait_send()
-            landed(received_ref.at[source, image], rows_recv.at[source, image])
+        @pl.when(image < last)
+        def _():
+            for k in range(groups):
+                source = lax.rem(me + k, groups)
+                if k:
+                    rows_copy(image, source).wait_send()
+                landed(received_ref.at[source, image], rows_recv.at[source, image])
+
         pltpu.make_async_copy(x_ref.at[image], x_hbm.at[image], store_sem.at[0, image]).wait()
         pltpu.make_async_copy(grad_ref.at[image], grad_hbm.at[image], store_sem.at[1, image]).wait()
         for k, (here, there) in enumerate(saves):
@@ -473,6 +490,7 @@
 
     lax.fori_loop(0, batches, finish, 0)
     weight_store.wait()
+    last_store.wait()
     for far in peers:
         line_copy(far).wait_send()
         small_copy(far).wait_send()
@@ -504,6 +522,7 @@
         functools.partial(front_kernel, experts, shards),
         out_shape=(
             jax.ShapeDtypeStruct((groups, batches, 2, cap_pad, width), BF),
+            jax.ShapeDtypeStruct((groups, 2, cap_pad, width), BF),
             shape(width, dtype=F32),
             shape(width, dtype=F32),
             jax.ShapeDtypeStruct((width, 4 * width), BF),
@@ -519,8 +538,11 @@
             jax.ShapeDtypeStruct((shards, tall, body.shape[1]), BF),
             jax.ShapeDtypeStruct((shards,) + out.shape, BF),
         ),
-        in_specs=[pl.BlockSpec(memory_space=pltpu.SMEM), inside, inside] + [anywhere] * 8,
-        out_specs=(anywhere,) * 9 + (inside,) * 4 + (anywhere,) * 2,
+        in_specs=[pl.BlockSpec(memory_space=pltpu.SMEM), inside, inside]
+        + [anywhere] * 4
+        + [inside]
+        + [anywhere] * 3,
+        out_specs=(anywhere,) * 10 + (inside,) * 4 + (anywhere,) * 2,
         scratch_shapes=[
             pltpu.VMEM(raw.shape, F32),
             pltpu.VMEM(raw.shape, F32),
@@ -532,7 +554,7 @@
             pltpu.VMEM((batches, rows, width), F32),
             pltpu.VMEM((batches, rows, width), BF),
             pltpu.VMEM((batches, rows, width), BF),
-            pltpu.VMEM((shards,) + dense[2].shape, BF),
+            pltpu.VMEM((shards, ceil_to(4 + experts, 16), ceil_to(dense[2].shape[0], 128)), BF),
             pltpu.VMEM((batches, 8, rows), jnp.int32),
             pltpu.VMEM((batches, groups, 2, cap_pad, width), BF),
             dma((6,)),
@@ -571,6 +593,7 @@
     shards,
     groups,
     x_hbm,
+    last_hbm,
     own_body,
     own_bias,
     own_out,
@@ -594,6 +617,8 @@
     land_out_ref,
     far_land,
     rows_sem,
+    last_send,
+    last_recv,
     own_sem,
     far_send,
     far_recv,
@@ -610,11 +635,9 @@
     me = lax.axis_index("expert")
     _, batches, _, cap_pad, width = rows_ref.shape
     _, tall, span = spread_in_ref.shape
-    group = max(1, 512 // (batches * cap_pad))
-    while groups % group:
-        group -= 1
-    blocks = groups // group
-    rows = group * batches * cap_pad
+    blocks = batches
+    rows = groups * cap_pad
+    last = batches - 1
     spread = (win_ref, wout_ref)
     early_spread = (spread_in_ref, spread_out_ref)
     own = (own_body, own_bias, own_out)
@@ -623,9 +646,9 @@
     pieces = pieces_of(tall, span)
     far_pieces = pieces_of(tall, span, FAR_CUTS)
 
-    for k in range(groups):
-        source = lax.rem(me + k, groups)
-        pltpu.make_async_copy(x_hbm.at[source], rows_ref.at[source], rows_sem.at[source]).start()
+    for image in range(last):
+        pltpu.make_async_copy(x_hbm.at[:, image], rows_ref.at[:, image], rows_sem.at[image]).start()
+    pltpu.make_async_copy(last_hbm.at[me], rows_ref.at[me, last], last_recv.at[me]).start()
     own_places = (
         (own_body, win_ref.at[z, pl.ds(0, width)], 0),
         (own_bias, win_ref.at[z, pl.ds(width, tall - width)], 1),
@@ -654,6 +677,19 @@
         copy.start()
 
     line.greet(me, groups)
+
+    def last_copy(target):
+        return pltpu.make_async_remote_copy(
+            src_ref=last_hbm.at[target],
+            dst_ref=rows_ref.at[me, last],
+            send_sem=last_send.at[target],
+            recv_sem=last_recv.at[me],
+            device_id={"expert": target},
+            device_id_type=MESH,
+        )
+
+    for k in range(1, groups):
+        last_copy(lax.rem(me + k, groups)).start()
     line.push(1, early_spread, spread, weight_send, arrived, LATE_PIECES)
     line.push(2, early_spread, spread, weight_send, arrived, EARLY_PIECES)
 
@@ -697,42 +733,25 @@
             parts[kind][q, cut].astype(F32) + lands[kind][slot, cut].astype(F32)
         ).astype(BF)
 
-    def back_copy(source):
+    def back_copy(target, image):
         return pltpu.make_async_remote_copy(
-            src_ref=rows_ref.at[source],
-            dst_ref=back_ref.at[me],
-            send_sem=back_send.at[source],
-            recv_sem=back_recv.at[me],
-            device_id={"expert": source},
+            src_ref=rows_ref.at[target, image],
+            dst_ref=back_ref.at[me, image],
+            send_sem=back_send.at[target, image],
+            recv_sem=back_recv.at[me, image],
+            device_id={"expert": target},
             device_id_type=MESH,
         )
 
-    def back_start(first):
-        for k in range(group):
-            source = first + k
-
-            @pl.when(source != me)
-            def _():
-                back_copy(source).start()
-
-            @pl.when(source == me)
-            def _():
-                pltpu.make_async_copy(
-                    rows_ref.at[source], back_ref.at[source], back_recv.at[source]
-                ).start()
-
-    def block_first(block):
-        lead = me // group
-        if blocks == 4:
-            order = (3 - lead, lead + 1 - 2 * lax.rem(lead, 2), lax.rem(lead + 2, 4), lead)
-            picked = 0
-            for k in range(4):
-                picked = picked + jnp.where(block == k, order[k], 0)
-            return picked * group
-        return lax.rem(lead + 1 + block, blocks) * group
+    def back_start(image):
+        for k in range(1, groups):
+            back_copy(lax.rem(me + k, groups), image).start()
+        pltpu.make_async_copy(
+            rows_ref.at[me, image], back_ref.at[me, image], back_recv.at[me, image]
+        ).start()
 
     plain = (shards - 2) * blocks
-    late_item = max(1, blocks - 1)
+    late_item = blocks
     inner = (z > 0) & (z < shards - 1)
 
     def do_item(item, carry):
@@ -776,21 +795,23 @@
 
         @pl.when((step == shards - 2) & (block > 0))
         def _():
-            back_start(block_first(block - 1))
-
-        lead = block_first(block)
-        low = pl.multiple_of(lead * (batches * cap_pad), rows)
-        here = pl.ds(low, rows)
-        mine = pl.ds(lead, group)
-
-        @pl.when(step == 0)
-        def _():
-            for k in range(group):
-                view = rows_ref.at[lead + k]
-                pltpu.make_async_copy(view, view, rows_sem.at[lead + k]).wait()
-
-        x = rows_ref[mine, :, 0].reshape(rows, width)
-        grad = rows_ref[mine, :, 1].reshape(rows, width)
+            back_start(block - 1)
+
+        here = pl.ds(pl.multiple_of(block * rows, rows), rows)
+
+        @pl.when((step == 0) & (block < last))
+        def _():
+            view = rows_ref.at[:, block]
+            pltpu.make_async_copy(view, view, rows_sem.at[block]).wait()
+
+        @pl.when((step == 0) & (block == last))
+        def _():
+            for source in range(groups):
+                view = rows_ref.at[source, last]
+                pltpu.make_async_copy(view, view, last_recv.at[source]).wait()
+
+        x = rows_ref[:, block, 0].reshape(rows, width)
+        grad = rows_ref[:, block, 1].reshape(rows, width)
         win = win_ref[q, :width, :]
         wout = wout_ref[q]
         pre = dot(x, win) + win_ref[q, width : width + 1, :].astype(F32)
@@ -829,9 +850,9 @@
 
         @pl.when(step == shards - 1)
         def _():
-            shape = (group, batches, cap_pad, width)
-            rows_ref[mine, :, 0] = y_acc[here, :].astype(BF).reshape(shape)
-            rows_ref[mine, :, 1] = dx_acc[here, :].astype(BF).reshape(shape)
+            shape = (groups, cap_pad, width)
+            rows_ref[:, block, 0] = y_acc[here, :].astype(BF).reshape(shape)
+            rows_ref[:, block, 1] = dx_acc[here, :].astype(BF).reshape(shape)
 
         @pl.when(block == blocks - 1)
         def _():
@@ -854,7 +875,7 @@
         return carry
 
     lax.fori_loop(0, shards * blocks, do_item, 0)
-    back_start(block_first(blocks - 1))
+    back_start(blocks - 1)
 
     def early_far(k, piece):
         _, low, size = far_pieces[piece]
@@ -962,17 +983,24 @@
         def _():
             early_far(0, piece).wait_send()
 
-    for k in range(groups):
-        source = lax.rem(me + k, groups)
-        if k:
-            back_copy(source).wait_send()
-        view = back_ref.at[source]
-        pltpu.make_async_copy(view, view, back_recv.at[source]).wait()
+    for k in range(1, groups):
+        last_copy(lax.rem(me + k, groups)).wait_send()
+
+    def finish_back(image, carry):
+        for k in range(groups):
+            source = lax.rem(me + k, groups)
+            if k:
+                back_copy(source, image).wait_send()
+            view = back_ref.at[source, image]
+            pltpu.make_async_copy(view, view, back_recv.at[source, image]).wait()
+        return carry
+
+    lax.fori_loop(0, batches, finish_back, 0)
     for copy in finals:
         copy.wait()
 
 
-def run_moe(received, own, spread_in, spread_out):
+def run_moe(received, last, own, spread_in, spread_out):
     groups, batches, _, cap_pad, width = received.shape
     shards, tall, span = spread_in.shape
     total = groups * batches * cap_pad
@@ -988,7 +1016,7 @@
             jax.ShapeDtypeStruct((2, tall, span), BF),
             jax.ShapeDtypeStruct((2, span, width), BF),
         ),
-        in_specs=[anywhere] * 6,
+        in_specs=[anywhere] * 7,
         out_specs=(anywhere,) * 5,
         scratch_shapes=[
             pltpu.VMEM(received.shape, BF),
@@ -1003,6 +1031,8 @@
             pltpu.VMEM((shards - 1, tall, span), BF),
             pltpu.VMEM((shards - 1, span, width), BF),
             pltpu.VMEM((2, early_rows, span), BF),
+            pltpu.SemaphoreType.DMA((batches,)),
+            pltpu.SemaphoreType.DMA((groups,)),
             pltpu.SemaphoreType.DMA((groups,)),
             pltpu.SemaphoreType.DMA((3,)),
             pltpu.SemaphoreType.DMA((EARLY_FAR,)),
@@ -1011,8 +1041,8 @@
             pltpu.SemaphoreType.DMA((shards, 4)),
             pltpu.SemaphoreType.DMA((2, shards, count)),
             pltpu.SemaphoreType.DMA((shards - 1, count)),
-            pltpu.SemaphoreType.DMA((groups,)),
-            pltpu.SemaphoreType.DMA((groups,)),
+            pltpu.SemaphoreType.DMA((groups, batches)),
+            pltpu.SemaphoreType.DMA((groups, batches)),
             pltpu.SemaphoreType.DMA((6,)),
         ],
         compiler_params=pltpu.CompilerParams(
@@ -1024,7 +1054,7 @@
             transcendentals=2 * total * span * shards,
         ),
         name="moe",
-    )(received, *own, spread_in, spread_out)
+    )(received, last, *own, spread_in, spread_out)
 
 
 def tail_kernel(
@@ -1557,7 +1587,6 @@
     out_store = pltpu.make_async_copy(raw_ref, out_hbm, store_sem.at[0, 0])
     out_store.start()
     pass_on(True, 2)
-    pass_on(True, 3)
     pass_on(False, 0)
     for kind, view in ((3, mixed_ref), (4, two_ref), (5, one_ref)):
         for image in range(batches):
@@ -1889,22 +1918,20 @@
     depth = qkv_weight.shape[0]
     both = ("dp", "expert")
 
-    used, wide = 4 + experts, gain_one.shape[0]
-    small = jnp.concatenate(
-        [gain_one, shift_one, gain_two, shift_two, router_weight.T.reshape(-1)]
-    ).reshape(used, wide)
-    small = jnp.pad(small, ((0, ceil_to(used, 16) - used), (0, ceil_to(wide, 128) - wide)))
+    vectors = jnp.stack([gain_one, shift_one, gain_two, shift_two], axis=1)
+    small = jnp.concatenate([vectors, router_weight], axis=1)
+    small = jnp.pad(small, ((0, 0), (0, SMALL - small.shape[1])))
     dense = (qkv_weight, proj_weight, small)
     own = (expert_in[0], jnp.pad(expert_bias, ((0, BIAS_ROWS - 1), (0, 0))), expert_out[0])
     cols = jnp.concatenate([routes, priority.reshape(batches * SEQ, 2)], axis=1)
     cols = cols.reshape(batches, SEQ, 4)
     cols = jnp.pad(cols, ((0, 0), (0, SEQ_PAD - SEQ), (0, 0)), constant_values=-1)
     rows_first = jnp.swapaxes(cols, 1, 2)
-    received, x, grad, weight, qkv, mixed, hidden, one, two, lse, probs, slot_cols, rows_small, *spread = run_front(
+    received, last, x, grad, weight, qkv, mixed, hidden, one, two, lse, probs, slot_cols, rows_small, *spread = run_front(
         inputs, out_grad, dense, own, cols, rows_first, capacity, experts, cap_pad
     )
     saved = (qkv, mixed, lse, hidden, one, two, probs)
-    back, sum_in, sum_out, far_in, far_out = run_moe(received, own, *spread)
+    back, sum_in, sum_out, far_in, far_out = run_moe(received, last, own, *spread)
     z = lax.axis_index("dp")
     at_end = (z == 0) | (z == lax.axis_size("dp") - 1)
     spot = 4 * width

time: 388 us -> 373 us (0.961)
  Pallas kernels: 360 us -> 350 us
  local copies, waits for them, and re-layouts: 19.1 us -> 15.2 us
    pallas_call x1, Pallas kernels: 116 us -> 103 us  [run_front(): pl.pallas_call(functools.partial(front_kernel, experts, shards), out_shap...]
    pallas_call x1, Pallas kernels: 145 us -> 154 us  [run_moe(): pl.pallas_call(functools.partial(moe_kernel, shards, groups), out_shape=(...]
    pallas_call x1, Pallas kernels: 99.1 us -> 92.6 us  [run_reduce(): pl.pallas_call(functools.partial(reduce_kernel, experts, shards), out_sha...]
where the time goes in v7:
time: 373 us; the launch traced here: 372 us
  Pallas kernels  350 us (94%)
  local copies, waits for them, and re-layouts  15.2 us (4%)
  other arithmetic  5.94 us (2%)
    pallas_call x1, Pallas kernels, run_moe(): pl.pallas_call(functools.partial(moe_kernel, shards, groups), out_shape=(...  154 us
    pallas_call x1, Pallas kernels, run_front(): pl.pallas_call(functools.partial(front_kernel, experts, shards), out_shap...  103 us
    pallas_call x1, Pallas kernels, run_reduce(): pl.pallas_call(functools.partial(reduce_kernel, experts, shards), out_sha...  92.6 us

profile of v7, /device:TPU:0, one launch (start us, length us, event | category | flops | bytes accessed | tf_op | source)
XLA Modules:
  0.0 372.0 jit_solution(1343791340132178702)
XLA Ops:
  0.6 0.0 copy-start.5
  0.7 0.0 copy-start.6
  0.7 0.0 copy-start.7
  0.7 0.0 copy-start.8
  0.7 0.0 copy-start.9
  0.7 0.0 copy-start.4
  0.7 0.9 concatenate.12
  1.6 0.2 copy.38
  1.8 0.8 concatenate.11
  2.6 0.2 copy.41
  2.8 0.8 pad.12.clone.cols_ref
  3.6 0.6 pad_bitcast_fusion.rows_ref
  4.3 0.0 copy-done.5
  4.3 0.6 pad.14.own_bias
  4.9 0.0 copy-done.6
  4.9 0.0 copy-done.7
  4.9 0.0 copy-done.8
  4.9 0.0 copy-done.9
  4.9 0.0 copy-done.4
  4.9 0.1 concatenate.14
  5.1 0.1 copy.39
  5.2 0.6 pad.13.small_own_ref
  5.8 103.4 %front.1 = (bf16[8,4,2,64,768]{4,3,2,1,0:T(8,128)(2,1)}, bf16[8,2,64,768]{3,2,1,0:T(8,128)(2,1)}, f32[4,208,768]{2,1,0:T(8,128)}, f32[4,208,768]{2,1,0:T(8,128)}...) custom-call(s32[4]{0:T(128)} %limit_ref.1, ...), custom_call_target="tpu_custom_call" | custom-call | flops 8000000000 | bytes 40000000 | tf_op jit(solution)/shard_map/front/pallas_call | solution.py:521
  109.2 154.0 %moe.1 = (bf16[8,4,2,64,768]{4,3,2,1,0:T(8,128)(2,1)}, bf16[784,768]{1,0:T(8,128)(2,1)}, bf16[768,768]{1,0:T(8,128)(2,1)}, bf16[2,784,768]{2,1,0:T(8,128)(2,1)}, bf16[2,768,768]{2,1,0:T(8,128)(2,1)}) custom-call(bf16[8,4,2,64,768]{4,3,2,1,0:T(8,128)(2,1)} %get-tuple-element.47.x_hbm, bf16[8,2,64,768]{3,2,1,0:T(8,128)(2,1)} %get-tuple-element.48.last_hbm, ...), custom_call_target="tpu_custom_call" | custom-call | flops 57982058496 | bytes 60000000 | tf_op jit(solution)/shard_map/moe/pallas_call | solution.py:1010
  263.2 92.6 %tail.1 = (f32[788,768]{1,0:T(8,128)}, f32[788,768]{1,0:T(8,128)}, bf16[784,768]{1,0:T(8,128)(2,1)}, bf16[768,768]{1,0:T(8,128)(2,1)}, f32[192,2304]{1,0:T(8,128...) custom-call(s32[4,208,8]{2,1,0:T(8,128)} %get-tuple-element.40.slot_cols_ref, f32[4,208,128]{2,1,0:T(8,128)} %get-tuple-element.41.lse_ref, ...), custom_call_target="tpu_custom_call" | custom-call | flops 16000000000 | bytes 50000000 | tf_op jit(solution)/shard_map/tail/pallas_call | solution.py:1822
  355.9 1.3 fusion
  357.2 0.0 copy-start.1
  357.2 4.6 %bitcast_convert_fusion = (f32[1,768,768]{2,1,0:T(8,128)}, f32[1,768,768]{2,1,0:T(8,128)}) fusion(bf16[768,768]{1,0:T(8,128)(2,1)} %get-tuple-element.66, bf16[768,768]{1,0:T(8,128)(2,1)} %get-tuple-element.67, pred[]{:T(512)S(6)} %or.3, bf16[784,768]{1,0:T(8,128)(2,1)} %get-tuple-element.65, bf16[784,768]{1,0:T(8,128)(2,1)} %get-tuple-element.64), kind=kLoop, calls=%fused_computation | loop fusion | flops 2359296 | bytes 9437185 | tf_op jit(solution)/shard_map/broadcast_in_dim | solution.py:1977
  361.8 1.4 dynamic-slice_bitcast_fusion
  363.3 1.5 fusion.1
  364.8 0.0 copy-done.1
  364.8 0.0 copy-start
  364.8 1.4 copy.46
  366.2 1.1 copy-done
  367.3 0.0 copy-start.2
  367.3 1.4 copy.47
  368.8 0.9 copy-done.2
  369.7 0.0 copy-start.3
  369.7 1.2 copy.48
  370.9 0.3 copy-done.3
  371.2 0.8 copy.49
  (6 shorter events, 0.0 us)
Async XLA Ops:
  0.6 3.6 copy-start.5
  0.7 4.2 %copy-start.6 = (bf16[192]{0:T(256)(128)(2,1)S(1)}, bf16[192]{0:T(256)(128)(2,1)}, u32[]{:S(2)}) copy-start(bf16[192]{0:T(256)(128)(2,1)} %param.16) | copy-start | bytes 1156
  0.7 4.2 %copy-start.7 = (bf16[192]{0:T(256)(128)(2,1)S(1)}, bf16[192]{0:T(256)(128)(2,1)}, u32[]{:S(2)}) copy-start(bf16[192]{0:T(256)(128)(2,1)} %param.17) | copy-start | bytes 1156
  0.7 4.2 %copy-start.8 = (bf16[192]{0:T(256)(128)(2,1)S(1)}, bf16[192]{0:T(256)(128)(2,1)}, u32[]{:S(2)}) copy-start(bf16[192]{0:T(256)(128)(2,1)} %param.20) | copy-start | bytes 1156
  0.7 4.2 %copy-start.9 = (bf16[192]{0:T(256)(128)(2,1)S(1)}, bf16[192]{0:T(256)(128)(2,1)}, u32[]{:S(2)}) copy-start(bf16[192]{0:T(256)(128)(2,1)} %param.21) | copy-start | bytes 1156
  0.7 4.2 %copy-start.4 = (bf16[192,8]{0,1:T(8,128)(2,1)S(1)}, bf16[192,8]{0,1:T(8,128)(2,1)}, u32[]{:S(2)}) copy-start(bf16[192,8]{0,1:T(8,128)(2,1)} %param.22) | copy-start | bytes 9220
  357.2 7.5 %copy-start.1 = (f32[788,768]{1,0:T(8,128)S(1)}, f32[788,768]{1,0:T(8,128)}, u32[]{:S(2)}) copy-start(f32[788,768]{1,0:T(8,128)} %get-tuple-element.86) | copy-start | bytes 7262212
  364.8 2.6 copy-start
  367.3 2.4 copy-start.2
  369.7 1.5 copy-start.3

commit v8 on v7

--- a/solution.py
+++ b/solution.py
@@ -18,7 +18,7 @@
 MESH = pl.DeviceIdType.MESH
 EARLY_PIECES = range(2)
 LATE_PIECES = range(2, 4)
-EARLY_FAR = 2
+EARLY_FAR = 3
 FAR_CUTS = 4
 FAR_TURNS = (
     (0, True, 3),

time: 373 us -> 369 us (0.989)
  no operation moved by 1% of the time
where the time goes in v8:
time: 369 us; the launch traced here: 368 us
  Pallas kernels  347 us (94%)
  local copies, waits for them, and re-layouts  15.2 us (4%)
  other arithmetic  5.94 us (2%)
    pallas_call x1, Pallas kernels, run_moe(): pl.pallas_call(functools.partial(moe_kernel, shards, groups), out_shape=(...  154 us
    pallas_call x1, Pallas kernels, run_front(): pl.pallas_call(functools.partial(front_kernel, experts, shards), out_shap...  103 us
    pallas_call x1, Pallas kernels, run_reduce(): pl.pallas_call(functools.partial(reduce_kernel, experts, shards), out_sha...  89.1 us
    unnamed x25, local copies, waits for them, and re-layouts  7.42 us

profile of v8, /device:TPU:0, one launch (start us, length us, event | category | flops | bytes accessed | tf_op | source)
XLA Modules:
  0.0 368.5 jit_solution(10759333334626795301)
XLA Ops:
  0.6 0.0 copy-start.5
  0.7 0.0 copy-start.6
  0.7 0.0 copy-start.7
  0.7 0.0 copy-start.8
  0.7 0.0 copy-start.9
  0.7 0.0 copy-start.4
  0.7 0.9 concatenate.12
  1.6 0.2 copy.38
  1.8 0.8 concatenate.11
  2.6 0.2 copy.41
  2.8 0.8 pad.12.clone.cols_ref
  3.6 0.6 pad_bitcast_fusion.rows_ref
  4.3 0.0 copy-done.5
  4.3 0.6 pad.14.own_bias
  4.9 0.0 copy-done.6
  4.9 0.0 copy-done.7
  4.9 0.0 copy-done.8
  4.9 0.0 copy-done.9
  4.9 0.0 copy-done.4
  4.9 0.1 concatenate.14
  5.1 0.1 copy.39
  5.2 0.6 pad.13.small_own_ref
  5.8 103.4 %front.1 = (bf16[8,4,2,64,768]{4,3,2,1,0:T(8,128)(2,1)}, bf16[8,2,64,768]{3,2,1,0:T(8,128)(2,1)}, f32[4,208,768]{2,1,0:T(8,128)}, f32[4,208,768]{2,1,0:T(8,128)}...) custom-call(s32[4]{0:T(128)} %limit_ref.1, ...), custom_call_target="tpu_custom_call" | custom-call | flops 8000000000 | bytes 40000000 | tf_op jit(solution)/shard_map/front/pallas_call | solution.py:521
  109.2 154.0 %moe.1 = (bf16[8,4,2,64,768]{4,3,2,1,0:T(8,128)(2,1)}, bf16[784,768]{1,0:T(8,128)(2,1)}, bf16[768,768]{1,0:T(8,128)(2,1)}, bf16[2,784,768]{2,1,0:T(8,128)(2,1)}, bf16[2,768,768]{2,1,0:T(8,128)(2,1)}) custom-call(bf16[8,4,2,64,768]{4,3,2,1,0:T(8,128)(2,1)} %get-tuple-element.47.x_hbm, bf16[8,2,64,768]{3,2,1,0:T(8,128)(2,1)} %get-tuple-element.48.last_hbm, ...), custom_call_target="tpu_custom_call" | custom-call | flops 57982058496 | bytes 60000000 | tf_op jit(solution)/shard_map/moe/pallas_call | solution.py:1010
  263.3 89.1 %tail.1 = (f32[788,768]{1,0:T(8,128)}, f32[788,768]{1,0:T(8,128)}, bf16[784,768]{1,0:T(8,128)(2,1)}, bf16[768,768]{1,0:T(8,128)(2,1)}, f32[192,2304]{1,0:T(8,128...) custom-call(s32[4,208,8]{2,1,0:T(8,128)} %get-tuple-element.40.slot_cols_ref, f32[4,208,128]{2,1,0:T(8,128)} %get-tuple-element.41.lse_ref, ...), custom_call_target="tpu_custom_call" | custom-call | flops 16000000000 | bytes 50000000 | tf_op jit(solution)/shard_map/tail/pallas_call | solution.py:1822
  352.4 1.3 fusion
  353.7 0.0 copy-start.1
  353.7 4.6 %bitcast_convert_fusion = (f32[1,768,768]{2,1,0:T(8,128)}, f32[1,768,768]{2,1,0:T(8,128)}) fusion(bf16[768,768]{1,0:T(8,128)(2,1)} %get-tuple-element.66, bf16[768,768]{1,0:T(8,128)(2,1)} %get-tuple-element.67, pred[]{:T(512)S(6)} %or.3, bf16[784,768]{1,0:T(8,128)(2,1)} %get-tuple-element.65, bf16[784,768]{1,0:T(8,128)(2,1)} %get-tuple-element.64), kind=kLoop, calls=%fused_computation | loop fusion | flops 2359296 | bytes 9437185 | tf_op jit(solution)/shard_map/broadcast_in_dim | solution.py:1977
  358.3 1.4 dynamic-slice_bitcast_fusion
  359.7 1.5 fusion.1
  361.2 0.0 copy-done.1
  361.2 0.0 copy-start
  361.3 1.4 copy.46
  362.7 1.1 copy-done
  363.8 0.0 copy-start.2
  363.8 1.4 copy.47
  365.2 0.9 copy-done.2
  366.2 0.0 copy-start.3
  366.2 1.2 copy.48
  367.4 0.3 copy-done.3
  367.6 0.8 copy.49
  (6 shorter events, 0.0 us)
Async XLA Ops:
  0.6 3.6 copy-start.5
  0.7 4.2 %copy-start.6 = (bf16[192]{0:T(256)(128)(2,1)S(1)}, bf16[192]{0:T(256)(128)(2,1)}, u32[]{:S(2)}) copy-start(bf16[192]{0:T(256)(128)(2,1)} %param.16) | copy-start | bytes 1156
  0.7 4.2 %copy-start.7 = (bf16[192]{0:T(256)(128)(2,1)S(1)}, bf16[192]{0:T(256)(128)(2,1)}, u32[]{:S(2)}) copy-start(bf16[192]{0:T(256)(128)(2,1)} %param.17) | copy-start | bytes 1156
  0.7 4.2 %copy-start.8 = (bf16[192]{0:T(256)(128)(2,1)S(1)}, bf16[192]{0:T(256)(128)(2,1)}, u32[]{:S(2)}) copy-start(bf16[192]{0:T(256)(128)(2,1)} %param.20) | copy-start | bytes 1156
  0.7 4.2 %copy-start.9 = (bf16[192]{0:T(256)(128)(2,1)S(1)}, bf16[192]{0:T(256)(128)(2,1)}, u32[]{:S(2)}) copy-start(bf16[192]{0:T(256)(128)(2,1)} %param.21) | copy-start | bytes 1156
  0.7 4.2 %copy-start.4 = (bf16[192,8]{0,1:T(8,128)(2,1)S(1)}, bf16[192,8]{0,1:T(8,128)(2,1)}, u32[]{:S(2)}) copy-start(bf16[192,8]{0,1:T(8,128)(2,1)} %param.22) | copy-start | bytes 9220
  353.7 7.5 %copy-start.1 = (f32[788,768]{1,0:T(8,128)S(1)}, f32[788,768]{1,0:T(8,128)}, u32[]{:S(2)}) copy-start(f32[788,768]{1,0:T(8,128)} %get-tuple-element.86) | copy-start | bytes 7262212
  361.2 2.6 copy-start
  363.8 2.4 copy-start.2
  366.2 1.5 copy-start.3

commit v9 on v8

--- a/solution.py
+++ b/solution.py
@@ -1525,6 +1525,8 @@
     pass_on(True, 0)
     pass_on(True, 1)
 
+    pass_on(True, 2)
+
     lane = lax.broadcasted_iota(jnp.int32, (1, 128), 1)
     groups, _, _, cap_pad, _ = back_ref.shape
     slots = groups * cap_pad
@@ -1586,7 +1588,6 @@
         raw_ref[image * SEQ : (image + 1) * SEQ] = hidden_ref[image, :SEQ]
     out_store = pltpu.make_async_copy(raw_ref, out_hbm, store_sem.at[0, 0])
     out_store.start()
-    pass_on(True, 2)
     pass_on(False, 0)
     for kind, view in ((3, mixed_ref), (4, two_ref), (5, one_ref)):
         for image in range(batches):
@@ -1640,8 +1641,11 @@
             for part in range(3):
                 d_qkv_ref[here, spots[part]] = total[part].astype(BF)
         first = head_tiles + 3 * pair
+        fresh_tiles = dot(
+            one_flip[...], jnp.concatenate([d_qkv_ref[:, spot] for spot in spots], axis=1)
+        ).astype(BF)
         for part in range(3):
-            tiles_ref[first + part] = dot(one_flip[...], d_qkv_ref[:, spots[part]]).astype(BF)
+            tiles_ref[first + part] = fresh_tiles[:, part * TILE : (part + 1) * TILE]
         for part in range(3):
             leave(first + part)
 

time: 369 us -> 369 us (level)
  no operation moved by 1% of the time
where the time goes in v9:
time: 369 us; the launch traced here: 368 us
  Pallas kernels  346 us (94%)
  local copies, waits for them, and re-layouts  15.2 us (4%)
  other arithmetic  5.94 us (2%)
    pallas_call x1, Pallas kernels, run_moe(): pl.pallas_call(functools.partial(moe_kernel, shards, groups), out_shape=(...  154 us
    pallas_call x1, Pallas kernels, run_front(): pl.pallas_call(functools.partial(front_kernel, experts, shards), out_shap...  103 us
    pallas_call x1, Pallas kernels, run_reduce(): pl.pallas_call(functools.partial(reduce_kernel, experts, shards), out_sha...  88.7 us
    unnamed x25, local copies, waits for them, and re-layouts  7.42 us

profile of v9, /device:TPU:0, one launch (start us, length us, event | category | flops | bytes accessed | tf_op | source)
XLA Modules:
  0.0 368.1 jit_solution(1911170175512917901)
XLA Ops:
  0.6 0.0 copy-start.5
  0.7 0.0 copy-start.6
  0.7 0.0 copy-start.7
  0.7 0.0 copy-start.8
  0.7 0.0 copy-start.9
  0.7 0.0 copy-start.4
  0.7 0.9 concatenate.12
  1.6 0.2 copy.38
  1.8 0.8 concatenate.11
  2.6 0.2 copy.41
  2.8 0.8 pad.12.clone.cols_ref
  3.6 0.6 pad_bitcast_fusion.rows_ref
  4.3 0.0 copy-done.5
  4.3 0.6 pad.14.own_bias
  4.9 0.0 copy-done.6
  4.9 0.0 copy-done.7
  4.9 0.0 copy-done.8
  4.9 0.0 copy-done.9
  4.9 0.0 copy-done.4
  4.9 0.1 concatenate.14
  5.1 0.1 copy.39
  5.2 0.6 pad.13.small_own_ref
  5.8 103.4 %front.1 = (bf16[8,4,2,64,768]{4,3,2,1,0:T(8,128)(2,1)}, bf16[8,2,64,768]{3,2,1,0:T(8,128)(2,1)}, f32[4,208,768]{2,1,0:T(8,128)}, f32[4,208,768]{2,1,0:T(8,128)}...) custom-call(s32[4]{0:T(128)} %limit_ref.1, ...), custom_call_target="tpu_custom_call" | custom-call | flops 8000000000 | bytes 40000000 | tf_op jit(solution)/shard_map/front/pallas_call | solution.py:521
  109.2 154.0 %moe.1 = (bf16[8,4,2,64,768]{4,3,2,1,0:T(8,128)(2,1)}, bf16[784,768]{1,0:T(8,128)(2,1)}, bf16[768,768]{1,0:T(8,128)(2,1)}, bf16[2,784,768]{2,1,0:T(8,128)(2,1)}, bf16[2,768,768]{2,1,0:T(8,128)(2,1)}) custom-call(bf16[8,4,2,64,768]{4,3,2,1,0:T(8,128)(2,1)} %get-tuple-element.47.x_hbm, bf16[8,2,64,768]{3,2,1,0:T(8,128)(2,1)} %get-tuple-element.48.last_hbm, ...), custom_call_target="tpu_custom_call" | custom-call | flops 57982058496 | bytes 60000000 | tf_op jit(solution)/shard_map/moe/pallas_call | solution.py:1010
  263.3 88.7 %tail.1 = (f32[788,768]{1,0:T(8,128)}, f32[788,768]{1,0:T(8,128)}, bf16[784,768]{1,0:T(8,128)(2,1)}, bf16[768,768]{1,0:T(8,128)(2,1)}, f32[192,2304]{1,0:T(8,128...) custom-call(s32[4,208,8]{2,1,0:T(8,128)} %get-tuple-element.40.slot_cols_ref, f32[4,208,128]{2,1,0:T(8,128)} %get-tuple-element.41.lse_ref, ...), custom_call_target="tpu_custom_call" | custom-call | flops 16000000000 | bytes 50000000 | tf_op jit(solution)/shard_map/tail/pallas_call | solution.py:1826
  352.0 1.3 fusion
  353.3 0.0 copy-start.1
  353.3 4.6 %bitcast_convert_fusion = (f32[1,768,768]{2,1,0:T(8,128)}, f32[1,768,768]{2,1,0:T(8,128)}) fusion(bf16[768,768]{1,0:T(8,128)(2,1)} %get-tuple-element.66, bf16[768,768]{1,0:T(8,128)(2,1)} %get-tuple-element.67, pred[]{:T(512)S(6)} %or.3, bf16[784,768]{1,0:T(8,128)(2,1)} %get-tuple-element.65, bf16[784,768]{1,0:T(8,128)(2,1)} %get-tuple-element.64), kind=kLoop, calls=%fused_computation | loop fusion | flops 2359296 | bytes 9437185 | tf_op jit(solution)/shard_map/broadcast_in_dim | solution.py:1981
  357.9 1.4 dynamic-slice_bitcast_fusion
  359.3 1.5 fusion.1
  360.9 0.0 copy-done.1
  360.9 0.0 copy-start
  360.9 1.4 copy.46
  362.3 1.1 copy-done
  363.4 0.0 copy-start.2
  363.4 1.4 copy.47
  364.9 0.9 copy-done.2
  365.8 0.0 copy-start.3
  365.8 1.2 copy.48
  367.0 0.3 copy-done.3
  367.2 0.8 copy.49
  (6 shorter events, 0.0 us)
Async XLA Ops:
  0.6 3.6 copy-start.5
  0.7 4.2 %copy-start.6 = (bf16[192]{0:T(256)(128)(2,1)S(1)}, bf16[192]{0:T(256)(128)(2,1)}, u32[]{:S(2)}) copy-start(bf16[192]{0:T(256)(128)(2,1)} %param.16) | copy-start | bytes 1156
  0.7 4.2 %copy-start.7 = (bf16[192]{0:T(256)(128)(2,1)S(1)}, bf16[192]{0:T(256)(128)(2,1)}, u32[]{:S(2)}) copy-start(bf16[192]{0:T(256)(128)(2,1)} %param.17) | copy-start | bytes 1156
  0.7 4.2 %copy-start.8 = (bf16[192]{0:T(256)(128)(2,1)S(1)}, bf16[192]{0:T(256)(128)(2,1)}, u32[]{:S(2)}) copy-start(bf16[192]{0:T(256)(128)(2,1)} %param.20) | copy-start | bytes 1156
  0.7 4.2 %copy-start.9 = (bf16[192]{0:T(256)(128)(2,1)S(1)}, bf16[192]{0:T(256)(128)(2,1)}, u32[]{:S(2)}) copy-start(bf16[192]{0:T(256)(128)(2,1)} %param.21) | copy-start | bytes 1156
  0.7 4.2 %copy-start.4 = (bf16[192,8]{0,1:T(8,128)(2,1)S(1)}, bf16[192,8]{0,1:T(8,128)(2,1)}, u32[]{:S(2)}) copy-start(bf16[192,8]{0,1:T(8,128)(2,1)} %param.22) | copy-start | bytes 9220
  353.3 7.5 %copy-start.1 = (f32[788,768]{1,0:T(8,128)S(1)}, f32[788,768]{1,0:T(8,128)}, u32[]{:S(2)}) copy-start(f32[788,768]{1,0:T(8,128)} %get-tuple-element.86) | copy-start | bytes 7262212
  360.9 2.6 copy-start
  363.4 2.4 copy-start.2
  365.8 1.5 copy-start.3
